TPU v7x, 32 devices: a whole 2x2x4 slice. The times are simulated.
32 devices in a mesh: grp: 16 (over z, y, core), chan: 2 (over x).
Axes of the slice: x: 2, y: 2, z: 4, core: 2. Of those that a mesh axis runs over, the one named last changes fastest.
Arguments:
- voltages: bfloat16 [32, 2, 4096, 256], P(None, None, 'grp', 'chan'), may hold values from -6 to 6
- input_flags: int32 [4096], P('grp'), may hold values 0 or 1
- pair_order: int32 [9], replicated, may hold values from 0 to 8, each once
Outputs:
- visibilities: float32 [16, 9, 32, 256, 512], P('grp', None, 'chan')
Inputs may be any that keep to these rules, and one draw needn't show every extreme that they name: `pair_order`: a permutation of 0 to 8.
All inputs are finite; a program needn't handle non-finite values. No bound on the sum of `input_flags` on one device may be relied on, other than what follows from the above.
Results may differ from a plain program's by a relative error of at most 0.0003.
Values may be sent and summed in bfloat16 or wider, within the bound.
No kernel may reach another device: no remote copies, remote signals or barrier semaphores. Data moves between devices by JAX's collectives and lax.ppermute only.
A program may use at most 320 MiB of HBM per device.

v0:
```python
import jax
import jax.numpy as jnp
from jax import lax
from jax.sharding import PartitionSpec as P


def from_behind(block, axis, distance):
    devices = range(lax.axis_size(axis))
    route = [((i - distance) % len(devices), i) for i in devices]
    return lax.ppermute(block, axis, route)


def accumulate(left_blocks, right_blocks):
    rotated = jnp.stack([-right_blocks[:, 1], right_blocks[:, 0]], axis=1)
    extended = jnp.concatenate([right_blocks, rotated], axis=3)
    return jnp.einsum(
        "cpeit,cpejt->ecij", left_blocks, extended, preferred_element_type=jnp.float32
    )


def on_device(voltages, input_flags, pair_order):
    turned = lax.all_to_all(voltages, "chan", split_axis=0, concat_axis=3, tiled=True)
    weights = input_flags.astype(jnp.bfloat16)
    flagged = turned * weights[None, None, :, None]
    channels = flagged.shape[0]
    group_size = flagged.shape[2]
    samples = flagged.shape[3]
    quarter = lax.axis_size("grp") // 4
    window_blocks = from_behind(flagged, "grp", quarter)
    filled = 1
    while filled < 2 * quarter + 1:
        amount = min(filled, 2 * quarter + 1 - filled)
        arrived = from_behind(window_blocks[:, :, : amount * group_size], "grp", -filled)
        window_blocks = jnp.concatenate([window_blocks, arrived], axis=2)
        filled = filled + amount
    shaped = window_blocks.reshape(channels, 2, 2 * quarter + 1, group_size, samples)
    behind_part = jnp.flip(shaped[:, :, : quarter + 1], axis=2)
    ahead_part = shaped[:, :, quarter:]
    inverse = jnp.float32(1.0 / samples)
    even_tiles = accumulate(behind_part, ahead_part) * inverse
    odd_tiles = accumulate(behind_part[:, :, :quarter], ahead_part[:, :, 1:]) * inverse
    slot_count = 2 * quarter + 1
    result = jnp.zeros((slot_count,) + even_tiles.shape[1:], jnp.float32)
    result = result.at[pair_order[0::2]].set(even_tiles).at[pair_order[1::2]].set(odd_tiles)
    return result[None]


def solution(mesh):
    return jax.shard_map(
        on_device,
        mesh=mesh,
        in_specs=(P(None, None, "grp", "chan"), P("grp"), P()),
        out_specs=P("grp", None, "chan", None, None),
        check_vma=False,
    )
```

profile of v0, /device:TPU:0, one launch (start us, length us, event | category | flops | bytes accessed | tf_op | source)
XLA Modules:
  0.0 1314.6 jit_solution(6586216404468347991)
XLA Ops:
  0.0 5.6 all-to-all-start
  6.3 48.2 %all-to-all-done = bf16[32,2,256,128]{3,2,1,0:T(8,128)(2,1)} async-done(((bf16[32,2,256,128]{3,2,1,0:T(8,128)(2,1)}), bf16[32,2,256,128]{3,2,1,0:T(8,128)(2,1)}, u32[]{:S(2)}, u32[]{:S(2)}) %all-to-all-start) | async-done | bytes 4194336 | tf_op jit(solution)/shard_map/all_to_all | solution.py:22
  54.5 6.4 copy.13
  60.9 2.5 bitcast_multiply_fusion.2
  65.2 91.8 %collective-permute-done = bf16[16,2,256,256]{2,3,1,0:T(8,128)(2,1)} collective-permute-done((bf16[16,2,256,256]{2,3,1,0:T(8,128)(2,1)S(1)}, bf16[16,2,256,256]{2,3,1,0:T(8,128)(2,1)}, u32[]{:S(2)}, u32[]{:S(2)}) %collective-permute-start) | collective-permute-done | bytes 4194336 | tf_op jit(solution)/shard_map/ppermute | solution.py:10
  157.4 46.3 %collective-permute-done.1 = bf16[16,2,256,256]{2,3,1,0:T(8,128)(2,1)} collective-permute-done((bf16[16,2,256,256]{2,3,1,0:T(8,128)(2,1)}, bf16[16,2,256,256]{2,3,1,0:T(8,128)(2,1)}, u32[]{:S(2)}, u32[]{:S(2)}) %collective-permute-start.1) | collective-permute-done | bytes 4194336 | tf_op jit(solution)/shard_map/ppermute | solution.py:10
  203.7 7.7 pad_maximum_fusion.1
  211.4 2.4 collective-permute-start.2
  213.8 180.8 %collective-permute-done.2 = bf16[16,2,512,256]{2,3,1,0:T(8,128)(2,1)S(1)} collective-permute-done((bf16[16,2,512,256]{2,3,1,0:T(8,128)(2,1)}, bf16[16,2,512,256]{2,3,1,0:T(8,128)(2,1)S(1)}, u32[]{:S(2)}, u32[]{:S(2)}) %collective-permute-start.2) | collective-permute-done | bytes 8388640 | tf_op jit(solution)/shard_map/ppermute | solution.py:10
  394.5 3.2 copy-done
  397.7 10.7 pad_maximum_fusion
  411.9 4.6 constant_dynamic-update-slice_fusion.4
  416.5 4.6 constant_dynamic-update-slice_fusion.3
  421.2 7.7 constant_dynamic-update-slice_fusion.2
  428.8 343.1 %collective-permute-done.3 = bf16[16,2,1024,256]{2,3,1,0:T(8,128)(2,1)} collective-permute-done((bf16[16,2,1024,256]{2,3,1,0:T(8,128)(2,1)}, bf16[16,2,1024,256]{2,3,1,0:T(8,128)(2,1)}, u32[]{:S(2)}, u32[]{:S(2)}) %collective-permute-start.3) | collective-permute-done | bytes 16777248 | tf_op jit(solution)/shard_map/ppermute | solution.py:10
  771.9 13.9 %constant_dynamic-update-slice_fusion.1 = bf16[16,2,2304,256]{2,3,1,0:T(8,128)(2,1)} fusion(bf16[16,2,2304,256]{2,3,1,0:T(8,128)(2,1)} %constant_dynamic-update-slice_fusion.2, bf16[16,2,1024,256]{2,3,1,0:T(8,128)(2,1)} %collective-permute-done.3), kind=kLoop, calls=%fused_computation.24 | loop fusion | bytes 33554432
  785.8 165.0 %collective-permute-done.4 = bf16[16,2,256,256]{2,3,1,0:T(8,128)(2,1)} collective-permute-done((bf16[16,2,256,256]{2,3,1,0:T(8,128)(2,1)}, bf16[16,2,256,256]{2,3,1,0:T(8,128)(2,1)}, u32[]{:S(2)}, u32[]{:S(2)}) %collective-permute-start.4) | collective-permute-done | bytes 4194336 | tf_op jit(solution)/shard_map/ppermute | solution.py:10
  950.8 4.6 constant_dynamic-update-slice_fusion
  955.4 47.1 %copy.14 = bf16[16,2,2304,256]{3,2,1,0:T(8,128)(2,1)} copy(bf16[16,2,2304,256]{2,3,1,0:T(8,128)(2,1)} %constant_dynamic-update-slice_fusion) | data formatting | bytes 75497472 | tf_op jit(solution)/shard_map/concatenate | solution.py:34
  1002.6 23.1 %fusion.24 = (bf16[16,2,4,256,256]{4,3,2,1,0:T(8,128)(2,1)}, bf16[16,2,4,256,256]{4,3,2,1,0:T(8,128)(2,1)}) fusion(bf16[16,2,9,256,256]{4,3,2,1,0:T(8,128)(2,1)} %bitcast.15), kind=kLoop, calls=%fused_computation.32 | loop fusion | bytes 67108864 | tf_op jit(solution)/shard_map/slice | solution.py:41
  1025.6 11.6 fusion.25
  1037.3 28.2 %fusion.26 = (bf16[16,2,5,256,256]{4,3,2,1,0:T(8,128)(2,1)}, bf16[16,2,5,256,256]{4,3,2,1,0:T(8,128)(2,1)}) fusion(bf16[16,2,9,256,256]{4,3,2,1,0:T(8,128)(2,1)} %bitcast.17), kind=kLoop, calls=%fused_computation.34 | loop fusion | bytes 83886080 | tf_op jit(solution)/shard_map/slice | solution.py:37
  1065.4 16.1 %fusion.27 = (bf16[16,1,5,256,256]{4,3,2,1,0:T(8,128)(2,1)}, bf16[16,1,5,256,256]{4,3,2,1,0:T(8,128)(2,1)}) fusion(bf16[16,2,9,256,256]{4,3,2,1,0:T(8,128)(2,1)} %bitcast.18), kind=kLoop, calls=%fused_computation.35 | loop fusion | bytes 41943040 | tf_op jit(solution)/shard_map/slice | solution.py:14
  1081.5 13.9 %slice.46 = bf16[16,2,4,256,256]{4,3,2,1,0:T(8,128)(2,1)} reverse(bf16[16,2,4,256,256]{4,3,2,1,0:T(8,128)(2,1)} %get-tuple-element.5), dimensions={2} | reverse | bytes 33554432 | tf_op jit(solution)/shard_map/slice | solution.py:41
  1095.4 7.1 copy_negate_fusion.1
  1102.6 17.4 %rev.4 = bf16[16,2,5,256,256]{4,3,2,1,0:T(8,128)(2,1)} reverse(bf16[16,2,5,256,256]{4,3,2,1,0:T(8,128)(2,1)} %get-tuple-element.9), dimensions={2} | reverse | bytes 41943040 | tf_op jit(solution)/shard_map/jit(_flip)/rev | solution.py:37
  1120.0 8.7 copy_negate_fusion
  1128.7 40.1 %bitcast_multiply_fusion = f32[5,16,256,512]{3,2,1,0:T(8,128)} fusion(bf16[16,1,5,256,256]{4,3,1,0,2:T(8,128)(2,1)} %copy_negate_fusion, bf16[16,2,5,256,256]{4,3,2,1,0:T(8,128)(2,1)} %rev.4, bf16[16,2,5,256,256]{4,3,2,1,0:T(8,128)(2,1)} %get-tuple-element.10, bf16[16,1,5,256,256]{4,3,2,1,0:T(8,128)(2,1)} %get-tuple-element.12), kind=kOutput, calls=%fused_computation.8 | convolution fusion | flops 10873733120 | bytes 104857600 | tf_op jit(solution)/shard_map/cpeit,cpejt->ecij/dot_general | solution.py:16
  1168.8 24.1 %broadcast_in_dim.13 = f32[9,16,256,512]{3,2,1,0:T(8,128)} broadcast(f32[]{:T(128)} %constant.4.clone.1), dimensions={} | broadcast | bytes 75497472 | tf_op jit(solution)/shard_map/broadcast_in_dim | solution.py:43
  1192.9 49.1 %scatter_fusion = f32[9,16,256,512]{3,2,1,0:T(8,128)} fusion(f32[9,16,256,512]{3,2,1,0:T(8,128)} %broadcast_in_dim.13, s32[5]{0:T(128)S(1)} %copy-done.1, f32[5,16,256,512]{3,2,1,0:T(8,128)} %bitcast_multiply_fusion), kind=kCustom, calls=%fused_computation | custom fusion | bytes 125829136 | tf_op jit(solution)/shard_map/scatter | solution.py:44
  1241.9 33.3 %bitcast_multiply_fusion.1 = f32[4,16,256,512]{3,2,1,0:T(8,128)} fusion(bf16[16,1,4,256,256]{4,3,1,0,2:T(8,128)(2,1)} %copy_negate_fusion.1, bf16[16,2,4,256,256]{4,3,2,1,0:T(8,128)(2,1)} %slice.46, bf16[16,2,4,256,256]{4,3,2,1,0:T(8,128)(2,1)} %get-tuple-element.6, bf16[16,1,4,256,256]{4,3,2,1,0:T(8,128)(2,1)} %get-tuple-element.8), kind=kOutput, calls=%fused_computation.15 | convolution fusion | flops 8698986496 | bytes 83886080 | tf_op jit(solution)/shard_map/cpeit,cpejt->ecij/dot_general | solution.py:16
  1275.2 39.4 %scatter_fusion.1 = f32[9,16,256,512]{3,2,1,0:T(8,128)} fusion(f32[9,16,256,512]{3,2,1,0:T(8,128)} %scatter_fusion, s32[4]{0:T(128)S(1)} %copy-done.2, f32[4,16,256,512]{3,2,1,0:T(8,128)} %bitcast_multiply_fusion.1), kind=kCustom, calls=%fused_computation.1 | custom fusion | bytes 100663312 | tf_op jit(solution)/shard_map/scatter | solution.py:44
  (16 shorter events, 6.3 us)
Async XLA Ops:
  0.0 54.5 %all-to-all-start = ((bf16[32,2,256,128]{3,2,1,0:T(8,128)(2,1)}), bf16[32,2,256,128]{3,2,1,0:T(8,128)(2,1)}, u32[]{:S(2)}, u32[]{:S(2)}) async-start(bf16[32,2,256,128]{3,2,1,0:T(8,128)(2,1)} %param.3), calls=%async_computation | async-start | bytes 8388608 | tf_op jit(solution)/shard_map/all_to_all | solution.py:22
  63.3 93.7 %collective-permute-start = (bf16[16,2,256,256]{2,3,1,0:T(8,128)(2,1)S(1)}, bf16[16,2,256,256]{2,3,1,0:T(8,128)(2,1)}, u32[]{:S(2)}, u32[]{:S(2)}) collective-permute-start(bf16[16,2,256,256]{2,3,1,0:T(8,128)(2,1)S(1)} %bitcast_multiply_fusion.2), channel_id=1, source_target_pairs={{24,0},{26,2},{28,4},{30,6},{0,8},{2,10},{4,12},{6,14},{8,16},{10,... | collective-permute-start | bytes 12582920 | tf_op jit(solution)/shard_map/ppermute | solution.py:10
  157.0 46.7 %collective-permute-start.1 = (bf16[16,2,256,256]{2,3,1,0:T(8,128)(2,1)}, bf16[16,2,256,256]{2,3,1,0:T(8,128)(2,1)}, u32[]{:S(2)}, u32[]{:S(2)}) collective-permute-start(bf16[16,2,256,256]{2,3,1,0:T(8,128)(2,1)} %collective-permute-done), channel_id=1, source_target_pairs={{2,0},{4,2},{6,4},{8,6},{10,8},{12,10},{14,12},{16,14},{18,16},{20... | collective-permute-start | bytes 12582920 | tf_op jit(solution)/shard_map/ppermute | solution.py:10
  211.4 199.2 %copy-start.3 = (s32[9]{0:T(128)S(1)}, s32[9]{0:T(128)}, u32[]{:S(2)}) copy-start(s32[9]{0:T(128)} %param.5) | copy-start | bytes 112
  211.4 183.1 %collective-permute-start.2 = (bf16[16,2,512,256]{2,3,1,0:T(8,128)(2,1)}, bf16[16,2,512,256]{2,3,1,0:T(8,128)(2,1)S(1)}, u32[]{:S(2)}, u32[]{:S(2)}) collective-permute-start(bf16[16,2,512,256]{2,3,1,0:T(8,128)(2,1)} %pad_maximum_fusion.1), channel_id=1, source_target_pairs={{4,0},{6,2},{8,4},{10,6},{12,8},{14,10},{16,12},{18,14},{20,16},{2... | collective-permute-start | bytes 25165832 | tf_op jit(solution)/shard_map/ppermute | solution.py:10
  394.5 3.2 copy-start
  408.5 363.4 %collective-permute-start.3 = (bf16[16,2,1024,256]{2,3,1,0:T(8,128)(2,1)}, bf16[16,2,1024,256]{2,3,1,0:T(8,128)(2,1)}, u32[]{:S(2)}, u32[]{:S(2)}) collective-permute-start(bf16[16,2,1024,256]{2,3,1,0:T(8,128)(2,1)} %pad_maximum_fusion), channel_id=1, source_target_pairs={{8,0},{10,2},{12,4},{14,6},{16,8},{18,10},{20,12},{22,14},{24,16},... | collective-permute-start | bytes 50331656 | tf_op jit(solution)/shard_map/ppermute | solution.py:10
  408.8 542.0 %collective-permute-start.4 = (bf16[16,2,256,256]{2,3,1,0:T(8,128)(2,1)}, bf16[16,2,256,256]{2,3,1,0:T(8,128)(2,1)}, u32[]{:S(2)}, u32[]{:S(2)}) collective-permute-start(bf16[16,2,256,256]{2,3,1,0:T(8,128)(2,1)} %collective-permute-done), channel_id=1, source_target_pairs={{16,0},{18,2},{20,4},{22,6},{24,8},{26,10},{28,12},{30,14},{0,16},... | collective-permute-start | bytes 12582920 | tf_op jit(solution)/shard_map/ppermute | solution.py:10
  1168.8 24.1 %copy-start.1 = (s32[5]{0:T(128)S(1)}, s32[5]{0:T(128)}, u32[]{:S(2)}) copy-start(s32[5]{0:T(128)} %compare_select_fusion.1) | copy-start | bytes 64
  1241.9 33.3 %copy-start.2 = (s32[4]{0:T(128)S(1)}, s32[4]{0:T(128)}, u32[]{:S(2)}) copy-start(s32[4]{0:T(128)} %compare_select_fusion) | copy-start | bytes 52
where the time goes:
time: 1320 us; the launch traced here: 1310 us
  waiting for transfers between devices  875 us (66%)
  local copies, waits for them, and re-layouts  315 us (24%)
  matrix products  73.3 us (6%)
  other arithmetic  38.6 us (3%)
    ppermute x5, waiting for transfers between devices, from_behind(): return lax.ppermute(block, axis, route)  827 us
    scatter x2, local copies, waits for them, and re-layouts, on_device(): result.at[pair_order[0::2]].set(even_tiles).at[pair_order[1::2]]  88.4 us
    dot_general x2, matrix products, accumulate(): jnp.einsum('cpeit,cpejt->ecij', left_blocks, extended, preferred_element_...  73.3 us
    concatenate x2, local copies, waits for them, and re-layouts, on_device(): window_blocks = jnp.concatenate([window_blocks, arrived], axis=2)  51.8 us
    all_to_all x1, waiting for transfers between devices, on_device(): lax.all_to_all(voltages, 'chan', split_axis=0, concat_axis=3, tiled=True)  48.2 us
    slice x2, local copies, waits for them, and re-layouts, on_device(): behind_part[:, :, :quarter]  37 us
    unnamed x12, local copies, waits for them, and re-layouts  34.1 us
    slice x1, local copies, waits for them, and re-layouts, on_device(): behind_part = jnp.flip(shaped[:, :, :quarter + 1], axis=2)  28.2 us
  transfers between devices with their start and end apart: 6, of which 6 were waited for; matrix products, arithmetic and copies ran while one was open for 2% of the time, Pallas kernels for 0%

commit v1 on v0

v1 whole, which is shorter than its diff:
```python
import functools

import jax
import jax.numpy as jnp
from jax import lax
from jax.experimental import pallas as pl
from jax.experimental.pallas import tpu as pltpu
from jax.sharding import PartitionSpec as P


def pair_kernel(variants, parts, blocks, table, *refs):
    width = len(variants[0])
    sources = refs[:blocks]
    out, window, sems = refs[-3:]
    step = pl.program_id(0)
    steps = pl.num_programs(0)

    def copy(source, channel, slot, entry, part):
        return pltpu.make_async_copy(
            sources[source * parts + part].at[channel],
            window.at[slot, entry, part],
            sems.at[slot, entry, part],
        )

    def fetch(channel, slot):
        for at, variant in enumerate(variants):

            @pl.when(table[0] == at)
            def _():
                for entry, source in enumerate(variant):
                    for part in range(parts):
                        copy(source, channel, slot, entry, part).start()

    @pl.when(step == 0)
    def _():
        fetch(0, 0)

    @pl.when(step + 1 < steps)
    def _():
        fetch(step + 1, lax.rem(step + 1, 2))

    slot = lax.rem(step, 2)
    for entry in range(width):
        for part in range(parts):
            copy(0, 0, slot, entry, part).wait()

    half = width // 2
    size = window.shape[-2]
    scale = jnp.float32(1.0 / (parts * window.shape[-1]))
    contract = (((1,), (1,)), ((), ()))

    def pair(d, carry):
        a = half - d // 2
        b = half + (d + 1) // 2
        real = jnp.zeros((size, size), jnp.float32)
        imag = jnp.zeros((size, size), jnp.float32)
        for part in range(parts):
            left = jnp.concatenate([window[slot, a, part, 0], window[slot, a, part, 1]], axis=1)
            b_r, b_i = window[slot, b, part, 0], window[slot, b, part, 1]
            real = real + lax.dot_general(
                left, jnp.concatenate([b_r, b_i], axis=1), contract, preferred_element_type=jnp.float32
            )
            imag = imag + lax.dot_general(
                left, jnp.concatenate([-b_i, b_r], axis=1), contract, preferred_element_type=jnp.float32
            )
        to = table[1 + d]
        out[0, to, 0, :, :size] = real * scale
        out[0, to, 0, :, size:] = imag * scale
        return carry

    if width <= 9:
        for d in range(width):
            pair(d, 0)
    else:
        lax.fori_loop(0, width, pair, 0)


def correlate(sources, parts, variants, table, first, channels, previous):
    count, _, size, samples = sources[0].shape
    width = len(variants[0])
    out_shape = (1, width, channels, size, 2 * size)
    operands = list(sources) + ([] if previous is None else [previous])
    return pl.pallas_call(
        functools.partial(pair_kernel, variants, parts, len(sources)),
        out_shape=jax.ShapeDtypeStruct(out_shape, jnp.float32),
        grid_spec=pltpu.PrefetchScalarGridSpec(
            num_scalar_prefetch=1,
            grid=(count,),
            in_specs=[pl.BlockSpec(memory_space=pl.ANY)] * len(operands),
            out_specs=pl.BlockSpec((1, width, 1, size, 2 * size), lambda c, t: (0, 0, first + c, 0, 0)),
            scratch_shapes=[
                pltpu.VMEM((2, width, parts, 2, size, samples), jnp.bfloat16),
                pltpu.SemaphoreType.DMA((2, width, parts)),
            ],
        ),
        input_output_aliases={} if previous is None else {len(operands): 0},
        compiler_params=pltpu.CompilerParams(
            dimension_semantics=("arbitrary",), vmem_limit_bytes=40 << 20
        ),
        cost_estimate=pl.CostEstimate(
            flops=8 * count * width * size * size * parts * samples,
            bytes_accessed=count * width * size * (8 * size + 4 * parts * samples),
            transcendentals=0,
        ),
    )(table, *operands)


def permute(route):
    return lambda block: lax.ppermute(block, "grp", route)


def split_exchange(voltages, weights, table, chunks):
    devices = lax.axis_size("grp")
    plane = devices // 4
    channels = voltages.shape[0] // 2
    me = lax.axis_index("grp")
    column = lax.axis_index("chan")

    def behind(i):
        return (i - plane) % devices

    def beyond(i):
        return (i + plane) % devices

    def upper(i):
        return i % plane >= plane // 2

    everyone = range(devices)
    forward = permute([(behind(i) if upper(i) else beyond(i), i) for i in everyone])
    straight = permute([(beyond(i) if upper(i) else behind(i), i) for i in everyone])
    across = permute([(i ^ (plane // 2), i) for i in everyone])
    twin = permute([(i ^ 1, i) for i in everyone])

    def piece(of_column, first, count):
        block = lax.dynamic_slice_in_dim(voltages, of_column * channels + first, count, axis=0)
        return block * weights

    def spread(own):
        theirs = forward(own)
        others = straight(own)
        partner = across(own)
        passed = across(theirs)
        direct = [own, partner, passed, theirs, others]
        return direct + [twin(block) for block in direct]

    own, partner, passed, theirs, others = range(5)
    variants = []
    for y in range(2):
        chips = (others, passed, own, partner, theirs) if y == 0 else (theirs, partner, own, passed, others)
        for core in range(2):
            entries = []
            for j in range(-plane, plane + 1):
                chip = chips[(core + j) // 2 + 2]
                entries.append(chip if (core + j) % 2 == core else chip + 5)
            variants.append(tuple(entries))
    position = lax.rem(me, plane)
    table = jnp.concatenate([position[None].astype(jnp.int32), table])

    result = None
    first = 0
    for count in chunks:
        mine = piece(column, first, count)
        turned = lax.ppermute(piece(1 - column, first, count), "chan", [(0, 1), (1, 0)])
        halves = [spread(mine), spread(turned)]
        sources = [halves[part][at] for at in range(10) for part in range(2)]
        result = correlate(sources, 2, tuple(variants), table, first, channels, result)
        first += count
    return result


def window_exchange(voltages, weights, table):
    turned = lax.all_to_all(voltages * weights, "chan", split_axis=0, concat_axis=3, tiled=True)
    devices = lax.axis_size("grp")
    quarter = devices // 4
    width = 2 * quarter + 1

    def from_behind(block, distance):
        return lax.ppermute(block, "grp", [((i - distance) % devices, i) for i in range(devices)])

    window = [from_behind(turned, quarter)]
    while len(window) < width:
        window += [from_behind(block, -len(window)) for block in window[: width - len(window)]]
    table = jnp.concatenate([jnp.zeros((1,), jnp.int32), table])
    return correlate(window, 1, (tuple(range(width)),), table, 0, turned.shape[0], None)


def on_device(voltages, input_flags, pair_order):
    weights = input_flags.astype(jnp.bfloat16)[None, None, :, None]
    if lax.axis_size("grp") == 16 and lax.axis_size("chan") == 2:
        return split_exchange(voltages, weights, pair_order, (4, 4, 4, 4))
    return window_exchange(voltages, weights, pair_order)


def solution(mesh):
    return jax.shard_map(
        on_device,
        mesh=mesh,
        in_specs=(P(None, None, "grp", "chan"), P("grp"), P()),
        out_specs=P("grp", None, "chan", None, None),
        check_vma=False,
    )
```

time: 1320 us -> 355 us (0.27)
  waiting for transfers between devices: 875 us -> 143 us
  local copies, waits for them, and re-layouts: 315 us -> 57.7 us
  Pallas kernels: 0 us -> 80.2 us
  matrix products: 73.3 us -> 0 us
  starting transfers between devices: 12.3 us -> 68.4 us
  other arithmetic: 38.6 us -> 3.94 us
    ppermute x5 -> x76, waiting for transfers between devices: 827 us -> 143 us  [the longest x72 135 us: permute(): return lambda block: lax.ppermute(block, 'grp', route)]
    slice x7 -> x0, local copies, waits for them, and re-layouts: 93 us -> none  [the longest x2 37 us: on_device(): behind_part[:, :, :quarter]]
    scatter x2 -> x0, local copies, waits for them, and re-layouts: 88.4 us -> none  [on_device(): result.at[pair_order[0::2]].set(even_tiles).at[pair_order[1::2]]]
    pallas_call x0 -> x4, Pallas kernels: none -> 80.2 us  [correlate(): pl.pallas_call(functools.partial(pair_kernel, variants, parts, len(source...]
    dot_general x2 -> x0, matrix products: 73.3 us -> none  [accumulate(): jnp.einsum('cpeit,cpejt->ecij', left_blocks, extended, preferred_element_...]
    ppermute x5 -> x76, starting transfers between devices: 6.67 us -> 68.4 us  [the longest x72 62.6 us: permute(): return lambda block: lax.ppermute(block, 'grp', route)]
    concatenate x2 -> x0, local copies, waits for them, and re-layouts: 51.8 us -> none  [on_device(): window_blocks = jnp.concatenate([window_blocks, arrived], axis=2)]
    all_to_all x1 -> x0, waiting for transfers between devices: 48.2 us -> none  [on_device(): lax.all_to_all(voltages, 'chan', split_axis=0, concat_axis=3, tiled=True)]
  transfers between devices with their start and end apart: 6 -> 76, of which waited for: 6 -> 20; matrix products, arithmetic and copies ran while one was open for 2% -> 0% of each run, Pallas kernels for 0% -> 17%
where the time goes in v1:
time: 355 us; the launch traced here: 354 us
  waiting for transfers between devices  143 us (40%)
  Pallas kernels  80.2 us (23%)
  starting transfers between devices  68.4 us (19%)
  local copies, waits for them, and re-layouts  57.7 us (16%)
  other arithmetic  3.94 us (1%)
    ppermute x72, waiting for transfers between devices, permute(): return lambda block: lax.ppermute(block, 'grp', route)  135 us
    pallas_call x4, Pallas kernels, correlate(): pl.pallas_call(functools.partial(pair_kernel, variants, parts, len(source...  80.2 us
    ppermute x72, starting transfers between devices, permute(): return lambda block: lax.ppermute(block, 'grp', route)  62.6 us
    unnamed x216, local copies, waits for them, and re-layouts  57.7 us
    ppermute x4, waiting for transfers between devices, split_exchange(): lax.ppermute(piece(1 - column, first, count), 'chan', [(0, 1), (1, 0)])  7.25 us
  transfers between devices with their start and end apart: 76, of which 20 were waited for; matrix products, arithmetic and copies ran while one was open for 0% of the time, Pallas kernels for 17%

profile of v1, /device:TPU:0, one launch (start us, length us, event | category | flops | bytes accessed | tf_op | source)
XLA Modules:
  0.0 353.7 jit_solution(10175439383919804968)
XLA Ops:
  0.7 2.5 dynamic-slice_multiply_fusion
  3.2 3.0 collective-permute-start.57
  6.2 3.6 %collective-permute-start.60 = (bf16[4,2,256,128]{3,2,1,0:T(8,128)(2,1)S(1)}, bf16[4,2,256,128]{3,2,1,0:T(8,128)(2,1)S(1)}, u32[]{:S(2)}, u32[]{:S(2)}) collective-permute-start(bf16[4,2,256,128]{3,2,1,0:T(8,128)(2,1)S(1)} %get-tuple-element.12.refs_0_), channel_id=1, source_target_pairs={{8,0},{10,2},{28,4},{30,6},{16,8},{18,10},{4,12},{6,14},{24,16},{2... | collective-permute-start | bytes 1572872 | tf_op jit(solution)/shard_map/ppermute | solution.py:109
  10.9 7.2 %collective-permute-done.57.refs_1_ = bf16[4,2,256,128]{3,2,1,0:T(8,128)(2,1)S(1)} collective-permute-done((bf16[4,2,256,128]{3,2,1,0:T(8,128)(2,1)S(1)}, bf16[4,2,256,128]{3,2,1,0:T(8,128)(2,1)S(1)}, u32[]{:S(2)}, u32[]{:S(2)}) %collective-permute-start.57) | collective-permute-done | bytes 524320 | tf_op jit(solution)/shard_map/ppermute | solution.py:163
  19.9 2.3 collective-permute-done.60.refs_6_
  22.2 4.3 %collective-permute-start.41 = (bf16[4,2,256,128]{3,2,1,0:T(8,128)(2,1)S(1)}, bf16[4,2,256,128]{3,2,1,0:T(8,128)(2,1)S(1)}, u32[]{:S(2)}, u32[]{:S(2)}) collective-permute-start(bf16[4,2,256,128]{3,2,1,0:T(8,128)(2,1)S(1)} %get-tuple-element.7.refs_0_), channel_id=1, source_target_pairs={{8,0},{10,2},{28,4},{30,6},{16,8},{18,10},{4,12},{6,14},{24,16},{2... | collective-permute-start | bytes 1572872 | tf_op jit(solution)/shard_map/ppermute | solution.py:109
  26.5 7.9 %collective-permute-done.64.refs_8_ = bf16[4,2,256,128]{3,2,1,0:T(8,128)(2,1)S(1)} collective-permute-done((bf16[4,2,256,128]{3,2,1,0:T(8,128)(2,1)S(1)}, bf16[4,2,256,128]{3,2,1,0:T(8,128)(2,1)S(1)}, u32[]{:S(2)}, u32[]{:S(2)}) %collective-permute-start.64) | collective-permute-done | bytes 524320 | tf_op jit(solution)/shard_map/ppermute | solution.py:109
  37.3 7.5 %collective-permute-done.41.refs_6_ = bf16[4,2,256,128]{3,2,1,0:T(8,128)(2,1)S(1)} collective-permute-done((bf16[4,2,256,128]{3,2,1,0:T(8,128)(2,1)S(1)}, bf16[4,2,256,128]{3,2,1,0:T(8,128)(2,1)S(1)}, u32[]{:S(2)}, u32[]{:S(2)}) %collective-permute-start.41) | collective-permute-done | bytes 524320 | tf_op jit(solution)/shard_map/ppermute | solution.py:109
  44.7 4.3 %collective-permute-start.22 = (bf16[4,2,256,128]{3,2,1,0:T(8,128)(2,1)S(1)}, bf16[4,2,256,128]{3,2,1,0:T(8,128)(2,1)S(1)}, u32[]{:S(2)}, u32[]{:S(2)}) collective-permute-start(bf16[4,2,256,128]{3,2,1,0:T(8,128)(2,1)S(1)} %get-tuple-element.9.refs_0_), channel_id=1, source_target_pairs={{8,0},{10,2},{28,4},{30,6},{16,8},{18,10},{4,12},{6,14},{24,16},{2... | collective-permute-start | bytes 1572872 | tf_op jit(solution)/shard_map/ppermute | solution.py:109
  49.0 5.4 %collective-permute-start.20 = (bf16[4,2,256,128]{3,2,1,0:T(8,128)(2,1)S(1)}, bf16[4,2,256,128]{3,2,1,0:T(8,128)(2,1)S(1)}, u32[]{:S(2)}, u32[]{:S(2)}) collective-permute-start(bf16[4,2,256,128]{3,2,1,0:T(8,128)(2,1)S(1)} %get-tuple-element.9.refs_0_), channel_id=1, source_target_pairs={{4,0},{6,2},{0,4},{2,6},{12,8},{14,10},{8,12},{10,14},{20,16},{22,... | collective-permute-start | bytes 1572872 | tf_op jit(solution)/shard_map/ppermute | solution.py:109
  54.5 2.4 collective-permute-done.45.refs_8_
  59.8 8.2 %collective-permute-done.22.refs_6_ = bf16[4,2,256,128]{3,2,1,0:T(8,128)(2,1)S(1)} collective-permute-done((bf16[4,2,256,128]{3,2,1,0:T(8,128)(2,1)S(1)}, bf16[4,2,256,128]{3,2,1,0:T(8,128)(2,1)S(1)}, u32[]{:S(2)}, u32[]{:S(2)}) %collective-permute-start.22) | collective-permute-done | bytes 524320 | tf_op jit(solution)/shard_map/ppermute | solution.py:109
  68.0 3.5 collective-permute-start.3
  71.5 5.9 %collective-permute-start.1 = (bf16[4,2,256,128]{3,2,1,0:T(8,128)(2,1)S(1)}, bf16[4,2,256,128]{3,2,1,0:T(8,128)(2,1)S(1)}, u32[]{:S(2)}, u32[]{:S(2)}) collective-permute-start(bf16[4,2,256,128]{3,2,1,0:T(8,128)(2,1)S(1)} %get-tuple-element.11.refs_0_), channel_id=1, source_target_pairs={{4,0},{6,2},{0,4},{2,6},{12,8},{14,10},{8,12},{10,14},{20,16},{22,... | collective-permute-start | bytes 1572872 | tf_op jit(solution)/shard_map/ppermute | solution.py:109
  84.0 6.7 %collective-permute-done.3.refs_6_ = bf16[4,2,256,128]{3,2,1,0:T(8,128)(2,1)S(1)} collective-permute-done((bf16[4,2,256,128]{3,2,1,0:T(8,128)(2,1)S(1)}, bf16[4,2,256,128]{3,2,1,0:T(8,128)(2,1)S(1)}, u32[]{:S(2)}, u32[]{:S(2)}) %collective-permute-start.3) | collective-permute-done | bytes 524320 | tf_op jit(solution)/shard_map/ppermute | solution.py:109
  90.7 3.9 %collective-permute-start.59 = (bf16[4,2,256,128]{3,2,1,0:T(8,128)(2,1)S(1)}, bf16[4,2,256,128]{3,2,1,0:T(8,128)(2,1)S(1)}, u32[]{:S(2)}, u32[]{:S(2)}) collective-permute-start(bf16[4,2,256,128]{3,2,1,0:T(8,128)(2,1)S(1)} %collective-permute-done.57.refs_1_), channel_id=1, source_target_pairs={{4,0},{6,2},{0,4},{2,6},{12,8},{14,10},{8,12},{10,14},{20,16},{22,... | collective-permute-start | bytes 1572872 | tf_op jit(solution)/shard_map/ppermute | solution.py:109
  94.7 7.2 %collective-permute-done.7.refs_8_ = bf16[4,2,256,128]{3,2,1,0:T(8,128)(2,1)S(1)} collective-permute-done((bf16[4,2,256,128]{3,2,1,0:T(8,128)(2,1)S(1)}, bf16[4,2,256,128]{3,2,1,0:T(8,128)(2,1)S(1)}, u32[]{:S(2)}, u32[]{:S(2)}) %collective-permute-start.7) | collective-permute-done | bytes 524320 | tf_op jit(solution)/shard_map/ppermute | solution.py:109
  105.1 7.9 %collective-permute-done.62.refs_7_ = bf16[4,2,256,128]{3,2,1,0:T(8,128)(2,1)S(1)} collective-permute-done((bf16[4,2,256,128]{3,2,1,0:T(8,128)(2,1)S(1)}, bf16[4,2,256,128]{3,2,1,0:T(8,128)(2,1)S(1)}, u32[]{:S(2)}, u32[]{:S(2)}) %collective-permute-start.62) | collective-permute-done | bytes 524320 | tf_op jit(solution)/shard_map/ppermute | solution.py:109
  116.3 6.6 %collective-permute-done.65.refs_9_ = bf16[4,2,256,128]{3,2,1,0:T(8,128)(2,1)S(1)} collective-permute-done((bf16[4,2,256,128]{3,2,1,0:T(8,128)(2,1)S(1)}, bf16[4,2,256,128]{3,2,1,0:T(8,128)(2,1)S(1)}, u32[]{:S(2)}, u32[]{:S(2)}) %collective-permute-start.65) | collective-permute-done | bytes 524320 | tf_op jit(solution)/shard_map/ppermute | solution.py:109
  122.9 3.4 collective-permute-start.43
  131.5 7.1 %collective-permute-done.43.refs_7_ = bf16[4,2,256,128]{3,2,1,0:T(8,128)(2,1)S(1)} collective-permute-done((bf16[4,2,256,128]{3,2,1,0:T(8,128)(2,1)S(1)}, bf16[4,2,256,128]{3,2,1,0:T(8,128)(2,1)S(1)}, u32[]{:S(2)}, u32[]{:S(2)}) %collective-permute-start.43) | collective-permute-done | bytes 524320 | tf_op jit(solution)/shard_map/ppermute | solution.py:109
  139.5 2.5 collective-permute-done.40.refs_3_
  141.9 9.9 %collective-permute-done.42.refs_4_ = bf16[4,2,256,128]{3,2,1,0:T(8,128)(2,1)S(1)} collective-permute-done((bf16[4,2,256,128]{3,2,1,0:T(8,128)(2,1)S(1)}, bf16[4,2,256,128]{3,2,1,0:T(8,128)(2,1)S(1)}, u32[]{:S(2)}, u32[]{:S(2)}) %collective-permute-start.42) | collective-permute-done | bytes 524320 | tf_op jit(solution)/shard_map/ppermute | solution.py:109
  160.7 17.6 %collective-permute-done.24.refs_7_ = bf16[4,2,256,128]{3,2,1,0:T(8,128)(2,1)} collective-permute-done((bf16[4,2,256,128]{3,2,1,0:T(8,128)(2,1)S(1)}, bf16[4,2,256,128]{3,2,1,0:T(8,128)(2,1)}, u32[]{:S(2)}, u32[]{:S(2)}) %collective-permute-start.24) | collective-permute-done | bytes 524320 | tf_op jit(solution)/shard_map/ppermute | solution.py:109
  189.4 17.4 %collective-permute-done.5.refs_7_ = bf16[4,2,256,128]{3,2,1,0:T(8,128)(2,1)S(1)} collective-permute-done((bf16[4,2,256,128]{3,2,1,0:T(8,128)(2,1)S(1)}, bf16[4,2,256,128]{3,2,1,0:T(8,128)(2,1)S(1)}, u32[]{:S(2)}, u32[]{:S(2)}) %collective-permute-start.5) | collective-permute-done | bytes 524320 | tf_op jit(solution)/shard_map/ppermute | solution.py:109
  217.6 6.6 %collective-permute-done.63.refs_5_ = bf16[4,2,256,128]{3,2,1,0:T(8,128)(2,1)} collective-permute-done((bf16[4,2,256,128]{3,2,1,0:T(8,128)(2,1)S(1)}, bf16[4,2,256,128]{3,2,1,0:T(8,128)(2,1)}, u32[]{:S(2)}, u32[]{:S(2)}) %collective-permute-start.63) | collective-permute-done | bytes 524320 | tf_op jit(solution)/shard_map/ppermute | solution.py:109
  231.2 6.4 %collective-permute-done.44.refs_5_ = bf16[4,2,256,128]{3,2,1,0:T(8,128)(2,1)S(1)} collective-permute-done((bf16[4,2,256,128]{3,2,1,0:T(8,128)(2,1)S(1)}, bf16[4,2,256,128]{3,2,1,0:T(8,128)(2,1)S(1)}, u32[]{:S(2)}, u32[]{:S(2)}) %collective-permute-start.44) | collective-permute-done | bytes 524320 | tf_op jit(solution)/shard_map/ppermute | solution.py:109
  241.8 8.5 %collective-permute-done.25.refs_5_ = bf16[4,2,256,128]{3,2,1,0:T(8,128)(2,1)} collective-permute-done((bf16[4,2,256,128]{3,2,1,0:T(8,128)(2,1)}, bf16[4,2,256,128]{3,2,1,0:T(8,128)(2,1)}, u32[]{:S(2)}, u32[]{:S(2)}) %collective-permute-start.25) | collective-permute-done | bytes 524320 | tf_op jit(solution)/shard_map/ppermute | solution.py:109
  270.4 20.4 %shard_map.37.refs_20_ = f32[1,9,16,256,512]{4,3,2,1,0:T(8,128)} custom-call(s32[10]{0:T(128)S(1)} %pad_add_fusion.table, bf16[4,2,256,128]{3,2,1,0:T(8,128)(2,1)S(1)} %get-tuple-element.12.refs_0_, bf16[4,2,256,128]{3,2,1,0:T(8,128)(2,1)S(1)} %copy-done.19, bf16[4,2,256,128]{3,2,1,0:T(8,128)(2,1)S(1)} %copy-done.27, ...), custom_call_target="tpu_custom_call" | custom-call | flops 4831838208 | bytes 28311552 | tf_op jit(solution)/shard_map/pallas_call | solution.py:83
  293.4 20.4 %shard_map.38.refs_20_ = f32[1,9,16,256,512]{4,3,2,1,0:T(8,128)} custom-call(s32[10]{0:T(128)S(1)} %pad_add_fusion.table, bf16[4,2,256,128]{3,2,1,0:T(8,128)(2,1)S(1)} %get-tuple-element.7.refs_0_, bf16[4,2,256,128]{3,2,1,0:T(8,128)(2,1)S(1)} %collective-permute-done.38.refs_1_, ...), custom_call_target="tpu_custom_call", output_to_operand_aliasing={{}: (21, {})} | custom-call | flops 4831838208 | bytes 28311552 | tf_op jit(solution)/shard_map/pallas_call | solution.py:83
  314.0 17.7 %shard_map.39.refs_20_ = f32[1,9,16,256,512]{4,3,2,1,0:T(8,128)} custom-call(s32[10]{0:T(128)S(1)} %pad_add_fusion.table, bf16[4,2,256,128]{3,2,1,0:T(8,128)(2,1)S(1)} %get-tuple-element.9.refs_0_, bf16[4,2,256,128]{3,2,1,0:T(8,128)(2,1)S(1)} %copy-done.5, bf16[4,2,256,128]{3,2,1,0:T(8,128)(2,1)S(1)} %copy-done.15, ...), custom_call_target="tpu_custom_call", output_to_operand_aliasing={{}: (21, {})} | custom-call | flops 4831838208 | bytes 28311552 | tf_op jit(solution)/shard_map/pallas_call | solution.py:83
  331.9 21.7 %shard_map.40 = f32[1,9,16,256,512]{4,3,2,1,0:T(8,128)} custom-call(s32[10]{0:T(128)S(1)} %pad_add_fusion.table, bf16[4,2,256,128]{3,2,1,0:T(8,128)(2,1)S(1)} %get-tuple-element.11.refs_0_, bf16[4,2,256,128]{3,2,1,0:T(8,128)(2,1)S(1)} %copy-done.3, bf16[4,2,256,128]{3,2,1,0:T(8,128)(2,1)S(1)} %copy-done.17, ...), custom_call_target="tpu_custom_call", output_to_operand_aliasing={{}: (21, {})} | custom-call | flops 4831838208 | bytes 28311552 | tf_op jit(solution)/shard_map/pallas_call | solution.py:83
  (343 shorter events, 92.7 us)
Async XLA Ops:
  9.8 24.6 %collective-permute-start.64 = (bf16[4,2,256,128]{3,2,1,0:T(8,128)(2,1)S(1)}, bf16[4,2,256,128]{3,2,1,0:T(8,128)(2,1)S(1)}, u32[]{:S(2)}, u32[]{:S(2)}) collective-permute-start(bf16[4,2,256,128]{3,2,1,0:T(8,128)(2,1)S(1)} %get-tuple-element.12.refs_0_), channel_id=1, source_target_pairs={{24,0},{26,2},{12,4},{14,6},{0,8},{2,10},{20,12},{22,14},{8,16},{1... | collective-permute-start | bytes 1572872 | tf_op jit(solution)/shard_map/ppermute | solution.py:109
  10.9 25.1 %collective-permute-start.66 = (bf16[4,2,256,128]{3,2,1,0:T(8,128)(2,1)S(1)}, bf16[4,2,256,128]{3,2,1,0:T(8,128)(2,1)S(1)}, u32[]{:S(2)}, u32[]{:S(2)}) collective-permute-start(bf16[4,2,256,128]{3,2,1,0:T(8,128)(2,1)S(1)} %get-tuple-element.12.refs_0_), channel_id=1, source_target_pairs={{2,0},{0,2},{6,4},{4,6},{10,8},{8,10},{14,12},{12,14},{18,16},{16,... | collective-permute-start | bytes 1572872 | tf_op jit(solution)/shard_map/ppermute | solution.py:109
  22.2 22.5 %collective-permute-start.41 = (bf16[4,2,256,128]{3,2,1,0:T(8,128)(2,1)S(1)}, bf16[4,2,256,128]{3,2,1,0:T(8,128)(2,1)S(1)}, u32[]{:S(2)}, u32[]{:S(2)}) collective-permute-start(bf16[4,2,256,128]{3,2,1,0:T(8,128)(2,1)S(1)} %get-tuple-element.7.refs_0_), channel_id=1, source_target_pairs={{8,0},{10,2},{28,4},{30,6},{16,8},{18,10},{4,12},{6,14},{24,16},{2... | collective-permute-start | bytes 1572872 | tf_op jit(solution)/shard_map/ppermute | solution.py:109
  26.5 22.5 %collective-permute-start.39 = (bf16[4,2,256,128]{3,2,1,0:T(8,128)(2,1)S(1)}, bf16[4,2,256,128]{3,2,1,0:T(8,128)(2,1)S(1)}, u32[]{:S(2)}, u32[]{:S(2)}) collective-permute-start(bf16[4,2,256,128]{3,2,1,0:T(8,128)(2,1)S(1)} %get-tuple-element.7.refs_0_), channel_id=1, source_target_pairs={{4,0},{6,2},{0,4},{2,6},{12,8},{14,10},{8,12},{10,14},{20,16},{22,... | collective-permute-start | bytes 1572872 | tf_op jit(solution)/shard_map/ppermute | solution.py:109
  44.7 23.3 %collective-permute-start.22 = (bf16[4,2,256,128]{3,2,1,0:T(8,128)(2,1)S(1)}, bf16[4,2,256,128]{3,2,1,0:T(8,128)(2,1)S(1)}, u32[]{:S(2)}, u32[]{:S(2)}) collective-permute-start(bf16[4,2,256,128]{3,2,1,0:T(8,128)(2,1)S(1)} %get-tuple-element.9.refs_0_), channel_id=1, source_target_pairs={{8,0},{10,2},{28,4},{30,6},{16,8},{18,10},{4,12},{6,14},{24,16},{2... | collective-permute-start | bytes 1572872 | tf_op jit(solution)/shard_map/ppermute | solution.py:109
  49.0 22.5 %collective-permute-start.20 = (bf16[4,2,256,128]{3,2,1,0:T(8,128)(2,1)S(1)}, bf16[4,2,256,128]{3,2,1,0:T(8,128)(2,1)S(1)}, u32[]{:S(2)}, u32[]{:S(2)}) collective-permute-start(bf16[4,2,256,128]{3,2,1,0:T(8,128)(2,1)S(1)} %get-tuple-element.9.refs_0_), channel_id=1, source_target_pairs={{4,0},{6,2},{0,4},{2,6},{12,8},{14,10},{8,12},{10,14},{20,16},{22,... | collective-permute-start | bytes 1572872 | tf_op jit(solution)/shard_map/ppermute | solution.py:109
  56.9 22.5 %collective-permute-start.26 = (bf16[4,2,256,128]{3,2,1,0:T(8,128)(2,1)S(1)}, bf16[4,2,256,128]{3,2,1,0:T(8,128)(2,1)S(1)}, u32[]{:S(2)}, u32[]{:S(2)}) collective-permute-start(bf16[4,2,256,128]{3,2,1,0:T(8,128)(2,1)S(1)} %get-tuple-element.9.refs_0_), channel_id=1, source_target_pairs={{24,0},{26,2},{12,4},{14,6},{0,8},{2,10},{20,12},{22,14},{8,16},{1... | collective-permute-start | bytes 1572872 | tf_op jit(solution)/shard_map/ppermute | solution.py:109
  59.3 22.5 %collective-permute-start = (bf16[4,2,256,128]{3,2,1,0:T(8,128)(2,1)S(1)}, bf16[4,2,256,128]{3,2,1,0:T(8,128)(2,1)S(1)}, u32[]{:S(2)}, u32[]{:S(2)}) collective-permute-start(bf16[4,2,256,128]{3,2,1,0:T(8,128)(2,1)S(1)} %get-tuple-element.10), channel_id=1, source_target_pairs={{0,1},{1,0},{2,3},{3,2},{4,5},{5,4},{6,7},{7,6},{8,9},{9,8},{10,11... | collective-permute-start | bytes 1572872 | tf_op jit(solution)/shard_map/ppermute | solution.py:163
  68.0 22.7 %collective-permute-start.3 = (bf16[4,2,256,128]{3,2,1,0:T(8,128)(2,1)S(1)}, bf16[4,2,256,128]{3,2,1,0:T(8,128)(2,1)S(1)}, u32[]{:S(2)}, u32[]{:S(2)}) collective-permute-start(bf16[4,2,256,128]{3,2,1,0:T(8,128)(2,1)S(1)} %get-tuple-element.11.refs_0_), channel_id=1, source_target_pairs={{8,0},{10,2},{28,4},{30,6},{16,8},{18,10},{4,12},{6,14},{24,16},{2... | collective-permute-start | bytes 1572872 | tf_op jit(solution)/shard_map/ppermute | solution.py:109
  71.5 23.1 %collective-permute-start.1 = (bf16[4,2,256,128]{3,2,1,0:T(8,128)(2,1)S(1)}, bf16[4,2,256,128]{3,2,1,0:T(8,128)(2,1)S(1)}, u32[]{:S(2)}, u32[]{:S(2)}) collective-permute-start(bf16[4,2,256,128]{3,2,1,0:T(8,128)(2,1)S(1)} %get-tuple-element.11.refs_0_), channel_id=1, source_target_pairs={{4,0},{6,2},{0,4},{2,6},{12,8},{14,10},{8,12},{10,14},{20,16},{22,... | collective-permute-start | bytes 1572872 | tf_op jit(solution)/shard_map/ppermute | solution.py:109
  79.4 22.5 %collective-permute-start.7 = (bf16[4,2,256,128]{3,2,1,0:T(8,128)(2,1)S(1)}, bf16[4,2,256,128]{3,2,1,0:T(8,128)(2,1)S(1)}, u32[]{:S(2)}, u32[]{:S(2)}) collective-permute-start(bf16[4,2,256,128]{3,2,1,0:T(8,128)(2,1)S(1)} %get-tuple-element.11.refs_0_), channel_id=1, source_target_pairs={{24,0},{26,2},{12,4},{14,6},{0,8},{2,10},{20,12},{22,14},{8,16},{1... | collective-permute-start | bytes 1572872 | tf_op jit(solution)/shard_map/ppermute | solution.py:109
  81.8 31.2 %collective-permute-start.62 = (bf16[4,2,256,128]{3,2,1,0:T(8,128)(2,1)S(1)}, bf16[4,2,256,128]{3,2,1,0:T(8,128)(2,1)S(1)}, u32[]{:S(2)}, u32[]{:S(2)}) collective-permute-start(bf16[4,2,256,128]{3,2,1,0:T(8,128)(2,1)S(1)} %collective-permute-done.57.refs_1_), channel_id=1, source_target_pairs={{8,0},{10,2},{28,4},{30,6},{16,8},{18,10},{4,12},{6,14},{24,16},{2... | collective-permute-start | bytes 1572872 | tf_op jit(solution)/shard_map/ppermute | solution.py:109
  90.7 23.1 %collective-permute-start.59 = (bf16[4,2,256,128]{3,2,1,0:T(8,128)(2,1)S(1)}, bf16[4,2,256,128]{3,2,1,0:T(8,128)(2,1)S(1)}, u32[]{:S(2)}, u32[]{:S(2)}) collective-permute-start(bf16[4,2,256,128]{3,2,1,0:T(8,128)(2,1)S(1)} %collective-permute-done.57.refs_1_), channel_id=1, source_target_pairs={{4,0},{6,2},{0,4},{2,6},{12,8},{14,10},{8,12},{10,14},{20,16},{22,... | collective-permute-start | bytes 1572872 | tf_op jit(solution)/shard_map/ppermute | solution.py:109
  127.9 23.9 %collective-permute-start.42 = (bf16[4,2,256,128]{3,2,1,0:T(8,128)(2,1)S(1)}, bf16[4,2,256,128]{3,2,1,0:T(8,128)(2,1)S(1)}, u32[]{:S(2)}, u32[]{:S(2)}) collective-permute-start(bf16[4,2,256,128]{3,2,1,0:T(8,128)(2,1)S(1)} %collective-permute-done.41.refs_6_), channel_id=1, source_target_pairs={{4,0},{6,2},{0,4},{2,6},{12,8},{14,10},{8,12},{10,14},{20,16},{22,... | collective-permute-start | bytes 1572872 | tf_op jit(solution)/shard_map/ppermute | solution.py:109
  152.6 25.7 %collective-permute-start.24 = (bf16[4,2,256,128]{3,2,1,0:T(8,128)(2,1)S(1)}, bf16[4,2,256,128]{3,2,1,0:T(8,128)(2,1)}, u32[]{:S(2)}, u32[]{:S(2)}) collective-permute-start(bf16[4,2,256,128]{3,2,1,0:T(8,128)(2,1)S(1)} %collective-permute-done.19.refs_1_), channel_id=1, source_target_pairs={{8,0},{10,2},{28,4},{30,6},{16,8},{18,10},{4,12},{6,14},{24,16},{2... | collective-permute-start | bytes 1572872 | tf_op jit(solution)/shard_map/ppermute | solution.py:109
  154.1 25.1 %collective-permute-start.21 = (bf16[4,2,256,128]{3,2,1,0:T(8,128)(2,1)S(1)}, bf16[4,2,256,128]{3,2,1,0:T(8,128)(2,1)}, u32[]{:S(2)}, u32[]{:S(2)}) collective-permute-start(bf16[4,2,256,128]{3,2,1,0:T(8,128)(2,1)S(1)} %collective-permute-done.19.refs_1_), channel_id=1, source_target_pairs={{4,0},{6,2},{0,4},{2,6},{12,8},{14,10},{8,12},{10,14},{20,16},{22,... | collective-permute-start | bytes 1572872 | tf_op jit(solution)/shard_map/ppermute | solution.py:109
  154.9 25.6 %collective-permute-start.23 = (bf16[4,2,256,128]{3,2,1,0:T(8,128)(2,1)S(1)}, bf16[4,2,256,128]{3,2,1,0:T(8,128)(2,1)}, u32[]{:S(2)}, u32[]{:S(2)}) collective-permute-start(bf16[4,2,256,128]{3,2,1,0:T(8,128)(2,1)S(1)} %collective-permute-done.22.refs_6_), channel_id=1, source_target_pairs={{4,0},{6,2},{0,4},{2,6},{12,8},{14,10},{8,12},{10,14},{20,16},{22,... | collective-permute-start | bytes 1572872 | tf_op jit(solution)/shard_map/ppermute | solution.py:109
  157.7 23.6 %collective-permute-start.27 = (bf16[4,2,256,128]{3,2,1,0:T(8,128)(2,1)S(1)}, bf16[4,2,256,128]{3,2,1,0:T(8,128)(2,1)S(1)}, u32[]{:S(2)}, u32[]{:S(2)}) collective-permute-start(bf16[4,2,256,128]{3,2,1,0:T(8,128)(2,1)S(1)} %collective-permute-done.19.refs_1_), channel_id=1, source_target_pairs={{24,0},{26,2},{12,4},{14,6},{0,8},{2,10},{20,12},{22,14},{8,16},{1... | collective-permute-start | bytes 1572872 | tf_op jit(solution)/shard_map/ppermute | solution.py:109
  181.3 25.6 %collective-permute-start.5 = (bf16[4,2,256,128]{3,2,1,0:T(8,128)(2,1)S(1)}, bf16[4,2,256,128]{3,2,1,0:T(8,128)(2,1)S(1)}, u32[]{:S(2)}, u32[]{:S(2)}) collective-permute-start(bf16[4,2,256,128]{3,2,1,0:T(8,128)(2,1)S(1)} %collective-permute-done.refs_1_), channel_id=1, source_target_pairs={{8,0},{10,2},{28,4},{30,6},{16,8},{18,10},{4,12},{6,14},{24,16},{2... | collective-permute-start | bytes 1572872 | tf_op jit(solution)/shard_map/ppermute | solution.py:109
  182.9 24.8 %collective-permute-start.2 = (bf16[4,2,256,128]{3,2,1,0:T(8,128)(2,1)S(1)}, bf16[4,2,256,128]{3,2,1,0:T(8,128)(2,1)S(1)}, u32[]{:S(2)}, u32[]{:S(2)}) collective-permute-start(bf16[4,2,256,128]{3,2,1,0:T(8,128)(2,1)S(1)} %collective-permute-done.refs_1_), channel_id=1, source_target_pairs={{4,0},{6,2},{0,4},{2,6},{12,8},{14,10},{8,12},{10,14},{20,16},{22,... | collective-permute-start | bytes 1572872 | tf_op jit(solution)/shard_map/ppermute | solution.py:109
  183.7 25.3 %collective-permute-start.4 = (bf16[4,2,256,128]{3,2,1,0:T(8,128)(2,1)S(1)}, bf16[4,2,256,128]{3,2,1,0:T(8,128)(2,1)S(1)}, u32[]{:S(2)}, u32[]{:S(2)}) collective-permute-start(bf16[4,2,256,128]{3,2,1,0:T(8,128)(2,1)S(1)} %collective-permute-done.3.refs_6_), channel_id=1, source_target_pairs={{4,0},{6,2},{0,4},{2,6},{12,8},{14,10},{8,12},{10,14},{20,16},{22,... | collective-permute-start | bytes 1572872 | tf_op jit(solution)/shard_map/ppermute | solution.py:109
  186.5 23.5 %collective-permute-start.8 = (bf16[4,2,256,128]{3,2,1,0:T(8,128)(2,1)S(1)}, bf16[4,2,256,128]{3,2,1,0:T(8,128)(2,1)S(1)}, u32[]{:S(2)}, u32[]{:S(2)}) collective-permute-start(bf16[4,2,256,128]{3,2,1,0:T(8,128)(2,1)S(1)} %collective-permute-done.refs_1_), channel_id=1, source_target_pairs={{24,0},{26,2},{12,4},{14,6},{0,8},{2,10},{20,12},{22,14},{8,16},{1... | collective-permute-start | bytes 1572872 | tf_op jit(solution)/shard_map/ppermute | solution.py:109
  241.2 49.7 %collective-permute-start.35 = (bf16[4,2,256,128]{3,2,1,0:T(8,128)(2,1)}, bf16[4,2,256,128]{3,2,1,0:T(8,128)(2,1)S(1)}, u32[]{:S(2)}, u32[]{:S(2)}) collective-permute-start(bf16[4,2,256,128]{3,2,1,0:T(8,128)(2,1)} %collective-permute-done.24.refs_7_), channel_id=1, source_target_pairs={{2,0},{0,2},{6,4},{4,6},{10,8},{8,10},{14,12},{12,14},{18,16},{16,... | collective-permute-start | bytes 1572872 | tf_op jit(solution)/shard_map/ppermute | solution.py:109
  250.3 40.9 %collective-permute-start.37 = (bf16[4,2,256,128]{3,2,1,0:T(8,128)(2,1)}, bf16[4,2,256,128]{3,2,1,0:T(8,128)(2,1)S(1)}, u32[]{:S(2)}, u32[]{:S(2)}) collective-permute-start(bf16[4,2,256,128]{3,2,1,0:T(8,128)(2,1)} %copy-done.66), channel_id=1, source_target_pairs={{2,0},{0,2},{6,4},{4,6},{10,8},{8,10},{14,12},{12,14},{18,16},{16,... | collective-permute-start | bytes 1572872 | tf_op jit(solution)/shard_map/ppermute | solution.py:109
  250.3 41.2 %collective-permute-start.6 = (bf16[4,2,256,128]{3,2,1,0:T(8,128)(2,1)}, bf16[4,2,256,128]{3,2,1,0:T(8,128)(2,1)S(1)}, u32[]{:S(2)}, u32[]{:S(2)}) collective-permute-start(bf16[4,2,256,128]{3,2,1,0:T(8,128)(2,1)} %copy-done.68), channel_id=1, source_target_pairs={{4,0},{6,2},{0,4},{2,6},{12,8},{14,10},{8,12},{10,14},{20,16},{22,... | collective-permute-start | bytes 1572872 | tf_op jit(solution)/shard_map/ppermute | solution.py:109
  251.3 40.4 %collective-permute-start.52 = (bf16[4,2,256,128]{3,2,1,0:T(8,128)(2,1)}, bf16[4,2,256,128]{3,2,1,0:T(8,128)(2,1)S(1)}, u32[]{:S(2)}, u32[]{:S(2)}) collective-permute-start(bf16[4,2,256,128]{3,2,1,0:T(8,128)(2,1)} %copy-done.92), channel_id=1, source_target_pairs={{2,0},{0,2},{6,4},{4,6},{10,8},{8,10},{14,12},{12,14},{18,16},{16,... | collective-permute-start | bytes 1572872 | tf_op jit(solution)/shard_map/ppermute | solution.py:109
  251.5 40.5 %collective-permute-start.33 = (bf16[4,2,256,128]{3,2,1,0:T(8,128)(2,1)}, bf16[4,2,256,128]{3,2,1,0:T(8,128)(2,1)S(1)}, u32[]{:S(2)}, u32[]{:S(2)}) collective-permute-start(bf16[4,2,256,128]{3,2,1,0:T(8,128)(2,1)} %collective-permute-done.25.refs_5_), channel_id=1, source_target_pairs={{2,0},{0,2},{6,4},{4,6},{10,8},{8,10},{14,12},{12,14},{18,16},{16,... | collective-permute-start | bytes 1572872 | tf_op jit(solution)/shard_map/ppermute | solution.py:109
  290.9 40.8 %collective-permute-start.16 = (bf16[4,2,256,128]{3,2,1,0:T(8,128)(2,1)S(1)}, bf16[4,2,256,128]{3,2,1,0:T(8,128)(2,1)S(1)}, u32[]{:S(2)}, u32[]{:S(2)}) collective-permute-start(bf16[4,2,256,128]{3,2,1,0:T(8,128)(2,1)S(1)} %copy-done.69), channel_id=1, source_target_pairs={{2,0},{0,2},{6,4},{4,6},{10,8},{8,10},{14,12},{12,14},{18,16},{16,... | collective-permute-start | bytes 1572872 | tf_op jit(solution)/shard_map/ppermute | solution.py:109
  291.2 40.5 %collective-permute-start.12 = (bf16[4,2,256,128]{3,2,1,0:T(8,128)(2,1)S(1)}, bf16[4,2,256,128]{3,2,1,0:T(8,128)(2,1)S(1)}, u32[]{:S(2)}, u32[]{:S(2)}) collective-permute-start(bf16[4,2,256,128]{3,2,1,0:T(8,128)(2,1)S(1)} %copy-done.73), channel_id=1, source_target_pairs={{2,0},{0,2},{6,4},{4,6},{10,8},{8,10},{14,12},{12,14},{18,16},{16,... | collective-permute-start | bytes 1572872 | tf_op jit(solution)/shard_map/ppermute | solution.py:109
  291.5 40.2 %collective-permute-start.13 = (bf16[4,2,256,128]{3,2,1,0:T(8,128)(2,1)S(1)}, bf16[4,2,256,128]{3,2,1,0:T(8,128)(2,1)S(1)}, u32[]{:S(2)}, u32[]{:S(2)}) collective-permute-start(bf16[4,2,256,128]{3,2,1,0:T(8,128)(2,1)S(1)} %copy-done.77), channel_id=1, source_target_pairs={{2,0},{0,2},{6,4},{4,6},{10,8},{8,10},{14,12},{12,14},{18,16},{16,... | collective-permute-start | bytes 1572872 | tf_op jit(solution)/shard_map/ppermute | solution.py:109
  291.8 40.0 %collective-permute-start.18 = (bf16[4,2,256,128]{3,2,1,0:T(8,128)(2,1)S(1)}, bf16[4,2,256,128]{3,2,1,0:T(8,128)(2,1)S(1)}, u32[]{:S(2)}, u32[]{:S(2)}) collective-permute-start(bf16[4,2,256,128]{3,2,1,0:T(8,128)(2,1)S(1)} %copy-done.81), channel_id=1, source_target_pairs={{2,0},{0,2},{6,4},{4,6},{10,8},{8,10},{14,12},{12,14},{18,16},{16,... | collective-permute-start | bytes 1572872 | tf_op jit(solution)/shard_map/ppermute | solution.py:109
  292.0 39.7 %collective-permute-start.14 = (bf16[4,2,256,128]{3,2,1,0:T(8,128)(2,1)S(1)}, bf16[4,2,256,128]{3,2,1,0:T(8,128)(2,1)S(1)}, u32[]{:S(2)}, u32[]{:S(2)}) collective-permute-start(bf16[4,2,256,128]{3,2,1,0:T(8,128)(2,1)S(1)} %collective-permute-done.6.refs_5_), channel_id=1, source_target_pairs={{2,0},{0,2},{6,4},{4,6},{10,8},{8,10},{14,12},{12,14},{18,16},{16,... | collective-permute-start | bytes 1572872 | tf_op jit(solution)/shard_map/ppermute | solution.py:109
  (152 other events, 1747.8 us)

commit v2 on v1

v2 whole, which is shorter than its diff:
```python
import functools

import jax
import jax.numpy as jnp
from jax import lax
from jax.experimental import pallas as pl
from jax.experimental.pallas import tpu as pltpu
from jax.sharding import PartitionSpec as P


def pair_kernel(variants, parts, blocks, joined, table, *refs):
    width = len(variants[0])
    sources = refs[:blocks]
    out, window, sems = refs[-3:]
    step = pl.program_id(0)
    steps = pl.num_programs(0)

    def copy(source, channel, slot, entry, part):
        if joined:
            block = sources[source].at[part, channel]
        else:
            block = sources[source * parts + part].at[channel]
        return pltpu.make_async_copy(block, window.at[slot, entry, part], sems.at[slot, entry, part])

    def fetch(channel, slot):
        for at, variant in enumerate(variants):

            @pl.when(table[0] == at)
            def _():
                for entry, source in enumerate(variant):
                    for part in range(parts):
                        copy(source, channel, slot, entry, part).start()

    @pl.when(step == 0)
    def _():
        fetch(0, 0)

    @pl.when(step + 1 < steps)
    def _():
        fetch(step + 1, lax.rem(step + 1, 2))

    slot = lax.rem(step, 2)
    for entry in range(width):
        for part in range(parts):
            copy(0, 0, slot, entry, part).wait()

    half = width // 2
    size = window.shape[-2]
    scale = jnp.float32(1.0 / (parts * window.shape[-1]))
    contract = (((1,), (1,)), ((), ()))

    def pair(d, carry):
        a = half - d // 2
        b = half + (d + 1) // 2
        left, real, imag = [], [], []
        for part in range(parts):
            b_r, b_i = window[slot, b, part, 0], window[slot, b, part, 1]
            left += [window[slot, a, part, 0], window[slot, a, part, 1]]
            real += [b_r, b_i]
            imag += [-b_i, b_r]
        left = jnp.concatenate(left, axis=1)
        for at, right in enumerate((real, imag)):
            sums = lax.dot_general(
                left, jnp.concatenate(right, axis=1), contract, preferred_element_type=jnp.float32
            )
            out[0, table[1 + d], 0, :, at * size : (at + 1) * size] = sums * scale
        return carry

    if width <= 9:
        for d in range(width):
            pair(d, 0)
    else:
        lax.fori_loop(0, width, pair, 0)


def correlate(blocks, variants, table, first, channels, previous):
    joined = not isinstance(blocks[0], (list, tuple))
    sources = list(blocks) if joined else [array for block in blocks for array in block]
    parts = sources[0].shape[0] if joined else len(blocks[0])
    count, _, size, samples = sources[0].shape[-4:]
    width = len(variants[0])
    out_shape = (1, width, channels, size, 2 * size)
    operands = sources + ([] if previous is None else [previous])
    return pl.pallas_call(
        functools.partial(pair_kernel, variants, parts, len(sources), joined),
        out_shape=jax.ShapeDtypeStruct(out_shape, jnp.float32),
        grid_spec=pltpu.PrefetchScalarGridSpec(
            num_scalar_prefetch=1,
            grid=(count,),
            in_specs=[pl.BlockSpec(memory_space=pltpu.HBM)] * len(operands),
            out_specs=pl.BlockSpec((1, width, 1, size, 2 * size), lambda c, t: (0, 0, first + c, 0, 0)),
            scratch_shapes=[
                pltpu.VMEM((2, width, parts, 2, size, samples), jnp.bfloat16),
                pltpu.SemaphoreType.DMA((2, width, parts)),
            ],
        ),
        input_output_aliases={} if previous is None else {len(operands): 0},
        compiler_params=pltpu.CompilerParams(dimension_semantics=("arbitrary",)),
        cost_estimate=pl.CostEstimate(
            flops=8 * count * width * size * size * parts * samples,
            bytes_accessed=count * width * size * (8 * size + 4 * parts * samples),
            transcendentals=0,
        ),
    )(table, *operands)


def after(kept, tokens):
    operands = list(kept) + list(tokens)
    return pl.pallas_call(
        lambda *refs: None,
        out_shape=tuple(jax.ShapeDtypeStruct(array.shape, array.dtype) for array in kept),
        in_specs=[pl.BlockSpec(memory_space=pltpu.HBM)] * len(operands),
        out_specs=(pl.BlockSpec(memory_space=pltpu.HBM),) * len(kept),
        input_output_aliases={at: at for at in range(len(kept))},
        cost_estimate=pl.CostEstimate(flops=0, bytes_accessed=0, transcendentals=0),
    )(*operands)


def permute(axis, route):
    return lambda block: lax.ppermute(block, axis, route)


class Piece:
    def __init__(self, own, moves):
        self.own = own
        self.forward, self.straight, self.across, self.twin = moves

    def near(self):
        self.theirs = self.forward(self.own)
        self.partner = self.across(self.own)

    def near_twins(self):
        twins = self.twin([self.own, self.theirs, self.partner])
        self.own_twin, self.theirs_twin, self.partner_twin = twins
        return twins

    def far(self):
        self.others = self.straight(self.own)
        self.passed = self.across(self.theirs)

    def far_twins(self):
        twins = self.twin([self.others, self.passed])
        self.others_twin, self.passed_twin = twins
        return twins

    def blocks(self):
        return [
            self.own,
            self.partner,
            self.passed,
            self.theirs,
            self.others,
            self.own_twin,
            self.partner_twin,
            self.passed_twin,
            self.theirs_twin,
            self.others_twin,
        ]


def split_exchange(voltages, weights, table, chunks):
    devices = lax.axis_size("grp")
    plane = devices // 4
    channels = voltages.shape[0] // 2
    me = lax.axis_index("grp")
    column = lax.axis_index("chan")

    def behind(i):
        return (i - plane) % devices

    def beyond(i):
        return (i + plane) % devices

    def upper(i):
        return i % plane >= plane // 2

    everyone = range(devices)
    forward = permute("grp", [(behind(i) if upper(i) else beyond(i), i) for i in everyone])
    straight = permute("grp", [(beyond(i) if upper(i) else behind(i), i) for i in everyone])
    across = permute("grp", [(i ^ (plane // 2), i) for i in everyone])
    swap = permute("grp", [(i ^ 1, i) for i in everyone])
    in_order = table[0] >= 0

    def twin(blocks):
        return lax.cond(
            in_order,
            lambda given: [swap(block) for block in given],
            lambda given: [jnp.zeros_like(block) for block in given],
            list(blocks),
        )

    turn = permute("chan", [(0, 1), (1, 0)])
    moves = (forward, straight, across, twin)

    own, partner, passed, theirs, others = range(5)
    variants = []
    for y in range(2):
        chips = (others, passed, own, partner, theirs) if y == 0 else (theirs, partner, own, passed, others)
        for core in range(2):
            entries = []
            for j in range(-plane, plane + 1):
                chip = chips[(core + j) // 2 + 2]
                entries.append(chip if (core + j) % 2 == core else chip + 5)
            variants.append(tuple(entries))
    variants = tuple(variants)
    position = lax.rem(me, plane)
    table = jnp.concatenate([position[None].astype(jnp.int32), table])

    columns = voltages.reshape(2, channels, *voltages.shape[1:])
    firsts = [sum(chunks[:at]) for at in range(len(chunks))]
    stay, go = [
        lax.dynamic_slice_in_dim(voltages, of * channels, chunks[0], axis=0) * weights
        for of in (column, 1 - column)
    ]
    pieces = [Piece(stay, moves), Piece(turn(go), moves)]

    def turned(at, token):
        mine = columns[:, firsts[at] : firsts[at] + chunks[at]] * weights
        (mine,) = after([mine], [token])
        return Piece(lax.all_to_all(mine, "chan", split_axis=0, concat_axis=0), moves)

    pieces.append(turned(1, pieces[1].own))

    count = len(chunks) + 1
    steps = [("near", 0), ("near", 1)]
    for at in range(count - 2):
        steps += [("far", at), ("near", at + 2)]
    steps += [("far", count - 2), ("far", count - 1)]

    def kernel(at, result):
        if at == 0:
            blocks = list(zip(pieces[0].blocks(), pieces[1].blocks()))
        else:
            blocks = pieces[at + 1].blocks()
        return correlate(blocks, variants, table, firsts[at], channels, result)

    result, ready, shared = None, [], []

    def share(step, token):
        nonlocal result
        kind, at = steps[step]
        piece = pieces[at]
        if kind == "near":
            if token is not None:
                piece.theirs, piece.partner = after([piece.theirs, piece.partner], [token])
            shared.append(piece.near_twins())
        else:
            if token is not None:
                piece.others, piece.passed = after([piece.others, piece.passed], [token])
            shared.append(piece.far_twins())
            if at >= 1:
                result = kernel(at - 1, result)
                ready.append(step + 3)

    token = None
    for step, (kind, at) in enumerate(steps):
        piece = pieces[at]
        if step >= 2:
            share(step - 2, token)
            kept, waits = [piece.own], list(shared[step - 2])
            if kind == "far":
                kept.append(piece.theirs)
                waits += [piece.partner, piece.own_twin, piece.theirs_twin]
                if ready and ready[0] <= step:
                    ready.pop(0)
                    kept.append(result)
            kept = after(kept, waits)
            piece.own = kept[0]
            if kind == "far":
                piece.theirs = kept[1]
                if len(kept) == 3:
                    result = kept[2]
            token = piece.own
        if kind == "near":
            piece.near()
            if 2 <= at < count - 1:
                pieces.append(turned(at, piece.own))
        else:
            piece.far()
    share(len(steps) - 2, token)
    share(len(steps) - 1, None)
    return result


def window_exchange(voltages, weights, table):
    turned = lax.all_to_all(voltages * weights, "chan", split_axis=0, concat_axis=3, tiled=True)
    devices = lax.axis_size("grp")
    quarter = devices // 4
    width = 2 * quarter + 1

    def from_behind(block, distance):
        return lax.ppermute(block, "grp", [((i - distance) % devices, i) for i in range(devices)])

    window = [from_behind(turned, quarter)]
    while len(window) < width:
        window += [from_behind(block, -len(window)) for block in window[: width - len(window)]]
    table = jnp.concatenate([jnp.zeros((1,), jnp.int32), table])
    return correlate([[block] for block in window], (tuple(range(width)),), table, 0, turned.shape[0], None)


def on_device(voltages, input_flags, pair_order):
    weights = input_flags.astype(jnp.bfloat16)[None, None, :, None]
    if lax.axis_size("grp") == 16 and lax.axis_size("chan") == 2:
        return split_exchange(voltages, weights, pair_order, (6, 6, 4))
    return window_exchange(voltages, weights, pair_order)


def solution(mesh):
    return jax.shard_map(
        on_device,
        mesh=mesh,
        in_specs=(P(None, None, "grp", "chan"), P("grp"), P()),
        out_specs=P("grp", None, "chan", None, None),
        check_vma=False,
    )
```

time: 355 us -> 244 us (0.69)
  local copies, waits for them, and re-layouts: 57.7 us -> 0.01 us
  Pallas kernels: 80.2 us -> 50 us
  starting transfers between devices: 68.4 us -> 50.7 us
  waiting for transfers between devices: 143 us -> 134 us
  other arithmetic: 3.94 us -> 7.96 us
    unnamed x216 -> x4, local copies, waits for them, and re-layouts: 57.7 us -> 0.01 us
    pallas_call x4 -> x3, Pallas kernels: 80.2 us -> 50 us  [correlate(): pl.pallas_call(functools.partial(pair_kernel, variants, parts, len(source...]
    ppermute x76 -> x37, starting transfers between devices: 68.4 us -> 43.3 us  [permute(): return lambda block: lax.ppermute(block, axis, route)]
    ppermute x76 -> x37, waiting for transfers between devices: 143 us -> 134 us  [permute(): return lambda block: lax.ppermute(block, axis, route)]
    all_to_all x0 -> x2, starting transfers between devices: none -> 7.39 us  [turned(): lax.all_to_all(mine, 'chan', split_axis=0, concat_axis=0)]
    mul x1 -> x3, other arithmetic: 2.53 us -> 6.63 us  [the longest x2 5.09 us: turned(): mine = columns[:, firsts[at]:firsts[at] + chunks[at]] * weights]
  transfers between devices with their start and end apart: 76 -> 39, of which waited for: 20 -> 31; matrix products, arithmetic and copies ran while one was open for 0% -> 2% of each run, Pallas kernels for 17% -> 15%
where the time goes in v2:
time: 244 us; the launch traced here: 243 us
  waiting for transfers between devices  134 us (55%)
  starting transfers between devices  50.7 us (21%)
  Pallas kernels  50 us (20%)
  other arithmetic  7.96 us (3%)
    ppermute x37, waiting for transfers between devices, permute(): return lambda block: lax.ppermute(block, axis, route)  134 us
    pallas_call x3, Pallas kernels, correlate(): pl.pallas_call(functools.partial(pair_kernel, variants, parts, len(source...  50 us
    ppermute x37, starting transfers between devices, permute(): return lambda block: lax.ppermute(block, axis, route)  43.3 us
    all_to_all x2, starting transfers between devices, turned(): lax.all_to_all(mine, 'chan', split_axis=0, concat_axis=0)  7.39 us
    mul x2, other arithmetic, turned(): mine = columns[:, firsts[at]:firsts[at] + chunks[at]] * weights  5.09 us
  transfers between devices with their start and end apart: 39, of which 31 were waited for; matrix products, arithmetic and copies ran while one was open for 2% of the time, Pallas kernels for 15%

profile of v2, /device:TPU:0, one launch (start us, length us, event | category | flops | bytes accessed | tf_op | source)
XLA Modules:
  0.0 242.9 jit_solution(16187278959981662954)
XLA Ops:
  2.2 3.0 %collective-permute-start.20 = (bf16[6,2,256,128]{3,2,1,0:T(8,128)(2,1)S(1)}, bf16[6,2,256,128]{3,2,1,0:T(8,128)(2,1)}, u32[]{:S(2)}, u32[]{:S(2)}) collective-permute-start(bf16[6,2,256,128]{3,2,1,0:T(8,128)(2,1)S(1)} %get-tuple-element.148), channel_id=1, source_target_pairs={{0,1},{1,0},{2,3},{3,2},{4,5},{5,4},{6,7},{7,6},{8,9},{9,8},{10,11... | collective-permute-start | bytes 2359304 | tf_op jit(solution)/shard_map/ppermute | solution.py:120
  6.8 3.6 %collective-permute-start.23 = (bf16[6,2,256,128]{3,2,1,0:T(8,128)(2,1)S(1)}, bf16[6,2,256,128]{3,2,1,0:T(8,128)(2,1)}, u32[]{:S(2)}, u32[]{:S(2)}) collective-permute-start(bf16[6,2,256,128]{3,2,1,0:T(8,128)(2,1)S(1)} %get-tuple-element.147.refs_0_), channel_id=1, source_target_pairs={{8,0},{10,2},{28,4},{30,6},{16,8},{18,10},{4,12},{6,14},{24,16},{2... | collective-permute-start | bytes 2359304 | tf_op jit(solution)/shard_map/ppermute | solution.py:120
  10.4 12.5 %collective-permute-done.20.refs_1_.refs_0_ = bf16[6,2,256,128]{3,2,1,0:T(8,128)(2,1)} collective-permute-done((bf16[6,2,256,128]{3,2,1,0:T(8,128)(2,1)S(1)}, bf16[6,2,256,128]{3,2,1,0:T(8,128)(2,1)}, u32[]{:S(2)}, u32[]{:S(2)}) %collective-permute-start.20) | collective-permute-done | bytes 786464 | tf_op jit(solution)/shard_map/ppermute | solution.py:120
  22.9 3.8 %collective-permute-start.21 = (bf16[6,2,256,128]{3,2,1,0:T(8,128)(2,1)}, bf16[6,2,256,128]{3,2,1,0:T(8,128)(2,1)}, u32[]{:S(2)}, u32[]{:S(2)}) collective-permute-start(bf16[6,2,256,128]{3,2,1,0:T(8,128)(2,1)} %collective-permute-done.20.refs_1_.refs_0_), channel_id=1, source_target_pairs={{8,0},{10,2},{28,4},{30,6},{16,8},{18,10},{4,12},{6,14},{24,16},{2... | collective-permute-start | bytes 2359304 | tf_op jit(solution)/shard_map/ppermute | solution.py:120
  26.7 2.7 %slice_multiply_fusion.refs_0_ = bf16[2,6,2,256,128]{4,3,2,1,0:T(8,128)(2,1)} fusion(bf16[2,16,2,256,128]{4,3,2,1,0:T(8,128)(2,1)} %bitcast.4, bf16[256]{0:T(256)(128)(2,1)S(1)} %convert_element_type.7), kind=kLoop, calls=%fused_computation | loop fusion | flops 786432 | bytes 3146240 | tf_op jit(solution)/shard_map/mul | solution.py:218
  29.5 3.8 %all-to-all-start = ((bf16[2,6,2,256,128]{4,3,2,1,0:T(8,128)(2,1)}), bf16[2,6,2,256,128]{4,3,2,1,0:T(8,128)(2,1)S(1)}, u32[]{:S(2)}, u32[]{:S(2)}) async-start(bf16[2,6,2,256,128]{4,3,2,1,0:T(8,128)(2,1)} %shard_map.37), calls=%async_computation | async-start | bytes 3145728 | tf_op jit(solution)/shard_map/all_to_all | solution.py:220
  33.4 5.0 %conditional.8 = (bf16[6,2,256,128]{3,2,1,0:T(8,128)(2,1)}, bf16[6,2,256,128]{3,2,1,0:T(8,128)(2,1)}, bf16[6,2,256,128]{3,2,1,0:T(8,128)(2,1)}) conditional(s32[]{:T(128)} %bitcast.2, () %tuple.67, (bf16[6,2,256,128]{3,2,1,0:T(8,128)(2,1)S(1)}, bf16[6,2,256,128]{3,2,1,0:T(8,128)(2,1)}, bf16[6,2,256,128]{3,2,1,0:T(8,128)(2,1)}) %tuple.68), branch_computations={%region_0.0_spmd, %region_1.0_spmd} | conditional | bytes 9437328 | solution.py:185
  40.8 4.3 %collective-permute-done.21.refs_0_ = bf16[6,2,256,128]{3,2,1,0:T(8,128)(2,1)} collective-permute-done((bf16[6,2,256,128]{3,2,1,0:T(8,128)(2,1)}, bf16[6,2,256,128]{3,2,1,0:T(8,128)(2,1)}, u32[]{:S(2)}, u32[]{:S(2)}) %collective-permute-start.21) | collective-permute-done | bytes 786464 | tf_op jit(solution)/shard_map/ppermute | solution.py:120
  47.4 4.9 %conditional.9 = (bf16[6,2,256,128]{3,2,1,0:T(8,128)(2,1)}, bf16[6,2,256,128]{3,2,1,0:T(8,128)(2,1)}, bf16[6,2,256,128]{3,2,1,0:T(8,128)(2,1)}) conditional(s32[]{:T(128)} %bitcast.2, () %tuple.66, (bf16[6,2,256,128]{3,2,1,0:T(8,128)(2,1)}, bf16[6,2,256,128]{3,2,1,0:T(8,128)(2,1)}, bf16[6,2,256,128]{3,2,1,0:T(8,128)(2,1)S(1)}) %tuple.69), branch_computations={%region_2.0_spmd, %region_3.0_spmd} | conditional | bytes 9437328 | solution.py:185
  54.3 8.6 %collective-permute-done.27.refs_0_ = bf16[6,2,256,128]{3,2,1,0:T(8,128)(2,1)} collective-permute-done((bf16[6,2,256,128]{3,2,1,0:T(8,128)(2,1)S(1)}, bf16[6,2,256,128]{3,2,1,0:T(8,128)(2,1)}, u32[]{:S(2)}, u32[]{:S(2)}) %collective-permute-start.27) | collective-permute-done | bytes 786464 | tf_op jit(solution)/shard_map/ppermute | solution.py:120
  64.4 3.8 %conditional.10 = (bf16[6,2,256,128]{3,2,1,0:T(8,128)(2,1)}, bf16[6,2,256,128]{3,2,1,0:T(8,128)(2,1)}) conditional(s32[]{:T(128)} %bitcast.2, () %tuple.71, (bf16[6,2,256,128]{3,2,1,0:T(8,128)(2,1)}, bf16[6,2,256,128]{3,2,1,0:T(8,128)(2,1)}) %shard_map.42), branch_computations={%region_4.0_spmd, %region_5.0_spmd} | conditional | bytes 6291552 | solution.py:185
  68.1 2.8 %collective-permute-start.31 = (bf16[6,2,256,128]{3,2,1,0:T(8,128)(2,1)}, bf16[6,2,256,128]{3,2,1,0:T(8,128)(2,1)}, u32[]{:S(2)}, u32[]{:S(2)}) collective-permute-start(bf16[6,2,256,128]{3,2,1,0:T(8,128)(2,1)} %get-tuple-element.118.refs_2_.refs_1_), channel_id=1, source_target_pairs={{24,0},{26,2},{12,4},{14,6},{0,8},{2,10},{20,12},{22,14},{8,16},{1... | collective-permute-start | bytes 2359304 | tf_op jit(solution)/shard_map/ppermute | solution.py:120
  74.0 3.6 %all-to-all-start.1 = ((bf16[2,4,2,256,128]{4,3,2,1,0:T(8,128)(2,1)}), bf16[2,4,2,256,128]{4,3,2,1,0:T(8,128)(2,1)S(1)}, u32[]{:S(2)}, u32[]{:S(2)}) async-start(bf16[2,4,2,256,128]{4,3,2,1,0:T(8,128)(2,1)} %shard_map.41), calls=%async_computation.1 | async-start | bytes 2097152 | tf_op jit(solution)/shard_map/all_to_all | solution.py:220
  77.6 19.0 %collective-permute-done.25.refs_0_ = bf16[2,6,2,256,128]{4,3,2,1,0:T(8,128)(2,1)} collective-permute-done((bf16[2,6,2,256,128]{4,3,2,1,0:T(8,128)(2,1)S(1)}, bf16[2,6,2,256,128]{4,3,2,1,0:T(8,128)(2,1)}, u32[]{:S(2)}, u32[]{:S(2)}) %collective-permute-start.25) | collective-permute-done | bytes 1572896 | tf_op jit(solution)/shard_map/ppermute | solution.py:120
  98.1 8.3 %conditional.11 = (bf16[2,6,2,256,128]{4,3,2,1,0:T(8,128)(2,1)}, bf16[2,6,2,256,128]{4,3,2,1,0:T(8,128)(2,1)}, bf16[2,6,2,256,128]{4,3,2,1,0:T(8,128)(2,1)}) conditional(s32[]{:T(128)} %bitcast.2, () %tuple.70, (bf16[2,6,2,256,128]{4,3,2,1,0:T(8,128)(2,1)S(1)}, bf16[2,6,2,256,128]{4,3,2,1,0:T(8,128)(2,1)}, ...), branch_computations={%region_6.0_spmd, %region_7.0_spmd} | conditional | bytes 18874512 | solution.py:185
  98.6 5.4 %collective-permute-done.10 = bf16[2,6,2,256,128]{4,3,2,1,0:T(8,128)(2,1)} collective-permute-done((bf16[2,6,2,256,128]{4,3,2,1,0:T(8,128)(2,1)}, bf16[2,6,2,256,128]{4,3,2,1,0:T(8,128)(2,1)}, u32[]{:S(2)}, u32[]{:S(2)}) %collective-permute-start.10) | collective-permute-done | bytes 1572896 | tf_op jit(solution)/shard_map/cond/branch_1_fun/ppermute | solution.py:120
  106.3 5.6 %collective-permute-done.31.refs_0_ = bf16[6,2,256,128]{3,2,1,0:T(8,128)(2,1)} collective-permute-done((bf16[6,2,256,128]{3,2,1,0:T(8,128)(2,1)}, bf16[6,2,256,128]{3,2,1,0:T(8,128)(2,1)}, u32[]{:S(2)}, u32[]{:S(2)}) %collective-permute-start.31) | collective-permute-done | bytes 786464 | tf_op jit(solution)/shard_map/ppermute | solution.py:120
  112.6 3.8 %conditional.12 = (bf16[6,2,256,128]{3,2,1,0:T(8,128)(2,1)}, bf16[6,2,256,128]{3,2,1,0:T(8,128)(2,1)}) conditional(s32[]{:T(128)} %bitcast.2, () %tuple.73, (bf16[6,2,256,128]{3,2,1,0:T(8,128)(2,1)}, bf16[6,2,256,128]{3,2,1,0:T(8,128)(2,1)}) %shard_map.46), branch_computations={%region_8.0_spmd, %region_9.0_spmd} | conditional | bytes 6291552 | solution.py:185
  116.4 5.9 %collective-permute-start.35 = (bf16[2,6,2,256,128]{4,3,2,1,0:T(8,128)(2,1)S(1)}, bf16[2,6,2,256,128]{4,3,2,1,0:T(8,128)(2,1)}, u32[]{:S(2)}, u32[]{:S(2)}) collective-permute-start(bf16[2,6,2,256,128]{4,3,2,1,0:T(8,128)(2,1)S(1)} %get-tuple-element.127.refs_2_.refs_0_), channel_id=1, source_target_pairs={{24,0},{26,2},{12,4},{14,6},{0,8},{2,10},{20,12},{22,14},{8,16},{1... | collective-permute-start | bytes 4718600 | tf_op jit(solution)/shard_map/ppermute | solution.py:120
  122.2 11.0 %collective-permute-start.36 = (bf16[2,6,2,256,128]{4,3,2,1,0:T(8,128)(2,1)}, bf16[2,6,2,256,128]{4,3,2,1,0:T(8,128)(2,1)}, u32[]{:S(2)}, u32[]{:S(2)}) collective-permute-start(bf16[2,6,2,256,128]{4,3,2,1,0:T(8,128)(2,1)} %get-tuple-element.141.refs_3_), channel_id=1, source_target_pairs={{4,0},{6,2},{0,4},{2,6},{12,8},{14,10},{8,12},{10,14},{20,16},{22,... | collective-permute-start | bytes 4718600 | tf_op jit(solution)/shard_map/ppermute | solution.py:120
  134.2 18.4 %shard_map.49.refs_2_ = f32[1,9,16,256,512]{4,3,2,1,0:T(8,128)} custom-call(s32[10]{0:T(128)} %pad_add_fusion.table, bf16[6,2,256,128]{3,2,1,0:T(8,128)(2,1)S(1)} %get-tuple-element.109.refs_2_.refs_0_, bf16[6,2,256,128]{3,2,1,0:T(8,128)(2,1)} %get-tuple-element.118.refs_2_.refs_1_, bf16[6,2,256,128]{3,2,1,0:T(8,128)(2,1)} %collective-permute-done.24.refs_5_.refs_2_, ...), custom_call_target="tpu_custom_call" | custom-call | flops 7247757312 | bytes 42467328 | tf_op jit(solution)/shard_map/pallas_call | solution.py:84
  152.6 27.9 %collective-permute-done.29.refs_0_ = bf16[2,4,2,256,128]{4,3,2,1,0:T(8,128)(2,1)} collective-permute-done((bf16[2,4,2,256,128]{4,3,2,1,0:T(8,128)(2,1)S(1)}, bf16[2,4,2,256,128]{4,3,2,1,0:T(8,128)(2,1)}, u32[]{:S(2)}, u32[]{:S(2)}) %collective-permute-start.29) | collective-permute-done | bytes 1048608 | tf_op jit(solution)/shard_map/ppermute | solution.py:120
  180.5 9.9 %collective-permute-done.30.refs_1_ = bf16[2,4,2,256,128]{4,3,2,1,0:T(8,128)(2,1)} collective-permute-done((bf16[2,4,2,256,128]{4,3,2,1,0:T(8,128)(2,1)S(1)}, bf16[2,4,2,256,128]{4,3,2,1,0:T(8,128)(2,1)}, u32[]{:S(2)}, u32[]{:S(2)}) %collective-permute-start.30) | collective-permute-done | bytes 1048608 | tf_op jit(solution)/shard_map/ppermute | solution.py:120
  190.4 6.0 %conditional.13 = (bf16[2,4,2,256,128]{4,3,2,1,0:T(8,128)(2,1)}, bf16[2,4,2,256,128]{4,3,2,1,0:T(8,128)(2,1)}, bf16[2,4,2,256,128]{4,3,2,1,0:T(8,128)(2,1)}) conditional(s32[]{:T(128)} %bitcast.2, () %tuple.74, (bf16[2,4,2,256,128]{4,3,2,1,0:T(8,128)(2,1)S(1)}, bf16[2,4,2,256,128]{4,3,2,1,0:T(8,128)(2,1)}, ...), branch_computations={%region_10.0_spmd, %region_11.0_spmd} | conditional | bytes 12583056 | solution.py:185
  190.9 3.7 %collective-permute-done.13 = bf16[2,4,2,256,128]{4,3,2,1,0:T(8,128)(2,1)} collective-permute-done((bf16[2,4,2,256,128]{4,3,2,1,0:T(8,128)(2,1)S(1)}, bf16[2,4,2,256,128]{4,3,2,1,0:T(8,128)(2,1)}, u32[]{:S(2)}, u32[]{:S(2)}) %collective-permute-start.13) | collective-permute-done | bytes 1048608 | tf_op jit(solution)/shard_map/cond/branch_1_fun/ppermute | solution.py:120
  198.3 6.1 %conditional.15 = (bf16[2,6,2,256,128]{4,3,2,1,0:T(8,128)(2,1)}, bf16[2,6,2,256,128]{4,3,2,1,0:T(8,128)(2,1)}) conditional(s32[]{:T(128)} %bitcast.2, () %tuple.78, (bf16[2,6,2,256,128]{4,3,2,1,0:T(8,128)(2,1)}, bf16[2,6,2,256,128]{4,3,2,1,0:T(8,128)(2,1)}) %shard_map.51), branch_computations={%region_14.0_spmd, %region_15.0_spmd} | conditional | bytes 12583008 | solution.py:185
  198.8 3.2 %collective-permute-done.18 = bf16[2,6,2,256,128]{4,3,2,1,0:T(8,128)(2,1)} collective-permute-done((bf16[2,6,2,256,128]{4,3,2,1,0:T(8,128)(2,1)}, bf16[2,6,2,256,128]{4,3,2,1,0:T(8,128)(2,1)}, u32[]{:S(2)}, u32[]{:S(2)}) %collective-permute-start.18) | collective-permute-done | bytes 1572896 | tf_op jit(solution)/shard_map/cond/branch_1_fun/ppermute | solution.py:120
  204.3 18.1 %shard_map.52.refs_10_ = f32[1,9,16,256,512]{4,3,2,1,0:T(8,128)} custom-call(s32[10]{0:T(128)} %pad_add_fusion.table, bf16[2,6,2,256,128]{4,3,2,1,0:T(8,128)(2,1)S(1)} %get-tuple-element.127.refs_2_.refs_0_, bf16[2,6,2,256,128]{4,3,2,1,0:T(8,128)(2,1)} %get-tuple-element.120.refs_4_.refs_1_, ...), custom_call_target="tpu_custom_call", output_to_operand_aliasing={{}: (11, {})} | custom-call | flops 7247757312 | bytes 42467328 | tf_op jit(solution)/shard_map/pallas_call | solution.py:84
  222.5 2.5 %collective-permute-done.34.refs_4_ = bf16[2,4,2,256,128]{4,3,2,1,0:T(8,128)(2,1)} collective-permute-done((bf16[2,4,2,256,128]{4,3,2,1,0:T(8,128)(2,1)S(1)}, bf16[2,4,2,256,128]{4,3,2,1,0:T(8,128)(2,1)}, u32[]{:S(2)}, u32[]{:S(2)}) %collective-permute-start.34) | collective-permute-done | bytes 1048608 | tf_op jit(solution)/shard_map/ppermute | solution.py:120
  225.0 4.5 %conditional.14 = (bf16[2,4,2,256,128]{4,3,2,1,0:T(8,128)(2,1)}, bf16[2,4,2,256,128]{4,3,2,1,0:T(8,128)(2,1)}) conditional(s32[]{:T(128)} %bitcast.2, () %tuple.76, (bf16[2,4,2,256,128]{4,3,2,1,0:T(8,128)(2,1)}, bf16[2,4,2,256,128]{4,3,2,1,0:T(8,128)(2,1)}) %tuple.77), branch_computations={%region_12.0_spmd, %region_13.0_spmd} | conditional | bytes 8388704 | solution.py:185
  225.5 2.5 %collective-permute-done.16 = bf16[2,4,2,256,128]{4,3,2,1,0:T(8,128)(2,1)} collective-permute-done((bf16[2,4,2,256,128]{4,3,2,1,0:T(8,128)(2,1)}, bf16[2,4,2,256,128]{4,3,2,1,0:T(8,128)(2,1)}, u32[]{:S(2)}, u32[]{:S(2)}) %collective-permute-start.16) | collective-permute-done | bytes 1048608 | tf_op jit(solution)/shard_map/cond/branch_1_fun/ppermute | solution.py:120
  229.5 13.4 %shard_map.53 = f32[1,9,16,256,512]{4,3,2,1,0:T(8,128)} custom-call(s32[10]{0:T(128)} %pad_add_fusion.table, bf16[2,4,2,256,128]{4,3,2,1,0:T(8,128)(2,1)S(1)} %get-tuple-element.137.refs_2_.refs_0_, bf16[2,4,2,256,128]{4,3,2,1,0:T(8,128)(2,1)} %get-tuple-element.133.refs_6_.refs_1_, ...), custom_call_target="tpu_custom_call", output_to_operand_aliasing={{}: (11, {})} | custom-call | flops 4831838208 | bytes 28311552 | tf_op jit(solution)/shard_map/pallas_call | solution.py:84
  (80 shorter events, 47.3 us)
Async XLA Ops:
  2.2 20.7 %collective-permute-start.20 = (bf16[6,2,256,128]{3,2,1,0:T(8,128)(2,1)S(1)}, bf16[6,2,256,128]{3,2,1,0:T(8,128)(2,1)}, u32[]{:S(2)}, u32[]{:S(2)}) collective-permute-start(bf16[6,2,256,128]{3,2,1,0:T(8,128)(2,1)S(1)} %get-tuple-element.148), channel_id=1, source_target_pairs={{0,1},{1,0},{2,3},{3,2},{4,5},{5,4},{6,7},{7,6},{8,9},{9,8},{10,11... | collective-permute-start | bytes 2359304 | tf_op jit(solution)/shard_map/ppermute | solution.py:120
  5.2 28.1 %collective-permute-start.24 = (bf16[6,2,256,128]{3,2,1,0:T(8,128)(2,1)S(1)}, bf16[6,2,256,128]{3,2,1,0:T(8,128)(2,1)}, u32[]{:S(2)}, u32[]{:S(2)}) collective-permute-start(bf16[6,2,256,128]{3,2,1,0:T(8,128)(2,1)S(1)} %get-tuple-element.147.refs_0_), channel_id=1, source_target_pairs={{4,0},{6,2},{0,4},{2,6},{12,8},{14,10},{8,12},{10,14},{20,16},{22,... | collective-permute-start | bytes 2359304 | tf_op jit(solution)/shard_map/ppermute | solution.py:120
  6.8 26.6 %collective-permute-start.23 = (bf16[6,2,256,128]{3,2,1,0:T(8,128)(2,1)S(1)}, bf16[6,2,256,128]{3,2,1,0:T(8,128)(2,1)}, u32[]{:S(2)}, u32[]{:S(2)}) collective-permute-start(bf16[6,2,256,128]{3,2,1,0:T(8,128)(2,1)S(1)} %get-tuple-element.147.refs_0_), channel_id=1, source_target_pairs={{8,0},{10,2},{28,4},{30,6},{16,8},{18,10},{4,12},{6,14},{24,16},{2... | collective-permute-start | bytes 2359304 | tf_op jit(solution)/shard_map/ppermute | solution.py:120
  22.9 22.2 %collective-permute-start.21 = (bf16[6,2,256,128]{3,2,1,0:T(8,128)(2,1)}, bf16[6,2,256,128]{3,2,1,0:T(8,128)(2,1)}, u32[]{:S(2)}, u32[]{:S(2)}) collective-permute-start(bf16[6,2,256,128]{3,2,1,0:T(8,128)(2,1)} %collective-permute-done.20.refs_1_.refs_0_), channel_id=1, source_target_pairs={{8,0},{10,2},{28,4},{30,6},{16,8},{18,10},{4,12},{6,14},{24,16},{2... | collective-permute-start | bytes 2359304 | tf_op jit(solution)/shard_map/ppermute | solution.py:120
  26.7 20.7 %collective-permute-start.22 = (bf16[6,2,256,128]{3,2,1,0:T(8,128)(2,1)}, bf16[6,2,256,128]{3,2,1,0:T(8,128)(2,1)S(1)}, u32[]{:S(2)}, u32[]{:S(2)}) collective-permute-start(bf16[6,2,256,128]{3,2,1,0:T(8,128)(2,1)} %collective-permute-done.20.refs_1_.refs_0_), channel_id=1, source_target_pairs={{4,0},{6,2},{0,4},{2,6},{12,8},{14,10},{8,12},{10,14},{20,16},{22,... | collective-permute-start | bytes 2359304 | tf_op jit(solution)/shard_map/ppermute | solution.py:120
  29.5 22.8 %all-to-all-start = ((bf16[2,6,2,256,128]{4,3,2,1,0:T(8,128)(2,1)}), bf16[2,6,2,256,128]{4,3,2,1,0:T(8,128)(2,1)S(1)}, u32[]{:S(2)}, u32[]{:S(2)}) async-start(bf16[2,6,2,256,128]{4,3,2,1,0:T(8,128)(2,1)} %shard_map.37), calls=%async_computation | async-start | bytes 3145728 | tf_op jit(solution)/shard_map/all_to_all | solution.py:220
  34.0 4.4 %collective-permute-start.2 = (bf16[6,2,256,128]{3,2,1,0:T(8,128)(2,1)}, bf16[6,2,256,128]{3,2,1,0:T(8,128)(2,1)}, u32[]{:S(2)}, u32[]{:S(2)}) collective-permute-start(bf16[6,2,256,128]{3,2,1,0:T(8,128)(2,1)} %get-tuple-element.47), channel_id=1, source_target_pairs={{2,0},{0,2},{6,4},{4,6},{10,8},{8,10},{14,12},{12,14},{18,16},{16,... | collective-permute-start | bytes 2359304 | tf_op jit(solution)/shard_map/cond/branch_1_fun/ppermute | solution.py:120
  38.3 24.6 %collective-permute-start.27 = (bf16[6,2,256,128]{3,2,1,0:T(8,128)(2,1)S(1)}, bf16[6,2,256,128]{3,2,1,0:T(8,128)(2,1)}, u32[]{:S(2)}, u32[]{:S(2)}) collective-permute-start(bf16[6,2,256,128]{3,2,1,0:T(8,128)(2,1)S(1)} %get-tuple-element.109.refs_2_.refs_0_), channel_id=1, source_target_pairs={{24,0},{26,2},{12,4},{14,6},{0,8},{2,10},{20,12},{22,14},{8,16},{1... | collective-permute-start | bytes 2359304 | tf_op jit(solution)/shard_map/ppermute | solution.py:120
  39.4 25.0 %collective-permute-start.28 = (bf16[6,2,256,128]{3,2,1,0:T(8,128)(2,1)}, bf16[6,2,256,128]{3,2,1,0:T(8,128)(2,1)}, u32[]{:S(2)}, u32[]{:S(2)}) collective-permute-start(bf16[6,2,256,128]{3,2,1,0:T(8,128)(2,1)} %get-tuple-element.115.refs_6_), channel_id=1, source_target_pairs={{4,0},{6,2},{0,4},{2,6},{12,8},{14,10},{8,12},{10,14},{20,16},{22,... | collective-permute-start | bytes 2359304 | tf_op jit(solution)/shard_map/ppermute | solution.py:120
  47.4 4.9 %collective-permute-start.4 = (bf16[6,2,256,128]{3,2,1,0:T(8,128)(2,1)}, bf16[6,2,256,128]{3,2,1,0:T(8,128)(2,1)}, u32[]{:S(2)}, u32[]{:S(2)}) collective-permute-start(bf16[6,2,256,128]{3,2,1,0:T(8,128)(2,1)} %get-tuple-element.49), channel_id=1, source_target_pairs={{2,0},{0,2},{6,4},{4,6},{10,8},{8,10},{14,12},{12,14},{18,16},{16,... | collective-permute-start | bytes 2359304 | tf_op jit(solution)/shard_map/cond/branch_1_fun/ppermute | solution.py:120
  47.9 4.4 %collective-permute-start.5 = (bf16[6,2,256,128]{3,2,1,0:T(8,128)(2,1)S(1)}, bf16[6,2,256,128]{3,2,1,0:T(8,128)(2,1)}, u32[]{:S(2)}, u32[]{:S(2)}) collective-permute-start(bf16[6,2,256,128]{3,2,1,0:T(8,128)(2,1)S(1)} %get-tuple-element.50), channel_id=1, source_target_pairs={{2,0},{0,2},{6,4},{4,6},{10,8},{8,10},{14,12},{12,14},{18,16},{16,... | collective-permute-start | bytes 2359304 | tf_op jit(solution)/shard_map/cond/branch_1_fun/ppermute | solution.py:120
  52.3 44.3 %collective-permute-start.25 = (bf16[2,6,2,256,128]{4,3,2,1,0:T(8,128)(2,1)S(1)}, bf16[2,6,2,256,128]{4,3,2,1,0:T(8,128)(2,1)}, u32[]{:S(2)}, u32[]{:S(2)}) collective-permute-start(bf16[2,6,2,256,128]{4,3,2,1,0:T(8,128)(2,1)S(1)} %shard_map.40.refs_1_.refs_2_.refs_0_), channel_id=1, source_target_pairs={{8,0},{10,2},{28,4},{30,6},{16,8},{18,10},{4,12},{6,14},{24,16},{2... | collective-permute-start | bytes 4718600 | tf_op jit(solution)/shard_map/ppermute | solution.py:120
  54.3 43.8 %collective-permute-start.26 = (bf16[2,6,2,256,128]{4,3,2,1,0:T(8,128)(2,1)S(1)}, bf16[2,6,2,256,128]{4,3,2,1,0:T(8,128)(2,1)}, u32[]{:S(2)}, u32[]{:S(2)}) collective-permute-start(bf16[2,6,2,256,128]{4,3,2,1,0:T(8,128)(2,1)S(1)} %shard_map.40.refs_1_.refs_2_.refs_0_), channel_id=1, source_target_pairs={{4,0},{6,2},{0,4},{2,6},{12,8},{14,10},{8,12},{10,14},{20,16},{22,... | collective-permute-start | bytes 4718600 | tf_op jit(solution)/shard_map/ppermute | solution.py:120
  64.4 3.7 %collective-permute-start.7 = (bf16[6,2,256,128]{3,2,1,0:T(8,128)(2,1)}, bf16[6,2,256,128]{3,2,1,0:T(8,128)(2,1)}, u32[]{:S(2)}, u32[]{:S(2)}) collective-permute-start(bf16[6,2,256,128]{3,2,1,0:T(8,128)(2,1)} %get-tuple-element.52), channel_id=1, source_target_pairs={{2,0},{0,2},{6,4},{4,6},{10,8},{8,10},{14,12},{12,14},{18,16},{16,... | collective-permute-start | bytes 2359304 | tf_op jit(solution)/shard_map/cond/branch_1_fun/ppermute | solution.py:120
  68.1 43.8 %collective-permute-start.31 = (bf16[6,2,256,128]{3,2,1,0:T(8,128)(2,1)}, bf16[6,2,256,128]{3,2,1,0:T(8,128)(2,1)}, u32[]{:S(2)}, u32[]{:S(2)}) collective-permute-start(bf16[6,2,256,128]{3,2,1,0:T(8,128)(2,1)} %get-tuple-element.118.refs_2_.refs_1_), channel_id=1, source_target_pairs={{24,0},{26,2},{12,4},{14,6},{0,8},{2,10},{20,12},{22,14},{8,16},{1... | collective-permute-start | bytes 2359304 | tf_op jit(solution)/shard_map/ppermute | solution.py:120
  71.0 41.6 %collective-permute-start.32 = (bf16[6,2,256,128]{3,2,1,0:T(8,128)(2,1)}, bf16[6,2,256,128]{3,2,1,0:T(8,128)(2,1)}, u32[]{:S(2)}, u32[]{:S(2)}) collective-permute-start(bf16[6,2,256,128]{3,2,1,0:T(8,128)(2,1)} %get-tuple-element.124.refs_7_), channel_id=1, source_target_pairs={{4,0},{6,2},{0,4},{2,6},{12,8},{14,10},{8,12},{10,14},{20,16},{22,... | collective-permute-start | bytes 2359304 | tf_op jit(solution)/shard_map/ppermute | solution.py:120
  74.0 32.3 %all-to-all-start.1 = ((bf16[2,4,2,256,128]{4,3,2,1,0:T(8,128)(2,1)}), bf16[2,4,2,256,128]{4,3,2,1,0:T(8,128)(2,1)S(1)}, u32[]{:S(2)}, u32[]{:S(2)}) async-start(bf16[2,4,2,256,128]{4,3,2,1,0:T(8,128)(2,1)} %shard_map.41), calls=%async_computation.1 | async-start | bytes 2097152 | tf_op jit(solution)/shard_map/all_to_all | solution.py:220
  98.1 6.0 %collective-permute-start.10 = (bf16[2,6,2,256,128]{4,3,2,1,0:T(8,128)(2,1)}, bf16[2,6,2,256,128]{4,3,2,1,0:T(8,128)(2,1)}, u32[]{:S(2)}, u32[]{:S(2)}) collective-permute-start(bf16[2,6,2,256,128]{4,3,2,1,0:T(8,128)(2,1)} %get-tuple-element.55), channel_id=1, source_target_pairs={{2,0},{0,2},{6,4},{4,6},{10,8},{8,10},{14,12},{12,14},{18,16},{16,... | collective-permute-start | bytes 4718600 | tf_op jit(solution)/shard_map/cond/branch_1_fun/ppermute | solution.py:120
  98.1 7.7 %collective-permute-start.8 = (bf16[2,6,2,256,128]{4,3,2,1,0:T(8,128)(2,1)S(1)}, bf16[2,6,2,256,128]{4,3,2,1,0:T(8,128)(2,1)}, u32[]{:S(2)}, u32[]{:S(2)}) collective-permute-start(bf16[2,6,2,256,128]{4,3,2,1,0:T(8,128)(2,1)S(1)} %get-tuple-element.53), channel_id=1, source_target_pairs={{2,0},{0,2},{6,4},{4,6},{10,8},{8,10},{14,12},{12,14},{18,16},{16,... | collective-permute-start | bytes 4718600 | tf_op jit(solution)/shard_map/cond/branch_1_fun/ppermute | solution.py:120
  98.6 7.7 %collective-permute-start.9 = (bf16[2,6,2,256,128]{4,3,2,1,0:T(8,128)(2,1)}, bf16[2,6,2,256,128]{4,3,2,1,0:T(8,128)(2,1)}, u32[]{:S(2)}, u32[]{:S(2)}) collective-permute-start(bf16[2,6,2,256,128]{4,3,2,1,0:T(8,128)(2,1)} %get-tuple-element.54), channel_id=1, source_target_pairs={{2,0},{0,2},{6,4},{4,6},{10,8},{8,10},{14,12},{12,14},{18,16},{16,... | collective-permute-start | bytes 4718600 | tf_op jit(solution)/shard_map/cond/branch_1_fun/ppermute | solution.py:120
  116.4 81.9 %collective-permute-start.35 = (bf16[2,6,2,256,128]{4,3,2,1,0:T(8,128)(2,1)S(1)}, bf16[2,6,2,256,128]{4,3,2,1,0:T(8,128)(2,1)}, u32[]{:S(2)}, u32[]{:S(2)}) collective-permute-start(bf16[2,6,2,256,128]{4,3,2,1,0:T(8,128)(2,1)S(1)} %get-tuple-element.127.refs_2_.refs_0_), channel_id=1, source_target_pairs={{24,0},{26,2},{12,4},{14,6},{0,8},{2,10},{20,12},{22,14},{8,16},{1... | collective-permute-start | bytes 4718600 | tf_op jit(solution)/shard_map/ppermute | solution.py:120
  122.2 76.0 %collective-permute-start.36 = (bf16[2,6,2,256,128]{4,3,2,1,0:T(8,128)(2,1)}, bf16[2,6,2,256,128]{4,3,2,1,0:T(8,128)(2,1)}, u32[]{:S(2)}, u32[]{:S(2)}) collective-permute-start(bf16[2,6,2,256,128]{4,3,2,1,0:T(8,128)(2,1)} %get-tuple-element.141.refs_3_), channel_id=1, source_target_pairs={{4,0},{6,2},{0,4},{2,6},{12,8},{14,10},{8,12},{10,14},{20,16},{22,... | collective-permute-start | bytes 4718600 | tf_op jit(solution)/shard_map/ppermute | solution.py:120
  133.2 47.3 %collective-permute-start.29 = (bf16[2,4,2,256,128]{4,3,2,1,0:T(8,128)(2,1)S(1)}, bf16[2,4,2,256,128]{4,3,2,1,0:T(8,128)(2,1)}, u32[]{:S(2)}, u32[]{:S(2)}) collective-permute-start(bf16[2,4,2,256,128]{4,3,2,1,0:T(8,128)(2,1)S(1)} %shard_map.45.refs_2_.refs_0_), channel_id=1, source_target_pairs={{8,0},{10,2},{28,4},{30,6},{16,8},{18,10},{4,12},{6,14},{24,16},{2... | collective-permute-start | bytes 3145736 | tf_op jit(solution)/shard_map/ppermute | solution.py:120
  133.5 56.9 %collective-permute-start.30 = (bf16[2,4,2,256,128]{4,3,2,1,0:T(8,128)(2,1)S(1)}, bf16[2,4,2,256,128]{4,3,2,1,0:T(8,128)(2,1)}, u32[]{:S(2)}, u32[]{:S(2)}) collective-permute-start(bf16[2,4,2,256,128]{4,3,2,1,0:T(8,128)(2,1)S(1)} %shard_map.45.refs_2_.refs_0_), channel_id=1, source_target_pairs={{4,0},{6,2},{0,4},{2,6},{12,8},{14,10},{8,12},{10,14},{20,16},{22,... | collective-permute-start | bytes 3145736 | tf_op jit(solution)/shard_map/ppermute | solution.py:120
  190.4 4.3 %collective-permute-start.13 = (bf16[2,4,2,256,128]{4,3,2,1,0:T(8,128)(2,1)S(1)}, bf16[2,4,2,256,128]{4,3,2,1,0:T(8,128)(2,1)}, u32[]{:S(2)}, u32[]{:S(2)}) collective-permute-start(bf16[2,4,2,256,128]{4,3,2,1,0:T(8,128)(2,1)S(1)} %get-tuple-element.58), channel_id=1, source_target_pairs={{2,0},{0,2},{6,4},{4,6},{10,8},{8,10},{14,12},{12,14},{18,16},{16,... | collective-permute-start | bytes 3145736 | tf_op jit(solution)/shard_map/cond/branch_1_fun/ppermute | solution.py:120
  190.4 4.5 %collective-permute-start.14 = (bf16[2,4,2,256,128]{4,3,2,1,0:T(8,128)(2,1)}, bf16[2,4,2,256,128]{4,3,2,1,0:T(8,128)(2,1)}, u32[]{:S(2)}, u32[]{:S(2)}) collective-permute-start(bf16[2,4,2,256,128]{4,3,2,1,0:T(8,128)(2,1)} %get-tuple-element.59), channel_id=1, source_target_pairs={{2,0},{0,2},{6,4},{4,6},{10,8},{8,10},{14,12},{12,14},{18,16},{16,... | collective-permute-start | bytes 3145736 | tf_op jit(solution)/shard_map/cond/branch_1_fun/ppermute | solution.py:120
  190.9 5.5 %collective-permute-start.15 = (bf16[2,4,2,256,128]{4,3,2,1,0:T(8,128)(2,1)}, bf16[2,4,2,256,128]{4,3,2,1,0:T(8,128)(2,1)}, u32[]{:S(2)}, u32[]{:S(2)}) collective-permute-start(bf16[2,4,2,256,128]{4,3,2,1,0:T(8,128)(2,1)} %get-tuple-element.60), channel_id=1, source_target_pairs={{2,0},{0,2},{6,4},{4,6},{10,8},{8,10},{14,12},{12,14},{18,16},{16,... | collective-permute-start | bytes 3145736 | tf_op jit(solution)/shard_map/cond/branch_1_fun/ppermute | solution.py:120
  196.4 26.1 %collective-permute-start.33 = (bf16[2,4,2,256,128]{4,3,2,1,0:T(8,128)(2,1)}, bf16[2,4,2,256,128]{4,3,2,1,0:T(8,128)(2,1)}, u32[]{:S(2)}, u32[]{:S(2)}) collective-permute-start(bf16[2,4,2,256,128]{4,3,2,1,0:T(8,128)(2,1)} %get-tuple-element.138.refs_3_), channel_id=1, source_target_pairs={{4,0},{6,2},{0,4},{2,6},{12,8},{14,10},{8,12},{10,14},{20,16},{22,... | collective-permute-start | bytes 3145736 | tf_op jit(solution)/shard_map/ppermute | solution.py:120
  198.1 26.8 %collective-permute-start.34 = (bf16[2,4,2,256,128]{4,3,2,1,0:T(8,128)(2,1)S(1)}, bf16[2,4,2,256,128]{4,3,2,1,0:T(8,128)(2,1)}, u32[]{:S(2)}, u32[]{:S(2)}) collective-permute-start(bf16[2,4,2,256,128]{4,3,2,1,0:T(8,128)(2,1)S(1)} %get-tuple-element.137.refs_2_.refs_0_), channel_id=1, source_target_pairs={{24,0},{26,2},{12,4},{14,6},{0,8},{2,10},{20,12},{22,14},{8,16},{1... | collective-permute-start | bytes 3145736 | tf_op jit(solution)/shard_map/ppermute | solution.py:120
  198.3 3.8 %collective-permute-start.18 = (bf16[2,6,2,256,128]{4,3,2,1,0:T(8,128)(2,1)}, bf16[2,6,2,256,128]{4,3,2,1,0:T(8,128)(2,1)}, u32[]{:S(2)}, u32[]{:S(2)}) collective-permute-start(bf16[2,6,2,256,128]{4,3,2,1,0:T(8,128)(2,1)} %get-tuple-element.63), channel_id=1, source_target_pairs={{2,0},{0,2},{6,4},{4,6},{10,8},{8,10},{14,12},{12,14},{18,16},{16,... | collective-permute-start | bytes 4718600 | tf_op jit(solution)/shard_map/cond/branch_1_fun/ppermute | solution.py:120
  198.3 6.0 %collective-permute-start.19 = (bf16[2,6,2,256,128]{4,3,2,1,0:T(8,128)(2,1)}, bf16[2,6,2,256,128]{4,3,2,1,0:T(8,128)(2,1)}, u32[]{:S(2)}, u32[]{:S(2)}) collective-permute-start(bf16[2,6,2,256,128]{4,3,2,1,0:T(8,128)(2,1)} %get-tuple-element.64), channel_id=1, source_target_pairs={{2,0},{0,2},{6,4},{4,6},{10,8},{8,10},{14,12},{12,14},{18,16},{16,... | collective-permute-start | bytes 4718600 | tf_op jit(solution)/shard_map/cond/branch_1_fun/ppermute | solution.py:120
  225.0 4.5 %collective-permute-start.17 = (bf16[2,4,2,256,128]{4,3,2,1,0:T(8,128)(2,1)}, bf16[2,4,2,256,128]{4,3,2,1,0:T(8,128)(2,1)}, u32[]{:S(2)}, u32[]{:S(2)}) collective-permute-start(bf16[2,4,2,256,128]{4,3,2,1,0:T(8,128)(2,1)} %get-tuple-element.62), channel_id=1, source_target_pairs={{2,0},{0,2},{6,4},{4,6},{10,8},{8,10},{14,12},{12,14},{18,16},{16,... | collective-permute-start | bytes 3145736 | tf_op jit(solution)/shard_map/cond/branch_1_fun/ppermute | solution.py:120
  (9 other events, 45.7 us)

commit v3 on v2

--- a/solution.py
+++ b/solution.py
@@ -6,6 +6,9 @@
 from jax.experimental import pallas as pl
 from jax.experimental.pallas import tpu as pltpu
 from jax.sharding import PartitionSpec as P
+
+
+HALVED, JOINED, STAGGER = (4, 4), (4, 4), True
 
 
 def pair_kernel(variants, parts, blocks, joined, table, *refs):
@@ -97,8 +100,8 @@
         input_output_aliases={} if previous is None else {len(operands): 0},
         compiler_params=pltpu.CompilerParams(dimension_semantics=("arbitrary",)),
         cost_estimate=pl.CostEstimate(
-            flops=8 * count * width * size * size * parts * samples,
-            bytes_accessed=count * width * size * (8 * size + 4 * parts * samples),
+            flops=4 * count * width * size * size * parts * samples,
+            bytes_accessed=count * width * size * (4 * size + 2 * parts * samples),
             transcendentals=0,
         ),
     )(table, *operands)
@@ -123,6 +126,8 @@
 class Piece:
     def __init__(self, own, moves):
         self.own = own
+        self.own_twin = None
+        self.read_by, self.theirs_read_by = [], []
         self.forward, self.straight, self.across, self.twin = moves
 
     def near(self):
@@ -130,9 +135,11 @@
         self.partner = self.across(self.own)
 
     def near_twins(self):
-        twins = self.twin([self.own, self.theirs, self.partner])
-        self.own_twin, self.theirs_twin, self.partner_twin = twins
-        return twins
+        if self.own_twin is None:
+            self.own_twin, self.theirs_twin, self.partner_twin = self.twin([self.own, self.theirs, self.partner])
+        else:
+            self.theirs_twin, self.partner_twin = self.twin([self.theirs, self.partner])
+        return [self.own_twin, self.theirs_twin, self.partner_twin]
 
     def far(self):
         self.others = self.straight(self.own)
@@ -158,7 +165,7 @@
         ]
 
 
-def split_exchange(voltages, weights, table, chunks):
+def split_exchange(voltages, weights, table, halved, joined, stagger):
     devices = lax.axis_size("grp")
     plane = devices // 4
     channels = voltages.shape[0] // 2
@@ -207,78 +214,101 @@
     table = jnp.concatenate([position[None].astype(jnp.int32), table])
 
     columns = voltages.reshape(2, channels, *voltages.shape[1:])
-    firsts = [sum(chunks[:at]) for at in range(len(chunks))]
-    stay, go = [
-        lax.dynamic_slice_in_dim(voltages, of * channels, chunks[0], axis=0) * weights
-        for of in (column, 1 - column)
-    ]
-    pieces = [Piece(stay, moves), Piece(turn(go), moves)]
-
-    def turned(at, token):
-        mine = columns[:, firsts[at] : firsts[at] + chunks[at]] * weights
-        (mine,) = after([mine], [token])
-        return Piece(lax.all_to_all(mine, "chan", split_axis=0, concat_axis=0), moves)
-
-    pieces.append(turned(1, pieces[1].own))
-
-    count = len(chunks) + 1
-    steps = [("near", 0), ("near", 1)]
-    for at in range(count - 2):
-        steps += [("far", at), ("near", at + 2)]
-    steps += [("far", count - 2), ("far", count - 1)]
-
-    def kernel(at, result):
-        if at == 0:
-            blocks = list(zip(pieces[0].blocks(), pieces[1].blocks()))
-        else:
-            blocks = pieces[at + 1].blocks()
-        return correlate(blocks, variants, table, firsts[at], channels, result)
-
-    result, ready, shared = None, [], []
+    sizes = halved + joined
+    firsts = [sum(sizes[:at]) for at in range(len(sizes))]
+
+    stays, mines = [], []
+    for chunk, (first, size) in enumerate(zip(firsts, sizes)):
+        if chunk < len(halved):
+            stay, mine = [
+                lax.dynamic_slice_in_dim(voltages, of * channels + first, size, axis=0) * weights
+                for of in (column, 1 - column)
+            ]
+            stays.append(Piece(stay, moves))
+        else:
+            mine = columns[:, first : first + size] * weights
+        mines.append(mine)
+    turns = [Piece(None, moves) for _ in sizes]
+
+    def corner_turn(chunk):
+        mine = mines[chunk]
+        if chunk:
+            earlier, step = turns[chunk - 1], steps[chunk - 1][1]
+            (mine,) = after([mine], [earlier.own, step.theirs])
+            earlier.read_by.append(mine)
+            step.theirs_read_by.append(mine)
+        if chunk < len(halved):
+            turns[chunk].own = turn(mine)
+        else:
+            turns[chunk].own = lax.all_to_all(mine, "chan", split_axis=0, concat_axis=0)
+
+    chunked = [[stays[at], turns[at]] if at < len(halved) else [turns[at]] for at in range(len(sizes))]
+    steps = [("near", piece) for piece in stays + turns]
+    steps += [("far", piece) for pieces in chunked for piece in pieces]
+
+    result, made, shared = None, None, []
+    work = list(range(len(sizes)))
 
     def share(step, token):
         nonlocal result
-        kind, at = steps[step]
-        piece = pieces[at]
+        kind, piece = steps[step]
         if kind == "near":
             if token is not None:
-                piece.theirs, piece.partner = after([piece.theirs, piece.partner], [token])
+                piece.theirs, piece.partner = after([piece.theirs, piece.partner], [token] + piece.theirs_read_by)
             shared.append(piece.near_twins())
-        else:
-            if token is not None:
-                piece.others, piece.passed = after([piece.others, piece.passed], [token])
-            shared.append(piece.far_twins())
-            if at >= 1:
-                result = kernel(at - 1, result)
-                ready.append(step + 3)
-
+            return
+        kept, waits = [piece.others, piece.passed], [] if token is None else [token]
+        if step >= len(steps) - 2 and result is not None:
+            kept.append(result)
+        kept = after(kept, waits) if waits or len(kept) == 3 else kept
+        piece.others, piece.passed = kept[:2]
+        result = kept[2] if len(kept) == 3 else result
+        shared.append(piece.far_twins())
+
+    def compute(step):
+        nonlocal result, made
+        kind, piece = steps[step]
+        if kind == "near" or piece is not chunked[work[0]][-1]:
+            return
+        chunk = work.pop(0)
+        blocks = [piece.blocks() for piece in chunked[chunk]]
+        blocks = list(zip(*blocks)) if len(blocks) > 1 else blocks[0]
+        result = correlate(blocks, variants, table, firsts[chunk], channels, result)
+        made = step
+
+    corner_turn(0)
+    first, second = steps[0][1], steps[1][1]
+    if stagger:
+        first.own_twin = twin([first.own])[0]
+        second.own = after([second.own], [first.own_twin] + second.read_by)[0]
     token = None
-    for step, (kind, at) in enumerate(steps):
-        piece = pieces[at]
+    for step, (kind, piece) in enumerate(steps):
         if step >= 2:
             share(step - 2, token)
-            kept, waits = [piece.own], list(shared[step - 2])
+            kept, waits = [piece.own], shared[step - 2] + piece.read_by
             if kind == "far":
                 kept.append(piece.theirs)
-                waits += [piece.partner, piece.own_twin, piece.theirs_twin]
-                if ready and ready[0] <= step:
-                    ready.pop(0)
+                waits = waits + [piece.partner, piece.own_twin, piece.theirs_twin]
+                if made is not None and made + 4 <= step:
+                    made = None
                     kept.append(result)
             kept = after(kept, waits)
-            piece.own = kept[0]
+            token = piece.own = kept[0]
             if kind == "far":
                 piece.theirs = kept[1]
                 if len(kept) == 3:
                     result = kept[2]
-            token = piece.own
         if kind == "near":
             piece.near()
-            if 2 <= at < count - 1:
-                pieces.append(turned(at, piece.own))
+            if step + 1 < len(sizes):
+                corner_turn(step + 1)
         else:
             piece.far()
-    share(len(steps) - 2, token)
-    share(len(steps) - 1, None)
+        if step >= 2:
+            compute(step - 2)
+    for step in range(len(steps) - 2, len(steps)):
+        share(step, token if step < len(steps) - 1 else None)
+        compute(step)
     return result
 
 
@@ -301,7 +331,7 @@
 def on_device(voltages, input_flags, pair_order):
     weights = input_flags.astype(jnp.bfloat16)[None, None, :, None]
     if lax.axis_size("grp") == 16 and lax.axis_size("chan") == 2:
-        return split_exchange(voltages, weights, pair_order, (6, 6, 4))
+        return split_exchange(voltages, weights, pair_order, HALVED, JOINED, STAGGER)
     return window_exchange(voltages, weights, pair_order)
 
 

time: 244 us -> 227 us (0.930)
  waiting for transfers between devices: 134 us -> 114 us
  Pallas kernels: 50 us -> 53.9 us
    ppermute x37 -> x56, waiting for transfers between devices: 134 us -> 108 us  [permute(): return lambda block: lax.ppermute(block, axis, route)]
    all_to_all x2, waiting for transfers between devices: 0.01 us -> 5.62 us  [corner_turn(): turns[chunk].own = lax.all_to_all(mine, 'chan', split_axis=0, concat_axis=0)]
    pallas_call x3 -> x4, Pallas kernels: 50 us -> 53.9 us  [correlate(): pl.pallas_call(functools.partial(pair_kernel, variants, parts, len(source...]
    mul x3 -> x2, other arithmetic: 6.63 us -> 5.9 us  [the longest x1 3.07 us: split_exchange(): mine = columns[:, first:first + size] * weights]
    ppermute x37 -> x56, starting transfers between devices: 43.3 us -> 43 us  [permute(): return lambda block: lax.ppermute(block, axis, route)]
  transfers between devices with their start and end apart: 39 -> 58, of which waited for: 31 -> 40; matrix products, arithmetic and copies ran while one was open for 2% -> 2% of each run, Pallas kernels for 15% -> 18%
where the time goes in v3:
time: 227 us; the launch traced here: 226 us
  waiting for transfers between devices  114 us (50%)
  Pallas kernels  53.9 us (24%)
  starting transfers between devices  50.1 us (22%)
  other arithmetic  7.21 us (3%)
    ppermute x56, waiting for transfers between devices, permute(): return lambda block: lax.ppermute(block, axis, route)  108 us
    pallas_call x4, Pallas kernels, correlate(): pl.pallas_call(functools.partial(pair_kernel, variants, parts, len(source...  53.9 us
    ppermute x56, starting transfers between devices, permute(): return lambda block: lax.ppermute(block, axis, route)  43 us
    all_to_all x2, starting transfers between devices, corner_turn(): turns[chunk].own = lax.all_to_all(mine, 'chan', split_axis=0, concat_axis=0)  7.16 us
    all_to_all x2, waiting for transfers between devices, corner_turn(): turns[chunk].own = lax.all_to_all(mine, 'chan', split_axis=0, concat_axis=0)  5.62 us
  transfers between devices with their start and end apart: 58, of which 40 were waited for; matrix products, arithmetic and copies ran while one was open for 2% of the time, Pallas kernels for 18%

profile of v3, /device:TPU:0, one launch (start us, length us, event | category | flops | bytes accessed | tf_op | source)
XLA Modules:
  0.0 226.3 jit_solution(4644245805866885402)
XLA Ops:
  0.7 2.8 %dynamic-slice_multiply_fusion = (bf16[4,2,256,128]{3,2,1,0:T(8,128)(2,1)}, bf16[4,2,256,128]{3,2,1,0:T(8,128)(2,1)S(1)}, bf16[4,2,256,128]{3,2,1,0:T(8,128)(2,1)}, bf16[4,2,256,128]{3,2,1,0:T(8,128)(2,1)}) fusion(bf16[32,2,256,128]{3,2,1,0:T(8,128)(2,1)} %param.29, s32[]{:T(128)S(6)} %select_n.15, bf16[256]{0:T(256)(128)(2,1)S(1)} %convert_element_type.7, ...), kind=kLoop, calls=%fused_computation.2 | loop fusion | flops 1048576 | bytes 4194832 | tf_op jit(solution)/shard_map/mul | solution.py:224
  3.5 5.0 %collective-permute-start.31 = (bf16[4,2,256,128]{3,2,1,0:T(8,128)(2,1)}, bf16[4,2,256,128]{3,2,1,0:T(8,128)(2,1)}, u32[]{:S(2)}, u32[]{:S(2)}) collective-permute-start(bf16[4,2,256,128]{3,2,1,0:T(8,128)(2,1)} %get-tuple-element.231.refs_0_), channel_id=1, source_target_pairs={{8,0},{10,2},{28,4},{30,6},{16,8},{18,10},{4,12},{6,14},{24,16},{2... | collective-permute-start | bytes 1572872 | tf_op jit(solution)/shard_map/ppermute | solution.py:123
  14.8 6.4 %collective-permute-done.31.refs_2_.refs_1_ = bf16[4,2,256,128]{3,2,1,0:T(8,128)(2,1)} collective-permute-done((bf16[4,2,256,128]{3,2,1,0:T(8,128)(2,1)}, bf16[4,2,256,128]{3,2,1,0:T(8,128)(2,1)}, u32[]{:S(2)}, u32[]{:S(2)}) %collective-permute-start.31) | collective-permute-done | bytes 524320 | tf_op jit(solution)/shard_map/ppermute | solution.py:123
  24.9 3.1 %slice_multiply_fusion = (bf16[2,4,2,256,128]{4,3,2,1,0:T(8,128)(2,1)}, bf16[2,4,2,256,128]{4,3,2,1,0:T(8,128)(2,1)}) fusion(bf16[2,16,2,256,128]{4,3,2,1,0:T(8,128)(2,1)} %bitcast.4, bf16[256]{0:T(256)(128)(2,1)S(1)} %convert_element_type.7), kind=kLoop, calls=%fused_computation | loop fusion | flops 1048576 | bytes 4194816 | tf_op jit(solution)/shard_map/mul | solution.py:229
  28.0 3.0 %conditional.14 = (bf16[4,2,256,128]{3,2,1,0:T(8,128)(2,1)}, bf16[4,2,256,128]{3,2,1,0:T(8,128)(2,1)}) conditional(s32[]{:T(128)} %bitcast.2, () %tuple.104, (bf16[4,2,256,128]{3,2,1,0:T(8,128)(2,1)}, bf16[4,2,256,128]{3,2,1,0:T(8,128)(2,1)}) %tuple.105), branch_computations={%region_2.0_spmd, %region_3.0_spmd} | conditional | bytes 4194400 | solution.py:192
  34.8 3.6 %all-to-all-start = ((bf16[2,4,2,256,128]{4,3,2,1,0:T(8,128)(2,1)}), bf16[2,4,2,256,128]{4,3,2,1,0:T(8,128)(2,1)S(1)}, u32[]{:S(2)}, u32[]{:S(2)}) async-start(bf16[2,4,2,256,128]{4,3,2,1,0:T(8,128)(2,1)} %shard_map.39.refs_3_.refs_4_), calls=%async_computation | async-start | bytes 2097152 | tf_op jit(solution)/shard_map/all_to_all | solution.py:243
  39.1 3.8 %conditional.15 = (bf16[4,2,256,128]{3,2,1,0:T(8,128)(2,1)}, bf16[4,2,256,128]{3,2,1,0:T(8,128)(2,1)}, bf16[4,2,256,128]{3,2,1,0:T(8,128)(2,1)}) conditional(s32[]{:T(128)} %bitcast.2, () %tuple.107, (bf16[4,2,256,128]{3,2,1,0:T(8,128)(2,1)}, bf16[4,2,256,128]{3,2,1,0:T(8,128)(2,1)}, bf16[4,2,256,128]{3,2,1,0:T(8,128)(2,1)}) %tuple.108), branch_computations={%region_4.0_spmd, %region_5.0_spmd} | conditional | bytes 6291600 | solution.py:192
  45.0 5.6 %all-to-all-done.refs_1_.refs_0_ = bf16[2,4,2,256,128]{4,3,2,1,0:T(8,128)(2,1)S(1)} async-done(((bf16[2,4,2,256,128]{4,3,2,1,0:T(8,128)(2,1)}), bf16[2,4,2,256,128]{4,3,2,1,0:T(8,128)(2,1)S(1)}, u32[]{:S(2)}, u32[]{:S(2)}) %all-to-all-start) | async-done | bytes 1048608 | tf_op jit(solution)/shard_map/all_to_all | solution.py:243
  50.6 3.6 %all-to-all-start.1 = ((bf16[2,4,2,256,128]{4,3,2,1,0:T(8,128)(2,1)}), bf16[2,4,2,256,128]{4,3,2,1,0:T(8,128)(2,1)S(1)}, u32[]{:S(2)}, u32[]{:S(2)}) async-start(bf16[2,4,2,256,128]{4,3,2,1,0:T(8,128)(2,1)} %shard_map.41.refs_3_.refs_4_), calls=%async_computation.1 | async-start | bytes 2097152 | tf_op jit(solution)/shard_map/all_to_all | solution.py:243
  54.2 3.8 %conditional.16 = (bf16[4,2,256,128]{3,2,1,0:T(8,128)(2,1)}, bf16[4,2,256,128]{3,2,1,0:T(8,128)(2,1)}, bf16[4,2,256,128]{3,2,1,0:T(8,128)(2,1)}) conditional(s32[]{:T(128)} %bitcast.2, () %tuple.109, (bf16[4,2,256,128]{3,2,1,0:T(8,128)(2,1)S(1)}, bf16[4,2,256,128]{3,2,1,0:T(8,128)(2,1)}, bf16[4,2,256,128]{3,2,1,0:T(8,128)(2,1)}) %tuple.110), branch_computations={%region_6.0_spmd, %region_7.0_spmd} | conditional | bytes 6291600 | solution.py:192
  61.8 3.8 %conditional.17 = (bf16[4,2,256,128]{3,2,1,0:T(8,128)(2,1)}, bf16[4,2,256,128]{3,2,1,0:T(8,128)(2,1)}, bf16[4,2,256,128]{3,2,1,0:T(8,128)(2,1)}) conditional(s32[]{:T(128)} %bitcast.2, () %tuple.106, (bf16[4,2,256,128]{3,2,1,0:T(8,128)(2,1)S(1)}, bf16[4,2,256,128]{3,2,1,0:T(8,128)(2,1)}, bf16[4,2,256,128]{3,2,1,0:T(8,128)(2,1)}) %tuple.111), branch_computations={%region_8.0_spmd, %region_9.0_spmd} | conditional | bytes 6291600 | solution.py:192
  65.6 2.5 %collective-permute-start.40 = (bf16[2,4,2,256,128]{4,3,2,1,0:T(8,128)(2,1)S(1)}, bf16[2,4,2,256,128]{4,3,2,1,0:T(8,128)(2,1)}, u32[]{:S(2)}, u32[]{:S(2)}) collective-permute-start(bf16[2,4,2,256,128]{4,3,2,1,0:T(8,128)(2,1)S(1)} %shard_map.47.refs_2_.refs_0_), channel_id=1, source_target_pairs={{8,0},{10,2},{28,4},{30,6},{16,8},{18,10},{4,12},{6,14},{24,16},{2... | collective-permute-start | bytes 3145736 | tf_op jit(solution)/shard_map/ppermute | solution.py:123
  68.1 16.1 %collective-permute-done.42.refs_0_ = bf16[2,4,2,256,128]{4,3,2,1,0:T(8,128)(2,1)} collective-permute-done((bf16[2,4,2,256,128]{4,3,2,1,0:T(8,128)(2,1)S(1)}, bf16[2,4,2,256,128]{4,3,2,1,0:T(8,128)(2,1)}, u32[]{:S(2)}, u32[]{:S(2)}) %collective-permute-start.42) | collective-permute-done | bytes 1048608 | tf_op jit(solution)/shard_map/ppermute | solution.py:123
  85.8 6.0 %conditional.18 = (bf16[2,4,2,256,128]{4,3,2,1,0:T(8,128)(2,1)}, bf16[2,4,2,256,128]{4,3,2,1,0:T(8,128)(2,1)}, bf16[2,4,2,256,128]{4,3,2,1,0:T(8,128)(2,1)}) conditional(s32[]{:T(128)} %bitcast.2, () %tuple.112, (bf16[2,4,2,256,128]{4,3,2,1,0:T(8,128)(2,1)S(1)}, bf16[2,4,2,256,128]{4,3,2,1,0:T(8,128)(2,1)}, ...), branch_computations={%region_10.0_spmd, %region_11.0_spmd} | conditional | bytes 12583056 | solution.py:192
  86.3 3.7 %collective-permute-done.12 = bf16[2,4,2,256,128]{4,3,2,1,0:T(8,128)(2,1)} collective-permute-done((bf16[2,4,2,256,128]{4,3,2,1,0:T(8,128)(2,1)S(1)}, bf16[2,4,2,256,128]{4,3,2,1,0:T(8,128)(2,1)}, u32[]{:S(2)}, u32[]{:S(2)}) %collective-permute-start.12) | collective-permute-done | bytes 1048608 | tf_op jit(solution)/shard_map/cond/branch_1_fun/ppermute | solution.py:123
  93.7 23.4 %collective-permute-done.40.refs_0_ = bf16[2,4,2,256,128]{4,3,2,1,0:T(8,128)(2,1)} collective-permute-done((bf16[2,4,2,256,128]{4,3,2,1,0:T(8,128)(2,1)S(1)}, bf16[2,4,2,256,128]{4,3,2,1,0:T(8,128)(2,1)}, u32[]{:S(2)}, u32[]{:S(2)}) %collective-permute-start.40) | collective-permute-done | bytes 1048608 | tf_op jit(solution)/shard_map/ppermute | solution.py:123
  117.0 6.0 %conditional.19 = (bf16[2,4,2,256,128]{4,3,2,1,0:T(8,128)(2,1)}, bf16[2,4,2,256,128]{4,3,2,1,0:T(8,128)(2,1)}, bf16[2,4,2,256,128]{4,3,2,1,0:T(8,128)(2,1)}) conditional(s32[]{:T(128)} %bitcast.2, () %tuple.114, (bf16[2,4,2,256,128]{4,3,2,1,0:T(8,128)(2,1)S(1)}, bf16[2,4,2,256,128]{4,3,2,1,0:T(8,128)(2,1)}, ...), branch_computations={%region_12.0_spmd, %region_13.0_spmd} | conditional | bytes 12583056 | solution.py:192
  117.6 3.0 %collective-permute-done.15 = bf16[2,4,2,256,128]{4,3,2,1,0:T(8,128)(2,1)} collective-permute-done((bf16[2,4,2,256,128]{4,3,2,1,0:T(8,128)(2,1)S(1)}, bf16[2,4,2,256,128]{4,3,2,1,0:T(8,128)(2,1)}, u32[]{:S(2)}, u32[]{:S(2)}) %collective-permute-start.15) | collective-permute-done | bytes 1048608 | tf_op jit(solution)/shard_map/cond/branch_1_fun/ppermute | solution.py:123
  123.1 3.1 %conditional.20 = (bf16[4,2,256,128]{3,2,1,0:T(8,128)(2,1)}, bf16[4,2,256,128]{3,2,1,0:T(8,128)(2,1)}) conditional(s32[]{:T(128)} %bitcast.2, () %tuple.116, (bf16[4,2,256,128]{3,2,1,0:T(8,128)(2,1)}, bf16[4,2,256,128]{3,2,1,0:T(8,128)(2,1)}) %shard_map.52), branch_computations={%region_14.0_spmd, %region_15.0_spmd} | conditional | bytes 4194400 | solution.py:192
  126.7 5.3 %collective-permute-start.51 = (bf16[4,2,256,128]{3,2,1,0:T(8,128)(2,1)}, bf16[4,2,256,128]{3,2,1,0:T(8,128)(2,1)}, u32[]{:S(2)}, u32[]{:S(2)}) collective-permute-start(bf16[4,2,256,128]{3,2,1,0:T(8,128)(2,1)} %get-tuple-element.204.refs_6_), channel_id=1, source_target_pairs={{4,0},{6,2},{0,4},{2,6},{12,8},{14,10},{8,12},{10,14},{20,16},{22,... | collective-permute-start | bytes 1572872 | tf_op jit(solution)/shard_map/ppermute | solution.py:123
  132.0 7.7 %collective-permute-done.46.refs_0_ = bf16[4,2,256,128]{3,2,1,0:T(8,128)(2,1)} collective-permute-done((bf16[4,2,256,128]{3,2,1,0:T(8,128)(2,1)S(1)}, bf16[4,2,256,128]{3,2,1,0:T(8,128)(2,1)}, u32[]{:S(2)}, u32[]{:S(2)}) %collective-permute-start.46) | collective-permute-done | bytes 524320 | tf_op jit(solution)/shard_map/ppermute | solution.py:123
  139.7 3.0 %conditional.21 = (bf16[4,2,256,128]{3,2,1,0:T(8,128)(2,1)}, bf16[4,2,256,128]{3,2,1,0:T(8,128)(2,1)}) conditional(s32[]{:T(128)} %bitcast.2, () %tuple.117, (bf16[4,2,256,128]{3,2,1,0:T(8,128)(2,1)}, bf16[4,2,256,128]{3,2,1,0:T(8,128)(2,1)}) %shard_map.54), branch_computations={%region_16.0_spmd, %region_17.0_spmd} | conditional | bytes 4194400 | solution.py:192
  145.8 5.1 %collective-permute-done.50.refs_0_ = bf16[4,2,256,128]{3,2,1,0:T(8,128)(2,1)} collective-permute-done((bf16[4,2,256,128]{3,2,1,0:T(8,128)(2,1)}, bf16[4,2,256,128]{3,2,1,0:T(8,128)(2,1)}, u32[]{:S(2)}, u32[]{:S(2)}) %collective-permute-start.50) | collective-permute-done | bytes 524320 | tf_op jit(solution)/shard_map/ppermute | solution.py:123
  150.9 3.0 %conditional.22 = (bf16[4,2,256,128]{3,2,1,0:T(8,128)(2,1)}, bf16[4,2,256,128]{3,2,1,0:T(8,128)(2,1)}) conditional(s32[]{:T(128)} %bitcast.2, () %tuple.119, (bf16[4,2,256,128]{3,2,1,0:T(8,128)(2,1)}, bf16[4,2,256,128]{3,2,1,0:T(8,128)(2,1)}) %shard_map.57), branch_computations={%region_18.0_spmd, %region_19.0_spmd} | conditional | bytes 4194400 | solution.py:192
  156.4 13.5 %shard_map.55.refs_2_ = f32[1,9,16,256,512]{4,3,2,1,0:T(8,128)} custom-call(s32[10]{0:T(128)} %pad_add_fusion.table, bf16[4,2,256,128]{3,2,1,0:T(8,128)(2,1)} %get-tuple-element.184.refs_2_.refs_0_, bf16[4,2,256,128]{3,2,1,0:T(8,128)(2,1)S(1)} %get-tuple-element.190.refs_2_.refs_1_, bf16[4,2,256,128]{3,2,1,0:T(8,128)(2,1)} %collective-permute-done.34.refs_5_.refs_2_, ...), custom_call_target="tpu_custom_call" | custom-call | flops 2415919104 | bytes 14155776 | tf_op jit(solution)/shard_map/pallas_call | solution.py:87
  170.0 3.1 %conditional.23 = (bf16[4,2,256,128]{3,2,1,0:T(8,128)(2,1)}, bf16[4,2,256,128]{3,2,1,0:T(8,128)(2,1)}) conditional(s32[]{:T(128)} %bitcast.2, () %tuple.118, (bf16[4,2,256,128]{3,2,1,0:T(8,128)(2,1)}, bf16[4,2,256,128]{3,2,1,0:T(8,128)(2,1)}) %shard_map.59), branch_computations={%region_20.0_spmd, %region_21.0_spmd} | conditional | bytes 4194400 | solution.py:192
  173.1 3.4 %collective-permute-start.53 = (bf16[2,4,2,256,128]{4,3,2,1,0:T(8,128)(2,1)}, bf16[2,4,2,256,128]{4,3,2,1,0:T(8,128)(2,1)}, u32[]{:S(2)}, u32[]{:S(2)}) collective-permute-start(bf16[2,4,2,256,128]{4,3,2,1,0:T(8,128)(2,1)} %get-tuple-element.211.refs_3_), channel_id=1, source_target_pairs={{4,0},{6,2},{0,4},{2,6},{12,8},{14,10},{8,12},{10,14},{20,16},{22,... | collective-permute-start | bytes 3145736 | tf_op jit(solution)/shard_map/ppermute | solution.py:123
  176.5 13.5 %shard_map.61.refs_2_ = f32[1,9,16,256,512]{4,3,2,1,0:T(8,128)} custom-call(s32[10]{0:T(128)} %pad_add_fusion.table, bf16[4,2,256,128]{3,2,1,0:T(8,128)(2,1)} %get-tuple-element.196.refs_2_.refs_0_, bf16[4,2,256,128]{3,2,1,0:T(8,128)(2,1)S(1)} %get-tuple-element.202.refs_2_.refs_1_, ...), custom_call_target="tpu_custom_call", output_to_operand_aliasing={{}: (21, {})} | custom-call | flops 2415919104 | bytes 14155776 | tf_op jit(solution)/shard_map/pallas_call | solution.py:87
  190.1 4.6 %conditional.24 = (bf16[2,4,2,256,128]{4,3,2,1,0:T(8,128)(2,1)}, bf16[2,4,2,256,128]{4,3,2,1,0:T(8,128)(2,1)}) conditional(s32[]{:T(128)} %bitcast.2, () %tuple.120, (bf16[2,4,2,256,128]{4,3,2,1,0:T(8,128)(2,1)}, bf16[2,4,2,256,128]{4,3,2,1,0:T(8,128)(2,1)}) %tuple.121), branch_computations={%region_22.0_spmd, %region_23.0_spmd} | conditional | bytes 8388704 | solution.py:192
  194.7 13.4 %shard_map.63.refs_2_ = f32[1,9,16,256,512]{4,3,2,1,0:T(8,128)} custom-call(s32[10]{0:T(128)} %pad_add_fusion.table, bf16[2,4,2,256,128]{4,3,2,1,0:T(8,128)(2,1)S(1)} %get-tuple-element.207.refs_2_.refs_0_, bf16[2,4,2,256,128]{4,3,2,1,0:T(8,128)(2,1)} %get-tuple-element.180.refs_5_.refs_1_, ...), custom_call_target="tpu_custom_call", output_to_operand_aliasing={{}: (11, {})} | custom-call | flops 2415919104 | bytes 14155776 | tf_op jit(solution)/shard_map/pallas_call | solution.py:87
  208.1 4.6 %conditional.25 = (bf16[2,4,2,256,128]{4,3,2,1,0:T(8,128)(2,1)}, bf16[2,4,2,256,128]{4,3,2,1,0:T(8,128)(2,1)}) conditional(s32[]{:T(128)} %bitcast.2, () %tuple.122, (bf16[2,4,2,256,128]{4,3,2,1,0:T(8,128)(2,1)}, bf16[2,4,2,256,128]{4,3,2,1,0:T(8,128)(2,1)}) %tuple.123), branch_computations={%region_24.0_spmd, %region_25.0_spmd} | conditional | bytes 8388704 | solution.py:192
  212.7 13.4 %shard_map.65 = f32[1,9,16,256,512]{4,3,2,1,0:T(8,128)} custom-call(s32[10]{0:T(128)} %pad_add_fusion.table, bf16[2,4,2,256,128]{4,3,2,1,0:T(8,128)(2,1)S(1)} %get-tuple-element.210.refs_3_.refs_0_, bf16[2,4,2,256,128]{4,3,2,1,0:T(8,128)(2,1)} %get-tuple-element.186.refs_5_.refs_1_, ...), custom_call_target="tpu_custom_call", output_to_operand_aliasing={{}: (11, {})} | custom-call | flops 2415919104 | bytes 14155776 | tf_op jit(solution)/shard_map/pallas_call | solution.py:87
  (134 shorter events, 73.2 us)
Async XLA Ops:
  3.5 17.7 %collective-permute-start.31 = (bf16[4,2,256,128]{3,2,1,0:T(8,128)(2,1)}, bf16[4,2,256,128]{3,2,1,0:T(8,128)(2,1)}, u32[]{:S(2)}, u32[]{:S(2)}) collective-permute-start(bf16[4,2,256,128]{3,2,1,0:T(8,128)(2,1)} %get-tuple-element.231.refs_0_), channel_id=1, source_target_pairs={{8,0},{10,2},{28,4},{30,6},{16,8},{18,10},{4,12},{6,14},{24,16},{2... | collective-permute-start | bytes 1572872 | tf_op jit(solution)/shard_map/ppermute | solution.py:123
  8.6 13.4 %collective-permute-start.30 = (bf16[4,2,256,128]{3,2,1,0:T(8,128)(2,1)S(1)}, bf16[4,2,256,128]{3,2,1,0:T(8,128)(2,1)S(1)}, u32[]{:S(2)}, u32[]{:S(2)}) collective-permute-start(bf16[4,2,256,128]{3,2,1,0:T(8,128)(2,1)S(1)} %get-tuple-element.229), channel_id=1, source_target_pairs={{0,1},{1,0},{2,3},{3,2},{4,5},{5,4},{6,7},{7,6},{8,9},{9,8},{10,11... | collective-permute-start | bytes 1572872 | tf_op jit(solution)/shard_map/ppermute | solution.py:123
  10.1 17.9 %collective-permute-start.34 = (bf16[4,2,256,128]{3,2,1,0:T(8,128)(2,1)}, bf16[4,2,256,128]{3,2,1,0:T(8,128)(2,1)}, u32[]{:S(2)}, u32[]{:S(2)}) collective-permute-start(bf16[4,2,256,128]{3,2,1,0:T(8,128)(2,1)} %get-tuple-element.231.refs_0_), channel_id=1, source_target_pairs={{4,0},{6,2},{0,4},{2,6},{12,8},{14,10},{8,12},{10,14},{20,16},{22,... | collective-permute-start | bytes 1572872 | tf_op jit(solution)/shard_map/ppermute | solution.py:123
  13.1 20.0 %collective-permute-start.33 = (bf16[4,2,256,128]{3,2,1,0:T(8,128)(2,1)}, bf16[4,2,256,128]{3,2,1,0:T(8,128)(2,1)}, u32[]{:S(2)}, u32[]{:S(2)}) collective-permute-start(bf16[4,2,256,128]{3,2,1,0:T(8,128)(2,1)} %shard_map.38.refs_0_), channel_id=1, source_target_pairs={{8,0},{10,2},{28,4},{30,6},{16,8},{18,10},{4,12},{6,14},{24,16},{2... | collective-permute-start | bytes 1572872 | tf_op jit(solution)/shard_map/ppermute | solution.py:123
  22.0 12.8 %collective-permute-start.32 = (bf16[4,2,256,128]{3,2,1,0:T(8,128)(2,1)}, bf16[4,2,256,128]{3,2,1,0:T(8,128)(2,1)S(1)}, u32[]{:S(2)}, u32[]{:S(2)}) collective-permute-start(bf16[4,2,256,128]{3,2,1,0:T(8,128)(2,1)} %shard_map.37.refs_4_.refs_5_), channel_id=1, source_target_pairs={{0,1},{1,0},{2,3},{3,2},{4,5},{5,4},{6,7},{7,6},{8,9},{9,8},{10,11... | collective-permute-start | bytes 1572872 | tf_op jit(solution)/shard_map/ppermute | solution.py:123
  23.5 15.6 %collective-permute-start.36 = (bf16[4,2,256,128]{3,2,1,0:T(8,128)(2,1)}, bf16[4,2,256,128]{3,2,1,0:T(8,128)(2,1)}, u32[]{:S(2)}, u32[]{:S(2)}) collective-permute-start(bf16[4,2,256,128]{3,2,1,0:T(8,128)(2,1)} %shard_map.38.refs_0_), channel_id=1, source_target_pairs={{4,0},{6,2},{0,4},{2,6},{12,8},{14,10},{8,12},{10,14},{20,16},{22,... | collective-permute-start | bytes 1572872 | tf_op jit(solution)/shard_map/ppermute | solution.py:123
  31.0 14.0 %collective-permute-start.35 = (bf16[4,2,256,128]{3,2,1,0:T(8,128)(2,1)S(1)}, bf16[4,2,256,128]{3,2,1,0:T(8,128)(2,1)S(1)}, u32[]{:S(2)}, u32[]{:S(2)}) collective-permute-start(bf16[4,2,256,128]{3,2,1,0:T(8,128)(2,1)S(1)} %shard_map.40.refs_2_.refs_0_), channel_id=1, source_target_pairs={{8,0},{10,2},{28,4},{30,6},{16,8},{18,10},{4,12},{6,14},{24,16},{2... | collective-permute-start | bytes 1572872 | tf_op jit(solution)/shard_map/ppermute | solution.py:123
  34.8 15.8 %all-to-all-start = ((bf16[2,4,2,256,128]{4,3,2,1,0:T(8,128)(2,1)}), bf16[2,4,2,256,128]{4,3,2,1,0:T(8,128)(2,1)S(1)}, u32[]{:S(2)}, u32[]{:S(2)}) async-start(bf16[2,4,2,256,128]{4,3,2,1,0:T(8,128)(2,1)} %shard_map.39.refs_3_.refs_4_), calls=%async_computation | async-start | bytes 2097152 | tf_op jit(solution)/shard_map/all_to_all | solution.py:243
  38.3 15.8 %collective-permute-start.39 = (bf16[4,2,256,128]{3,2,1,0:T(8,128)(2,1)S(1)}, bf16[4,2,256,128]{3,2,1,0:T(8,128)(2,1)}, u32[]{:S(2)}, u32[]{:S(2)}) collective-permute-start(bf16[4,2,256,128]{3,2,1,0:T(8,128)(2,1)S(1)} %shard_map.40.refs_2_.refs_0_), channel_id=1, source_target_pairs={{4,0},{6,2},{0,4},{2,6},{12,8},{14,10},{8,12},{10,14},{20,16},{22,... | collective-permute-start | bytes 1572872 | tf_op jit(solution)/shard_map/ppermute | solution.py:123
  42.8 16.8 %collective-permute-start.37 = (bf16[4,2,256,128]{3,2,1,0:T(8,128)(2,1)S(1)}, bf16[4,2,256,128]{3,2,1,0:T(8,128)(2,1)}, u32[]{:S(2)}, u32[]{:S(2)}) collective-permute-start(bf16[4,2,256,128]{3,2,1,0:T(8,128)(2,1)S(1)} %shard_map.43.refs_2_.refs_0_), channel_id=1, source_target_pairs={{8,0},{10,2},{28,4},{30,6},{16,8},{18,10},{4,12},{6,14},{24,16},{2... | collective-permute-start | bytes 1572872 | tf_op jit(solution)/shard_map/ppermute | solution.py:123
  44.9 16.9 %collective-permute-start.38 = (bf16[4,2,256,128]{3,2,1,0:T(8,128)(2,1)S(1)}, bf16[4,2,256,128]{3,2,1,0:T(8,128)(2,1)}, u32[]{:S(2)}, u32[]{:S(2)}) collective-permute-start(bf16[4,2,256,128]{3,2,1,0:T(8,128)(2,1)S(1)} %shard_map.43.refs_2_.refs_0_), channel_id=1, source_target_pairs={{4,0},{6,2},{0,4},{2,6},{12,8},{14,10},{8,12},{10,14},{20,16},{22,... | collective-permute-start | bytes 1572872 | tf_op jit(solution)/shard_map/ppermute | solution.py:123
  50.6 15.0 %all-to-all-start.1 = ((bf16[2,4,2,256,128]{4,3,2,1,0:T(8,128)(2,1)}), bf16[2,4,2,256,128]{4,3,2,1,0:T(8,128)(2,1)S(1)}, u32[]{:S(2)}, u32[]{:S(2)}) async-start(bf16[2,4,2,256,128]{4,3,2,1,0:T(8,128)(2,1)} %shard_map.41.refs_3_.refs_4_), calls=%async_computation.1 | async-start | bytes 2097152 | tf_op jit(solution)/shard_map/all_to_all | solution.py:243
  58.0 26.1 %collective-permute-start.42 = (bf16[2,4,2,256,128]{4,3,2,1,0:T(8,128)(2,1)S(1)}, bf16[2,4,2,256,128]{4,3,2,1,0:T(8,128)(2,1)}, u32[]{:S(2)}, u32[]{:S(2)}) collective-permute-start(bf16[2,4,2,256,128]{4,3,2,1,0:T(8,128)(2,1)S(1)} %shard_map.45.refs_2_.refs_0_), channel_id=1, source_target_pairs={{8,0},{10,2},{28,4},{30,6},{16,8},{18,10},{4,12},{6,14},{24,16},{2... | collective-permute-start | bytes 3145736 | tf_op jit(solution)/shard_map/ppermute | solution.py:123
  59.6 26.1 %collective-permute-start.43 = (bf16[2,4,2,256,128]{4,3,2,1,0:T(8,128)(2,1)S(1)}, bf16[2,4,2,256,128]{4,3,2,1,0:T(8,128)(2,1)}, u32[]{:S(2)}, u32[]{:S(2)}) collective-permute-start(bf16[2,4,2,256,128]{4,3,2,1,0:T(8,128)(2,1)S(1)} %shard_map.45.refs_2_.refs_0_), channel_id=1, source_target_pairs={{4,0},{6,2},{0,4},{2,6},{12,8},{14,10},{8,12},{10,14},{20,16},{22,... | collective-permute-start | bytes 3145736 | tf_op jit(solution)/shard_map/ppermute | solution.py:123
  65.6 51.5 %collective-permute-start.40 = (bf16[2,4,2,256,128]{4,3,2,1,0:T(8,128)(2,1)S(1)}, bf16[2,4,2,256,128]{4,3,2,1,0:T(8,128)(2,1)}, u32[]{:S(2)}, u32[]{:S(2)}) collective-permute-start(bf16[2,4,2,256,128]{4,3,2,1,0:T(8,128)(2,1)S(1)} %shard_map.47.refs_2_.refs_0_), channel_id=1, source_target_pairs={{8,0},{10,2},{28,4},{30,6},{16,8},{18,10},{4,12},{6,14},{24,16},{2... | collective-permute-start | bytes 3145736 | tf_op jit(solution)/shard_map/ppermute | solution.py:123
  68.1 49.0 %collective-permute-start.41 = (bf16[2,4,2,256,128]{4,3,2,1,0:T(8,128)(2,1)S(1)}, bf16[2,4,2,256,128]{4,3,2,1,0:T(8,128)(2,1)}, u32[]{:S(2)}, u32[]{:S(2)}) collective-permute-start(bf16[2,4,2,256,128]{4,3,2,1,0:T(8,128)(2,1)S(1)} %shard_map.47.refs_2_.refs_0_), channel_id=1, source_target_pairs={{4,0},{6,2},{0,4},{2,6},{12,8},{14,10},{8,12},{10,14},{20,16},{22,... | collective-permute-start | bytes 3145736 | tf_op jit(solution)/shard_map/ppermute | solution.py:123
  85.8 4.5 %collective-permute-start.13 = (bf16[2,4,2,256,128]{4,3,2,1,0:T(8,128)(2,1)}, bf16[2,4,2,256,128]{4,3,2,1,0:T(8,128)(2,1)}, u32[]{:S(2)}, u32[]{:S(2)}) collective-permute-start(bf16[2,4,2,256,128]{4,3,2,1,0:T(8,128)(2,1)} %get-tuple-element.79), channel_id=1, source_target_pairs={{2,0},{0,2},{6,4},{4,6},{10,8},{8,10},{14,12},{12,14},{18,16},{16,... | collective-permute-start | bytes 3145736 | tf_op jit(solution)/shard_map/cond/branch_1_fun/ppermute | solution.py:123
  86.3 5.5 %collective-permute-start.14 = (bf16[2,4,2,256,128]{4,3,2,1,0:T(8,128)(2,1)}, bf16[2,4,2,256,128]{4,3,2,1,0:T(8,128)(2,1)}, u32[]{:S(2)}, u32[]{:S(2)}) collective-permute-start(bf16[2,4,2,256,128]{4,3,2,1,0:T(8,128)(2,1)} %get-tuple-element.80), channel_id=1, source_target_pairs={{2,0},{0,2},{6,4},{4,6},{10,8},{8,10},{14,12},{12,14},{18,16},{16,... | collective-permute-start | bytes 3145736 | tf_op jit(solution)/shard_map/cond/branch_1_fun/ppermute | solution.py:123
  91.8 31.3 %collective-permute-start.44 = (bf16[4,2,256,128]{3,2,1,0:T(8,128)(2,1)}, bf16[4,2,256,128]{3,2,1,0:T(8,128)(2,1)}, u32[]{:S(2)}, u32[]{:S(2)}) collective-permute-start(bf16[4,2,256,128]{3,2,1,0:T(8,128)(2,1)} %get-tuple-element.184.refs_2_.refs_0_), channel_id=1, source_target_pairs={{24,0},{26,2},{12,4},{14,6},{0,8},{2,10},{20,12},{22,14},{8,16},{1... | collective-permute-start | bytes 1572872 | tf_op jit(solution)/shard_map/ppermute | solution.py:123
  92.2 30.9 %collective-permute-start.45 = (bf16[4,2,256,128]{3,2,1,0:T(8,128)(2,1)}, bf16[4,2,256,128]{3,2,1,0:T(8,128)(2,1)}, u32[]{:S(2)}, u32[]{:S(2)}) collective-permute-start(bf16[4,2,256,128]{3,2,1,0:T(8,128)(2,1)} %get-tuple-element.191.refs_6_), channel_id=1, source_target_pairs={{4,0},{6,2},{0,4},{2,6},{12,8},{14,10},{8,12},{10,14},{20,16},{22,... | collective-permute-start | bytes 1572872 | tf_op jit(solution)/shard_map/ppermute | solution.py:123
  117.0 4.5 %collective-permute-start.16 = (bf16[2,4,2,256,128]{4,3,2,1,0:T(8,128)(2,1)}, bf16[2,4,2,256,128]{4,3,2,1,0:T(8,128)(2,1)}, u32[]{:S(2)}, u32[]{:S(2)}) collective-permute-start(bf16[2,4,2,256,128]{4,3,2,1,0:T(8,128)(2,1)} %get-tuple-element.82), channel_id=1, source_target_pairs={{2,0},{0,2},{6,4},{4,6},{10,8},{8,10},{14,12},{12,14},{18,16},{16,... | collective-permute-start | bytes 3145736 | tf_op jit(solution)/shard_map/cond/branch_1_fun/ppermute | solution.py:123
  117.5 5.5 %collective-permute-start.17 = (bf16[2,4,2,256,128]{4,3,2,1,0:T(8,128)(2,1)}, bf16[2,4,2,256,128]{4,3,2,1,0:T(8,128)(2,1)}, u32[]{:S(2)}, u32[]{:S(2)}) collective-permute-start(bf16[2,4,2,256,128]{4,3,2,1,0:T(8,128)(2,1)} %get-tuple-element.83), channel_id=1, source_target_pairs={{2,0},{0,2},{6,4},{4,6},{10,8},{8,10},{14,12},{12,14},{18,16},{16,... | collective-permute-start | bytes 3145736 | tf_op jit(solution)/shard_map/cond/branch_1_fun/ppermute | solution.py:123
  123.0 16.7 %collective-permute-start.46 = (bf16[4,2,256,128]{3,2,1,0:T(8,128)(2,1)S(1)}, bf16[4,2,256,128]{3,2,1,0:T(8,128)(2,1)}, u32[]{:S(2)}, u32[]{:S(2)}) collective-permute-start(bf16[4,2,256,128]{3,2,1,0:T(8,128)(2,1)S(1)} %get-tuple-element.190.refs_2_.refs_1_), channel_id=1, source_target_pairs={{24,0},{26,2},{12,4},{14,6},{0,8},{2,10},{20,12},{22,14},{8,16},{1... | collective-permute-start | bytes 1572872 | tf_op jit(solution)/shard_map/ppermute | solution.py:123
  123.0 16.7 %collective-permute-start.47 = (bf16[4,2,256,128]{3,2,1,0:T(8,128)(2,1)}, bf16[4,2,256,128]{3,2,1,0:T(8,128)(2,1)}, u32[]{:S(2)}, u32[]{:S(2)}) collective-permute-start(bf16[4,2,256,128]{3,2,1,0:T(8,128)(2,1)} %get-tuple-element.193.refs_7_), channel_id=1, source_target_pairs={{4,0},{6,2},{0,4},{2,6},{12,8},{14,10},{8,12},{10,14},{20,16},{22,... | collective-permute-start | bytes 1572872 | tf_op jit(solution)/shard_map/ppermute | solution.py:123
  126.2 24.8 %collective-permute-start.50 = (bf16[4,2,256,128]{3,2,1,0:T(8,128)(2,1)}, bf16[4,2,256,128]{3,2,1,0:T(8,128)(2,1)}, u32[]{:S(2)}, u32[]{:S(2)}) collective-permute-start(bf16[4,2,256,128]{3,2,1,0:T(8,128)(2,1)} %get-tuple-element.196.refs_2_.refs_0_), channel_id=1, source_target_pairs={{24,0},{26,2},{12,4},{14,6},{0,8},{2,10},{20,12},{22,14},{8,16},{1... | collective-permute-start | bytes 1572872 | tf_op jit(solution)/shard_map/ppermute | solution.py:123
  126.7 24.3 %collective-permute-start.51 = (bf16[4,2,256,128]{3,2,1,0:T(8,128)(2,1)}, bf16[4,2,256,128]{3,2,1,0:T(8,128)(2,1)}, u32[]{:S(2)}, u32[]{:S(2)}) collective-permute-start(bf16[4,2,256,128]{3,2,1,0:T(8,128)(2,1)} %get-tuple-element.204.refs_6_), channel_id=1, source_target_pairs={{4,0},{6,2},{0,4},{2,6},{12,8},{14,10},{8,12},{10,14},{20,16},{22,... | collective-permute-start | bytes 1572872 | tf_op jit(solution)/shard_map/ppermute | solution.py:123
  142.7 27.3 %collective-permute-start.48 = (bf16[4,2,256,128]{3,2,1,0:T(8,128)(2,1)S(1)}, bf16[4,2,256,128]{3,2,1,0:T(8,128)(2,1)}, u32[]{:S(2)}, u32[]{:S(2)}) collective-permute-start(bf16[4,2,256,128]{3,2,1,0:T(8,128)(2,1)S(1)} %get-tuple-element.202.refs_2_.refs_1_), channel_id=1, source_target_pairs={{24,0},{26,2},{12,4},{14,6},{0,8},{2,10},{20,12},{22,14},{8,16},{1... | collective-permute-start | bytes 1572872 | tf_op jit(solution)/shard_map/ppermute | solution.py:123
  142.7 27.3 %collective-permute-start.49 = (bf16[4,2,256,128]{3,2,1,0:T(8,128)(2,1)}, bf16[4,2,256,128]{3,2,1,0:T(8,128)(2,1)}, u32[]{:S(2)}, u32[]{:S(2)}) collective-permute-start(bf16[4,2,256,128]{3,2,1,0:T(8,128)(2,1)} %get-tuple-element.203.refs_7_), channel_id=1, source_target_pairs={{4,0},{6,2},{0,4},{2,6},{12,8},{14,10},{8,12},{10,14},{20,16},{22,... | collective-permute-start | bytes 1572872 | tf_op jit(solution)/shard_map/ppermute | solution.py:123
  154.0 36.1 %collective-permute-start.54 = (bf16[2,4,2,256,128]{4,3,2,1,0:T(8,128)(2,1)S(1)}, bf16[2,4,2,256,128]{4,3,2,1,0:T(8,128)(2,1)}, u32[]{:S(2)}, u32[]{:S(2)}) collective-permute-start(bf16[2,4,2,256,128]{4,3,2,1,0:T(8,128)(2,1)S(1)} %get-tuple-element.207.refs_2_.refs_0_), channel_id=1, source_target_pairs={{24,0},{26,2},{12,4},{14,6},{0,8},{2,10},{20,12},{22,14},{8,16},{1... | collective-permute-start | bytes 3145736 | tf_op jit(solution)/shard_map/ppermute | solution.py:123
  154.0 36.1 %collective-permute-start.55 = (bf16[2,4,2,256,128]{4,3,2,1,0:T(8,128)(2,1)}, bf16[2,4,2,256,128]{4,3,2,1,0:T(8,128)(2,1)}, u32[]{:S(2)}, u32[]{:S(2)}) collective-permute-start(bf16[2,4,2,256,128]{4,3,2,1,0:T(8,128)(2,1)} %get-tuple-element.212.refs_3_), channel_id=1, source_target_pairs={{4,0},{6,2},{0,4},{2,6},{12,8},{14,10},{8,12},{10,14},{20,16},{22,... | collective-permute-start | bytes 3145736 | tf_op jit(solution)/shard_map/ppermute | solution.py:123
  173.1 35.0 %collective-permute-start.52 = (bf16[2,4,2,256,128]{4,3,2,1,0:T(8,128)(2,1)S(1)}, bf16[2,4,2,256,128]{4,3,2,1,0:T(8,128)(2,1)}, u32[]{:S(2)}, u32[]{:S(2)}) collective-permute-start(bf16[2,4,2,256,128]{4,3,2,1,0:T(8,128)(2,1)S(1)} %get-tuple-element.210.refs_3_.refs_0_), channel_id=1, source_target_pairs={{24,0},{26,2},{12,4},{14,6},{0,8},{2,10},{20,12},{22,14},{8,16},{1... | collective-permute-start | bytes 3145736 | tf_op jit(solution)/shard_map/ppermute | solution.py:123
  173.1 35.0 %collective-permute-start.53 = (bf16[2,4,2,256,128]{4,3,2,1,0:T(8,128)(2,1)}, bf16[2,4,2,256,128]{4,3,2,1,0:T(8,128)(2,1)}, u32[]{:S(2)}, u32[]{:S(2)}) collective-permute-start(bf16[2,4,2,256,128]{4,3,2,1,0:T(8,128)(2,1)} %get-tuple-element.211.refs_3_), channel_id=1, source_target_pairs={{4,0},{6,2},{0,4},{2,6},{12,8},{14,10},{8,12},{10,14},{20,16},{22,... | collective-permute-start | bytes 3145736 | tf_op jit(solution)/shard_map/ppermute | solution.py:123
  (28 other events, 228.3 us)

commit v4 on v2

--- a/solution.py
+++ b/solution.py
@@ -97,8 +97,8 @@
         input_output_aliases={} if previous is None else {len(operands): 0},
         compiler_params=pltpu.CompilerParams(dimension_semantics=("arbitrary",)),
         cost_estimate=pl.CostEstimate(
-            flops=8 * count * width * size * size * parts * samples,
-            bytes_accessed=count * width * size * (8 * size + 4 * parts * samples),
+            flops=4 * count * width * size * size * parts * samples,
+            bytes_accessed=count * width * size * (4 * size + 2 * parts * samples),
             transcendentals=0,
         ),
     )(table, *operands)
@@ -214,18 +214,15 @@
     ]
     pieces = [Piece(stay, moves), Piece(turn(go), moves)]
 
-    def turned(at, token):
-        mine = columns[:, firsts[at] : firsts[at] + chunks[at]] * weights
-        (mine,) = after([mine], [token])
-        return Piece(lax.all_to_all(mine, "chan", split_axis=0, concat_axis=0), moves)
-
-    pieces.append(turned(1, pieces[1].own))
+    begun = [None, None]
+    for first, size in zip(firsts[1:], chunks[1:]):
+        mine = columns[:, first : first + size] * weights
+        begun.append(None)
+        pieces.append(Piece(lax.all_to_all(mine, "chan", split_axis=0, concat_axis=0), moves))
+    begun.append(None)
 
     count = len(chunks) + 1
-    steps = [("near", 0), ("near", 1)]
-    for at in range(count - 2):
-        steps += [("far", at), ("near", at + 2)]
-    steps += [("far", count - 2), ("far", count - 1)]
+    steps = [(kind, at) for kind in ("near", "far") for at in range(count)]
 
     def kernel(at, result):
         if at == 0:
@@ -245,12 +242,16 @@
                 piece.theirs, piece.partner = after([piece.theirs, piece.partner], [token])
             shared.append(piece.near_twins())
         else:
-            if token is not None:
-                piece.others, piece.passed = after([piece.others, piece.passed], [token])
+            kept, waits = [piece.others, piece.passed], [] if token is None else [token]
+            if result is not None and step < len(steps) - 1:
+                kept.append(result)
+            kept = after(kept, waits) if waits or len(kept) == 3 else kept
+            piece.others, piece.passed = kept[:2]
+            result = kept[2] if len(kept) == 3 else result
             shared.append(piece.far_twins())
             if at >= 1:
                 result = kernel(at - 1, result)
-                ready.append(step + 3)
+                ready.append(step + 4)
 
     token = None
     for step, (kind, at) in enumerate(steps):
@@ -264,6 +265,8 @@
                 if ready and ready[0] <= step:
                     ready.pop(0)
                     kept.append(result)
+            elif begun[at + 1] is not None:
+                waits.append(begun[at + 1])
             kept = after(kept, waits)
             piece.own = kept[0]
             if kind == "far":
@@ -273,8 +276,6 @@
             token = piece.own
         if kind == "near":
             piece.near()
-            if 2 <= at < count - 1:
-                pieces.append(turned(at, piece.own))
         else:
             piece.far()
     share(len(steps) - 2, token)
@@ -301,7 +302,7 @@
 def on_device(voltages, input_flags, pair_order):
     weights = input_flags.astype(jnp.bfloat16)[None, None, :, None]
     if lax.axis_size("grp") == 16 and lax.axis_size("chan") == 2:
-        return split_exchange(voltages, weights, pair_order, (6, 6, 4))
+        return split_exchange(voltages, weights, pair_order, (8, 4, 4))
     return window_exchange(voltages, weights, pair_order)
 
 

time: 244 us -> 223 us (0.914)
  waiting for transfers between devices: 134 us -> 111 us
  blocking collectives: 0 us -> 15.2 us
  starting transfers between devices: 50.7 us -> 39.6 us
    ppermute x37, waiting for transfers between devices: 134 us -> 111 us  [permute(): return lambda block: lax.ppermute(block, axis, route)]
    all_to_all x0 -> x1, blocking collectives: none -> 15.2 us  [split_exchange(): lax.all_to_all(mine, 'chan', split_axis=0, concat_axis=0)]
    ppermute x37, starting transfers between devices: 43.3 us -> 36 us  [permute(): return lambda block: lax.ppermute(block, axis, route)]
    all_to_all x2 -> x1, starting transfers between devices: 7.39 us -> 3.58 us  [split_exchange(): lax.all_to_all(mine, 'chan', split_axis=0, concat_axis=0)]
    mul x2 -> x1, other arithmetic: 5.09 us -> 2.73 us  [split_exchange(): mine = columns[:, first:first + size] * weights]
  transfers between devices with their start and end apart: 39 -> 38, of which waited for: 31 -> 28; matrix products, arithmetic and copies ran while one was open for 2% -> 2% of each run, Pallas kernels for 15% -> 17%
where the time goes in v4:
time: 223 us; the launch traced here: 222 us
  waiting for transfers between devices  111 us (50%)
  Pallas kernels  50.2 us (23%)
  starting transfers between devices  39.6 us (18%)
  blocking collectives  15.2 us (7%)
  other arithmetic  5.79 us (3%)
    ppermute x37, waiting for transfers between devices, permute(): return lambda block: lax.ppermute(block, axis, route)  111 us
    pallas_call x3, Pallas kernels, correlate(): pl.pallas_call(functools.partial(pair_kernel, variants, parts, len(source...  50.1 us
    ppermute x37, starting transfers between devices, permute(): return lambda block: lax.ppermute(block, axis, route)  36 us
    all_to_all x1, blocking collectives, split_exchange(): lax.all_to_all(mine, 'chan', split_axis=0, concat_axis=0)  15.2 us
  transfers between devices with their start and end apart: 38, of which 28 were waited for; matrix products, arithmetic and copies ran while one was open for 2% of the time, Pallas kernels for 17%

profile of v4, /device:TPU:0, one launch (start us, length us, event | category | flops | bytes accessed | tf_op | source)
XLA Modules:
  0.0 222.2 jit_solution(18429735602895864336)
XLA Ops:
  2.5 3.0 %collective-permute-start.20 = (bf16[8,2,256,128]{3,2,1,0:T(8,128)(2,1)S(1)}, bf16[8,2,256,128]{3,2,1,0:T(8,128)(2,1)}, u32[]{:S(2)}, u32[]{:S(2)}) collective-permute-start(bf16[8,2,256,128]{3,2,1,0:T(8,128)(2,1)S(1)} %get-tuple-element.148), channel_id=1, source_target_pairs={{0,1},{1,0},{2,3},{3,2},{4,5},{5,4},{6,7},{7,6},{8,9},{9,8},{10,11... | collective-permute-start | bytes 3145736 | tf_op jit(solution)/shard_map/ppermute | solution.py:120
  7.0 3.6 %collective-permute-start.23 = (bf16[8,2,256,128]{3,2,1,0:T(8,128)(2,1)S(1)}, bf16[8,2,256,128]{3,2,1,0:T(8,128)(2,1)}, u32[]{:S(2)}, u32[]{:S(2)}) collective-permute-start(bf16[8,2,256,128]{3,2,1,0:T(8,128)(2,1)S(1)} %get-tuple-element.147.refs_0_), channel_id=1, source_target_pairs={{8,0},{10,2},{28,4},{30,6},{16,8},{18,10},{4,12},{6,14},{24,16},{2... | collective-permute-start | bytes 3145736 | tf_op jit(solution)/shard_map/ppermute | solution.py:120
  10.6 18.1 %collective-permute-done.20.refs_0_ = bf16[8,2,256,128]{3,2,1,0:T(8,128)(2,1)} collective-permute-done((bf16[8,2,256,128]{3,2,1,0:T(8,128)(2,1)S(1)}, bf16[8,2,256,128]{3,2,1,0:T(8,128)(2,1)}, u32[]{:S(2)}, u32[]{:S(2)}) %collective-permute-start.20) | collective-permute-done | bytes 1048608 | tf_op jit(solution)/shard_map/ppermute | solution.py:120
  28.7 3.8 %collective-permute-start.21 = (bf16[8,2,256,128]{3,2,1,0:T(8,128)(2,1)}, bf16[8,2,256,128]{3,2,1,0:T(8,128)(2,1)}, u32[]{:S(2)}, u32[]{:S(2)}) collective-permute-start(bf16[8,2,256,128]{3,2,1,0:T(8,128)(2,1)} %collective-permute-done.20.refs_0_), channel_id=1, source_target_pairs={{8,0},{10,2},{28,4},{30,6},{16,8},{18,10},{4,12},{6,14},{24,16},{2... | collective-permute-start | bytes 3145736 | tf_op jit(solution)/shard_map/ppermute | solution.py:120
  32.6 2.7 %slice_multiply_fusion = (bf16[2,4,2,256,128]{4,3,2,1,0:T(8,128)(2,1)S(1)}, bf16[2,4,2,256,128]{4,3,2,1,0:T(8,128)(2,1)}) fusion(bf16[2,16,2,256,128]{4,3,2,1,0:T(8,128)(2,1)} %bitcast.4, bf16[256]{0:T(256)(128)(2,1)S(1)} %convert_element_type.7), kind=kLoop, calls=%fused_computation | loop fusion | flops 1048576 | bytes 4194816 | tf_op jit(solution)/shard_map/mul | solution.py:219
  35.3 15.2 %all_to_all.10.refs_0_ = bf16[2,4,2,256,128]{4,3,2,1,0:T(8,128)(2,1)S(1)} all-to-all(bf16[2,4,2,256,128]{4,3,2,1,0:T(8,128)(2,1)S(1)} %get-tuple-element.149), channel_id=1, replica_groups=mesh['grp'=16,'chan'=2] {'chan'}, dimensions={0} | all-to-all | bytes 2097152 | tf_op jit(solution)/shard_map/all_to_all | solution.py:221
  50.5 3.6 %all-to-all-start = ((bf16[2,4,2,256,128]{4,3,2,1,0:T(8,128)(2,1)}), bf16[2,4,2,256,128]{4,3,2,1,0:T(8,128)(2,1)S(1)}, u32[]{:S(2)}, u32[]{:S(2)}) async-start(bf16[2,4,2,256,128]{4,3,2,1,0:T(8,128)(2,1)} %get-tuple-element.150), calls=%async_computation | async-start | bytes 2097152 | tf_op jit(solution)/shard_map/all_to_all | solution.py:221
  54.7 6.1 %conditional.8 = (bf16[8,2,256,128]{3,2,1,0:T(8,128)(2,1)}, bf16[8,2,256,128]{3,2,1,0:T(8,128)(2,1)}, bf16[8,2,256,128]{3,2,1,0:T(8,128)(2,1)}) conditional(s32[]{:T(128)} %bitcast.2, () %tuple.68, (bf16[8,2,256,128]{3,2,1,0:T(8,128)(2,1)S(1)}, bf16[8,2,256,128]{3,2,1,0:T(8,128)(2,1)}, bf16[8,2,256,128]{3,2,1,0:T(8,128)(2,1)}) %tuple.69), branch_computations={%region_0.0_spmd, %region_1.0_spmd} | conditional | bytes 12583056 | solution.py:185
  55.4 2.9 %collective-permute-done = bf16[8,2,256,128]{3,2,1,0:T(8,128)(2,1)} collective-permute-done((bf16[8,2,256,128]{3,2,1,0:T(8,128)(2,1)S(1)}, bf16[8,2,256,128]{3,2,1,0:T(8,128)(2,1)}, u32[]{:S(2)}, u32[]{:S(2)}) %collective-permute-start) | collective-permute-done | bytes 1048608 | tf_op jit(solution)/shard_map/cond/branch_1_fun/ppermute | solution.py:120
  62.6 6.1 %conditional.9 = (bf16[8,2,256,128]{3,2,1,0:T(8,128)(2,1)}, bf16[8,2,256,128]{3,2,1,0:T(8,128)(2,1)}, bf16[8,2,256,128]{3,2,1,0:T(8,128)(2,1)}) conditional(s32[]{:T(128)} %bitcast.2, () %tuple.67, (bf16[8,2,256,128]{3,2,1,0:T(8,128)(2,1)}, bf16[8,2,256,128]{3,2,1,0:T(8,128)(2,1)}, bf16[8,2,256,128]{3,2,1,0:T(8,128)(2,1)}) %tuple.70), branch_computations={%region_2.0_spmd, %region_3.0_spmd} | conditional | bytes 12583056 | solution.py:185
  68.6 3.8 %collective-permute-start.25 = (bf16[2,4,2,256,128]{4,3,2,1,0:T(8,128)(2,1)S(1)}, bf16[2,4,2,256,128]{4,3,2,1,0:T(8,128)(2,1)}, u32[]{:S(2)}, u32[]{:S(2)}) collective-permute-start(bf16[2,4,2,256,128]{4,3,2,1,0:T(8,128)(2,1)S(1)} %shard_map.39.refs_2_.refs_0_), channel_id=1, source_target_pairs={{8,0},{10,2},{28,4},{30,6},{16,8},{18,10},{4,12},{6,14},{24,16},{2... | collective-permute-start | bytes 3145736 | tf_op jit(solution)/shard_map/ppermute | solution.py:120
  72.5 14.5 %collective-permute-done.27.refs_0_ = bf16[2,4,2,256,128]{4,3,2,1,0:T(8,128)(2,1)} collective-permute-done((bf16[2,4,2,256,128]{4,3,2,1,0:T(8,128)(2,1)S(1)}, bf16[2,4,2,256,128]{4,3,2,1,0:T(8,128)(2,1)}, u32[]{:S(2)}, u32[]{:S(2)}) %collective-permute-start.27) | collective-permute-done | bytes 1048608 | tf_op jit(solution)/shard_map/ppermute | solution.py:120
  88.5 6.0 %conditional.10 = (bf16[2,4,2,256,128]{4,3,2,1,0:T(8,128)(2,1)}, bf16[2,4,2,256,128]{4,3,2,1,0:T(8,128)(2,1)}, bf16[2,4,2,256,128]{4,3,2,1,0:T(8,128)(2,1)}) conditional(s32[]{:T(128)} %bitcast.2, () %tuple.71, (bf16[2,4,2,256,128]{4,3,2,1,0:T(8,128)(2,1)S(1)}, bf16[2,4,2,256,128]{4,3,2,1,0:T(8,128)(2,1)}, ...), branch_computations={%region_4.0_spmd, %region_5.0_spmd} | conditional | bytes 12583056 | solution.py:185
  89.0 3.7 %collective-permute-done.6 = bf16[2,4,2,256,128]{4,3,2,1,0:T(8,128)(2,1)} collective-permute-done((bf16[2,4,2,256,128]{4,3,2,1,0:T(8,128)(2,1)S(1)}, bf16[2,4,2,256,128]{4,3,2,1,0:T(8,128)(2,1)}, u32[]{:S(2)}, u32[]{:S(2)}) %collective-permute-start.6) | collective-permute-done | bytes 1048608 | tf_op jit(solution)/shard_map/cond/branch_1_fun/ppermute | solution.py:120
  95.0 3.5 %collective-permute-start.32 = (bf16[8,2,256,128]{3,2,1,0:T(8,128)(2,1)}, bf16[8,2,256,128]{3,2,1,0:T(8,128)(2,1)}, u32[]{:S(2)}, u32[]{:S(2)}) collective-permute-start(bf16[8,2,256,128]{3,2,1,0:T(8,128)(2,1)} %get-tuple-element.127.refs_6_), channel_id=1, source_target_pairs={{4,0},{6,2},{0,4},{2,6},{12,8},{14,10},{8,12},{10,14},{20,16},{22,... | collective-permute-start | bytes 3145736 | tf_op jit(solution)/shard_map/ppermute | solution.py:120
  98.5 10.1 %collective-permute-done.25.refs_0_ = bf16[2,4,2,256,128]{4,3,2,1,0:T(8,128)(2,1)} collective-permute-done((bf16[2,4,2,256,128]{4,3,2,1,0:T(8,128)(2,1)S(1)}, bf16[2,4,2,256,128]{4,3,2,1,0:T(8,128)(2,1)}, u32[]{:S(2)}, u32[]{:S(2)}) %collective-permute-start.25) | collective-permute-done | bytes 1048608 | tf_op jit(solution)/shard_map/ppermute | solution.py:120
  111.0 6.0 %conditional.11 = (bf16[2,4,2,256,128]{4,3,2,1,0:T(8,128)(2,1)}, bf16[2,4,2,256,128]{4,3,2,1,0:T(8,128)(2,1)}, bf16[2,4,2,256,128]{4,3,2,1,0:T(8,128)(2,1)}) conditional(s32[]{:T(128)} %bitcast.2, () %tuple.74, (bf16[2,4,2,256,128]{4,3,2,1,0:T(8,128)(2,1)S(1)}, bf16[2,4,2,256,128]{4,3,2,1,0:T(8,128)(2,1)}, ...), branch_computations={%region_6.0_spmd, %region_7.0_spmd} | conditional | bytes 12583056 | solution.py:185
  114.0 3.0 %collective-permute-done.11 = bf16[2,4,2,256,128]{4,3,2,1,0:T(8,128)(2,1)} collective-permute-done((bf16[2,4,2,256,128]{4,3,2,1,0:T(8,128)(2,1)}, bf16[2,4,2,256,128]{4,3,2,1,0:T(8,128)(2,1)}, u32[]{:S(2)}, u32[]{:S(2)}) %collective-permute-start.11) | collective-permute-done | bytes 1048608 | tf_op jit(solution)/shard_map/cond/branch_1_fun/ppermute | solution.py:120
  117.5 3.5 %collective-permute-start.30 = (bf16[8,2,256,128]{3,2,1,0:T(8,128)(2,1)}, bf16[8,2,256,128]{3,2,1,0:T(8,128)(2,1)}, u32[]{:S(2)}, u32[]{:S(2)}) collective-permute-start(bf16[8,2,256,128]{3,2,1,0:T(8,128)(2,1)} %get-tuple-element.126.refs_7_), channel_id=1, source_target_pairs={{4,0},{6,2},{0,4},{2,6},{12,8},{14,10},{8,12},{10,14},{20,16},{22,... | collective-permute-start | bytes 3145736 | tf_op jit(solution)/shard_map/ppermute | solution.py:120
  121.0 12.1 %collective-permute-done.31.refs_0_ = bf16[8,2,256,128]{3,2,1,0:T(8,128)(2,1)} collective-permute-done((bf16[8,2,256,128]{3,2,1,0:T(8,128)(2,1)S(1)}, bf16[8,2,256,128]{3,2,1,0:T(8,128)(2,1)}, u32[]{:S(2)}, u32[]{:S(2)}) %collective-permute-start.31) | collective-permute-done | bytes 1048608 | tf_op jit(solution)/shard_map/ppermute | solution.py:120
  133.4 4.5 %conditional.12 = (bf16[8,2,256,128]{3,2,1,0:T(8,128)(2,1)}, bf16[8,2,256,128]{3,2,1,0:T(8,128)(2,1)}) conditional(s32[]{:T(128)} %bitcast.2, () %tuple.76, (bf16[8,2,256,128]{3,2,1,0:T(8,128)(2,1)}, bf16[8,2,256,128]{3,2,1,0:T(8,128)(2,1)}) %shard_map.44), branch_computations={%region_8.0_spmd, %region_9.0_spmd} | conditional | bytes 8388704 | solution.py:185
  133.9 2.5 %collective-permute-done.12 = bf16[8,2,256,128]{3,2,1,0:T(8,128)(2,1)} collective-permute-done((bf16[8,2,256,128]{3,2,1,0:T(8,128)(2,1)}, bf16[8,2,256,128]{3,2,1,0:T(8,128)(2,1)}, u32[]{:S(2)}, u32[]{:S(2)}) %collective-permute-start.12) | collective-permute-done | bytes 1048608 | tf_op jit(solution)/shard_map/cond/branch_1_fun/ppermute | solution.py:120
  138.4 3.5 %collective-permute-start.36 = (bf16[2,4,2,256,128]{4,3,2,1,0:T(8,128)(2,1)}, bf16[2,4,2,256,128]{4,3,2,1,0:T(8,128)(2,1)}, u32[]{:S(2)}, u32[]{:S(2)}) collective-permute-start(bf16[2,4,2,256,128]{4,3,2,1,0:T(8,128)(2,1)} %get-tuple-element.137.refs_3_), channel_id=1, source_target_pairs={{4,0},{6,2},{0,4},{2,6},{12,8},{14,10},{8,12},{10,14},{20,16},{22,... | collective-permute-start | bytes 3145736 | tf_op jit(solution)/shard_map/ppermute | solution.py:120
  142.0 13.6 %collective-permute-done.29.refs_0_ = bf16[8,2,256,128]{3,2,1,0:T(8,128)(2,1)} collective-permute-done((bf16[8,2,256,128]{3,2,1,0:T(8,128)(2,1)}, bf16[8,2,256,128]{3,2,1,0:T(8,128)(2,1)}, u32[]{:S(2)}, u32[]{:S(2)}) %collective-permute-start.29) | collective-permute-done | bytes 1048608 | tf_op jit(solution)/shard_map/ppermute | solution.py:120
  155.9 4.5 %conditional.13 = (bf16[8,2,256,128]{3,2,1,0:T(8,128)(2,1)}, bf16[8,2,256,128]{3,2,1,0:T(8,128)(2,1)}) conditional(s32[]{:T(128)} %bitcast.2, () %tuple.73, (bf16[8,2,256,128]{3,2,1,0:T(8,128)(2,1)}, bf16[8,2,256,128]{3,2,1,0:T(8,128)(2,1)}) %shard_map.46), branch_computations={%region_10.0_spmd, %region_11.0_spmd} | conditional | bytes 8388704 | solution.py:185
  156.4 2.5 %collective-permute-done.14 = bf16[8,2,256,128]{3,2,1,0:T(8,128)(2,1)} collective-permute-done((bf16[8,2,256,128]{3,2,1,0:T(8,128)(2,1)}, bf16[8,2,256,128]{3,2,1,0:T(8,128)(2,1)}, u32[]{:S(2)}, u32[]{:S(2)}) %collective-permute-start.14) | collective-permute-done | bytes 1048608 | tf_op jit(solution)/shard_map/cond/branch_1_fun/ppermute | solution.py:120
  162.8 23.3 %shard_map.48.refs_2_ = f32[1,9,16,256,512]{4,3,2,1,0:T(8,128)} custom-call(s32[10]{0:T(128)} %pad_add_fusion.table, bf16[8,2,256,128]{3,2,1,0:T(8,128)(2,1)S(1)} %get-tuple-element.119.refs_2_.refs_0_, bf16[8,2,256,128]{3,2,1,0:T(8,128)(2,1)} %get-tuple-element.125.refs_2_.refs_1_, bf16[8,2,256,128]{3,2,1,0:T(8,128)(2,1)} %collective-permute-done.24.refs_5_.refs_2_, ...), custom_call_target="tpu_custom_call" | custom-call | flops 4831838208 | bytes 28311552 | tf_op jit(solution)/shard_map/pallas_call | solution.py:84
  186.2 4.6 %conditional.15 = (bf16[2,4,2,256,128]{4,3,2,1,0:T(8,128)(2,1)}, bf16[2,4,2,256,128]{4,3,2,1,0:T(8,128)(2,1)}) conditional(s32[]{:T(128)} %bitcast.2, () %tuple.79, (bf16[2,4,2,256,128]{4,3,2,1,0:T(8,128)(2,1)}, bf16[2,4,2,256,128]{4,3,2,1,0:T(8,128)(2,1)}) %tuple.80), branch_computations={%region_14.0_spmd, %region_15.0_spmd} | conditional | bytes 8388704 | solution.py:185
  186.8 2.5 %collective-permute-done.18 = bf16[2,4,2,256,128]{4,3,2,1,0:T(8,128)(2,1)} collective-permute-done((bf16[2,4,2,256,128]{4,3,2,1,0:T(8,128)(2,1)}, bf16[2,4,2,256,128]{4,3,2,1,0:T(8,128)(2,1)}, u32[]{:S(2)}, u32[]{:S(2)}) %collective-permute-start.18) | collective-permute-done | bytes 1048608 | tf_op jit(solution)/shard_map/cond/branch_1_fun/ppermute | solution.py:120
  190.8 13.4 %shard_map.50.refs_10_ = f32[1,9,16,256,512]{4,3,2,1,0:T(8,128)} custom-call(s32[10]{0:T(128)} %pad_add_fusion.table, bf16[2,4,2,256,128]{4,3,2,1,0:T(8,128)(2,1)S(1)} %get-tuple-element.130.refs_2_.refs_0_, bf16[2,4,2,256,128]{4,3,2,1,0:T(8,128)(2,1)} %get-tuple-element.115.refs_4_.refs_1_, ...), custom_call_target="tpu_custom_call", output_to_operand_aliasing={{}: (11, {})} | custom-call | flops 2415919104 | bytes 14155776 | tf_op jit(solution)/shard_map/pallas_call | solution.py:84
  204.2 4.6 %conditional.14 = (bf16[2,4,2,256,128]{4,3,2,1,0:T(8,128)(2,1)}, bf16[2,4,2,256,128]{4,3,2,1,0:T(8,128)(2,1)}) conditional(s32[]{:T(128)} %bitcast.2, () %tuple.77, (bf16[2,4,2,256,128]{4,3,2,1,0:T(8,128)(2,1)}, bf16[2,4,2,256,128]{4,3,2,1,0:T(8,128)(2,1)}) %tuple.78), branch_computations={%region_12.0_spmd, %region_13.0_spmd} | conditional | bytes 8388704 | solution.py:185
  208.8 13.4 %shard_map.51 = f32[1,9,16,256,512]{4,3,2,1,0:T(8,128)} custom-call(s32[10]{0:T(128)} %pad_add_fusion.table, bf16[2,4,2,256,128]{4,3,2,1,0:T(8,128)(2,1)S(1)} %get-tuple-element.133.refs_3_.refs_0_, bf16[2,4,2,256,128]{4,3,2,1,0:T(8,128)(2,1)} %get-tuple-element.121.refs_4_.refs_1_, ...), custom_call_target="tpu_custom_call", output_to_operand_aliasing={{}: (11, {})} | custom-call | flops 2415919104 | bytes 14155776 | tf_op jit(solution)/shard_map/pallas_call | solution.py:84
  (74 shorter events, 39.4 us)
Async XLA Ops:
  2.5 26.3 %collective-permute-start.20 = (bf16[8,2,256,128]{3,2,1,0:T(8,128)(2,1)S(1)}, bf16[8,2,256,128]{3,2,1,0:T(8,128)(2,1)}, u32[]{:S(2)}, u32[]{:S(2)}) collective-permute-start(bf16[8,2,256,128]{3,2,1,0:T(8,128)(2,1)S(1)} %get-tuple-element.148), channel_id=1, source_target_pairs={{0,1},{1,0},{2,3},{3,2},{4,5},{5,4},{6,7},{7,6},{8,9},{9,8},{10,11... | collective-permute-start | bytes 3145736 | tf_op jit(solution)/shard_map/ppermute | solution.py:120
  5.5 49.3 %collective-permute-start.24 = (bf16[8,2,256,128]{3,2,1,0:T(8,128)(2,1)S(1)}, bf16[8,2,256,128]{3,2,1,0:T(8,128)(2,1)}, u32[]{:S(2)}, u32[]{:S(2)}) collective-permute-start(bf16[8,2,256,128]{3,2,1,0:T(8,128)(2,1)S(1)} %get-tuple-element.147.refs_0_), channel_id=1, source_target_pairs={{4,0},{6,2},{0,4},{2,6},{12,8},{14,10},{8,12},{10,14},{20,16},{22,... | collective-permute-start | bytes 3145736 | tf_op jit(solution)/shard_map/ppermute | solution.py:120
  7.0 47.7 %collective-permute-start.23 = (bf16[8,2,256,128]{3,2,1,0:T(8,128)(2,1)S(1)}, bf16[8,2,256,128]{3,2,1,0:T(8,128)(2,1)}, u32[]{:S(2)}, u32[]{:S(2)}) collective-permute-start(bf16[8,2,256,128]{3,2,1,0:T(8,128)(2,1)S(1)} %get-tuple-element.147.refs_0_), channel_id=1, source_target_pairs={{8,0},{10,2},{28,4},{30,6},{16,8},{18,10},{4,12},{6,14},{24,16},{2... | collective-permute-start | bytes 3145736 | tf_op jit(solution)/shard_map/ppermute | solution.py:120
  28.7 33.8 %collective-permute-start.21 = (bf16[8,2,256,128]{3,2,1,0:T(8,128)(2,1)}, bf16[8,2,256,128]{3,2,1,0:T(8,128)(2,1)}, u32[]{:S(2)}, u32[]{:S(2)}) collective-permute-start(bf16[8,2,256,128]{3,2,1,0:T(8,128)(2,1)} %collective-permute-done.20.refs_0_), channel_id=1, source_target_pairs={{8,0},{10,2},{28,4},{30,6},{16,8},{18,10},{4,12},{6,14},{24,16},{2... | collective-permute-start | bytes 3145736 | tf_op jit(solution)/shard_map/ppermute | solution.py:120
  32.6 30.0 %collective-permute-start.22 = (bf16[8,2,256,128]{3,2,1,0:T(8,128)(2,1)}, bf16[8,2,256,128]{3,2,1,0:T(8,128)(2,1)}, u32[]{:S(2)}, u32[]{:S(2)}) collective-permute-start(bf16[8,2,256,128]{3,2,1,0:T(8,128)(2,1)} %collective-permute-done.20.refs_0_), channel_id=1, source_target_pairs={{4,0},{6,2},{0,4},{2,6},{12,8},{14,10},{8,12},{10,14},{20,16},{22,... | collective-permute-start | bytes 3145736 | tf_op jit(solution)/shard_map/ppermute | solution.py:120
  50.5 18.2 %all-to-all-start = ((bf16[2,4,2,256,128]{4,3,2,1,0:T(8,128)(2,1)}), bf16[2,4,2,256,128]{4,3,2,1,0:T(8,128)(2,1)S(1)}, u32[]{:S(2)}, u32[]{:S(2)}) async-start(bf16[2,4,2,256,128]{4,3,2,1,0:T(8,128)(2,1)} %get-tuple-element.150), calls=%async_computation | async-start | bytes 2097152 | tf_op jit(solution)/shard_map/all_to_all | solution.py:221
  54.8 3.6 %collective-permute-start = (bf16[8,2,256,128]{3,2,1,0:T(8,128)(2,1)S(1)}, bf16[8,2,256,128]{3,2,1,0:T(8,128)(2,1)}, u32[]{:S(2)}, u32[]{:S(2)}) collective-permute-start(bf16[8,2,256,128]{3,2,1,0:T(8,128)(2,1)S(1)} %get-tuple-element.45), channel_id=1, source_target_pairs={{2,0},{0,2},{6,4},{4,6},{10,8},{8,10},{14,12},{12,14},{18,16},{16,... | collective-permute-start | bytes 3145736 | tf_op jit(solution)/shard_map/cond/branch_1_fun/ppermute | solution.py:120
  54.8 4.5 %collective-permute-start.1 = (bf16[8,2,256,128]{3,2,1,0:T(8,128)(2,1)}, bf16[8,2,256,128]{3,2,1,0:T(8,128)(2,1)}, u32[]{:S(2)}, u32[]{:S(2)}) collective-permute-start(bf16[8,2,256,128]{3,2,1,0:T(8,128)(2,1)} %get-tuple-element.46), channel_id=1, source_target_pairs={{2,0},{0,2},{6,4},{4,6},{10,8},{8,10},{14,12},{12,14},{18,16},{16,... | collective-permute-start | bytes 3145736 | tf_op jit(solution)/shard_map/cond/branch_1_fun/ppermute | solution.py:120
  55.3 5.5 %collective-permute-start.2 = (bf16[8,2,256,128]{3,2,1,0:T(8,128)(2,1)}, bf16[8,2,256,128]{3,2,1,0:T(8,128)(2,1)}, u32[]{:S(2)}, u32[]{:S(2)}) collective-permute-start(bf16[8,2,256,128]{3,2,1,0:T(8,128)(2,1)} %get-tuple-element.47), channel_id=1, source_target_pairs={{2,0},{0,2},{6,4},{4,6},{10,8},{8,10},{14,12},{12,14},{18,16},{16,... | collective-permute-start | bytes 3145736 | tf_op jit(solution)/shard_map/cond/branch_1_fun/ppermute | solution.py:120
  60.8 26.1 %collective-permute-start.27 = (bf16[2,4,2,256,128]{4,3,2,1,0:T(8,128)(2,1)S(1)}, bf16[2,4,2,256,128]{4,3,2,1,0:T(8,128)(2,1)}, u32[]{:S(2)}, u32[]{:S(2)}) collective-permute-start(bf16[2,4,2,256,128]{4,3,2,1,0:T(8,128)(2,1)S(1)} %shard_map.37.refs_2_.refs_0_), channel_id=1, source_target_pairs={{8,0},{10,2},{28,4},{30,6},{16,8},{18,10},{4,12},{6,14},{24,16},{2... | collective-permute-start | bytes 3145736 | tf_op jit(solution)/shard_map/ppermute | solution.py:120
  62.3 26.1 %collective-permute-start.28 = (bf16[2,4,2,256,128]{4,3,2,1,0:T(8,128)(2,1)S(1)}, bf16[2,4,2,256,128]{4,3,2,1,0:T(8,128)(2,1)}, u32[]{:S(2)}, u32[]{:S(2)}) collective-permute-start(bf16[2,4,2,256,128]{4,3,2,1,0:T(8,128)(2,1)S(1)} %shard_map.37.refs_2_.refs_0_), channel_id=1, source_target_pairs={{4,0},{6,2},{0,4},{2,6},{12,8},{14,10},{8,12},{10,14},{20,16},{22,... | collective-permute-start | bytes 3145736 | tf_op jit(solution)/shard_map/ppermute | solution.py:120
  62.7 4.5 %collective-permute-start.4 = (bf16[8,2,256,128]{3,2,1,0:T(8,128)(2,1)}, bf16[8,2,256,128]{3,2,1,0:T(8,128)(2,1)}, u32[]{:S(2)}, u32[]{:S(2)}) collective-permute-start(bf16[8,2,256,128]{3,2,1,0:T(8,128)(2,1)} %get-tuple-element.49), channel_id=1, source_target_pairs={{2,0},{0,2},{6,4},{4,6},{10,8},{8,10},{14,12},{12,14},{18,16},{16,... | collective-permute-start | bytes 3145736 | tf_op jit(solution)/shard_map/cond/branch_1_fun/ppermute | solution.py:120
  63.2 5.5 %collective-permute-start.5 = (bf16[8,2,256,128]{3,2,1,0:T(8,128)(2,1)}, bf16[8,2,256,128]{3,2,1,0:T(8,128)(2,1)}, u32[]{:S(2)}, u32[]{:S(2)}) collective-permute-start(bf16[8,2,256,128]{3,2,1,0:T(8,128)(2,1)} %get-tuple-element.50), channel_id=1, source_target_pairs={{2,0},{0,2},{6,4},{4,6},{10,8},{8,10},{14,12},{12,14},{18,16},{16,... | collective-permute-start | bytes 3145736 | tf_op jit(solution)/shard_map/cond/branch_1_fun/ppermute | solution.py:120
  68.6 40.0 %collective-permute-start.25 = (bf16[2,4,2,256,128]{4,3,2,1,0:T(8,128)(2,1)S(1)}, bf16[2,4,2,256,128]{4,3,2,1,0:T(8,128)(2,1)}, u32[]{:S(2)}, u32[]{:S(2)}) collective-permute-start(bf16[2,4,2,256,128]{4,3,2,1,0:T(8,128)(2,1)S(1)} %shard_map.39.refs_2_.refs_0_), channel_id=1, source_target_pairs={{8,0},{10,2},{28,4},{30,6},{16,8},{18,10},{4,12},{6,14},{24,16},{2... | collective-permute-start | bytes 3145736 | tf_op jit(solution)/shard_map/ppermute | solution.py:120
  72.5 38.5 %collective-permute-start.26 = (bf16[2,4,2,256,128]{4,3,2,1,0:T(8,128)(2,1)S(1)}, bf16[2,4,2,256,128]{4,3,2,1,0:T(8,128)(2,1)}, u32[]{:S(2)}, u32[]{:S(2)}) collective-permute-start(bf16[2,4,2,256,128]{4,3,2,1,0:T(8,128)(2,1)S(1)} %shard_map.39.refs_2_.refs_0_), channel_id=1, source_target_pairs={{4,0},{6,2},{0,4},{2,6},{12,8},{14,10},{8,12},{10,14},{20,16},{22,... | collective-permute-start | bytes 3145736 | tf_op jit(solution)/shard_map/ppermute | solution.py:120
  88.5 4.3 %collective-permute-start.6 = (bf16[2,4,2,256,128]{4,3,2,1,0:T(8,128)(2,1)S(1)}, bf16[2,4,2,256,128]{4,3,2,1,0:T(8,128)(2,1)}, u32[]{:S(2)}, u32[]{:S(2)}) collective-permute-start(bf16[2,4,2,256,128]{4,3,2,1,0:T(8,128)(2,1)S(1)} %get-tuple-element.51), channel_id=1, source_target_pairs={{2,0},{0,2},{6,4},{4,6},{10,8},{8,10},{14,12},{12,14},{18,16},{16,... | collective-permute-start | bytes 3145736 | tf_op jit(solution)/shard_map/cond/branch_1_fun/ppermute | solution.py:120
  88.5 4.5 %collective-permute-start.7 = (bf16[2,4,2,256,128]{4,3,2,1,0:T(8,128)(2,1)}, bf16[2,4,2,256,128]{4,3,2,1,0:T(8,128)(2,1)}, u32[]{:S(2)}, u32[]{:S(2)}) collective-permute-start(bf16[2,4,2,256,128]{4,3,2,1,0:T(8,128)(2,1)} %get-tuple-element.52), channel_id=1, source_target_pairs={{2,0},{0,2},{6,4},{4,6},{10,8},{8,10},{14,12},{12,14},{18,16},{16,... | collective-permute-start | bytes 3145736 | tf_op jit(solution)/shard_map/cond/branch_1_fun/ppermute | solution.py:120
  89.0 5.5 %collective-permute-start.8 = (bf16[2,4,2,256,128]{4,3,2,1,0:T(8,128)(2,1)}, bf16[2,4,2,256,128]{4,3,2,1,0:T(8,128)(2,1)}, u32[]{:S(2)}, u32[]{:S(2)}) collective-permute-start(bf16[2,4,2,256,128]{4,3,2,1,0:T(8,128)(2,1)} %get-tuple-element.53), channel_id=1, source_target_pairs={{2,0},{0,2},{6,4},{4,6},{10,8},{8,10},{14,12},{12,14},{18,16},{16,... | collective-permute-start | bytes 3145736 | tf_op jit(solution)/shard_map/cond/branch_1_fun/ppermute | solution.py:120
  94.5 38.6 %collective-permute-start.31 = (bf16[8,2,256,128]{3,2,1,0:T(8,128)(2,1)S(1)}, bf16[8,2,256,128]{3,2,1,0:T(8,128)(2,1)}, u32[]{:S(2)}, u32[]{:S(2)}) collective-permute-start(bf16[8,2,256,128]{3,2,1,0:T(8,128)(2,1)S(1)} %get-tuple-element.119.refs_2_.refs_0_), channel_id=1, source_target_pairs={{24,0},{26,2},{12,4},{14,6},{0,8},{2,10},{20,12},{22,14},{8,16},{1... | collective-permute-start | bytes 3145736 | tf_op jit(solution)/shard_map/ppermute | solution.py:120
  95.0 38.4 %collective-permute-start.32 = (bf16[8,2,256,128]{3,2,1,0:T(8,128)(2,1)}, bf16[8,2,256,128]{3,2,1,0:T(8,128)(2,1)}, u32[]{:S(2)}, u32[]{:S(2)}) collective-permute-start(bf16[8,2,256,128]{3,2,1,0:T(8,128)(2,1)} %get-tuple-element.127.refs_6_), channel_id=1, source_target_pairs={{4,0},{6,2},{0,4},{2,6},{12,8},{14,10},{8,12},{10,14},{20,16},{22,... | collective-permute-start | bytes 3145736 | tf_op jit(solution)/shard_map/ppermute | solution.py:120
  111.0 6.0 %collective-permute-start.11 = (bf16[2,4,2,256,128]{4,3,2,1,0:T(8,128)(2,1)}, bf16[2,4,2,256,128]{4,3,2,1,0:T(8,128)(2,1)}, u32[]{:S(2)}, u32[]{:S(2)}) collective-permute-start(bf16[2,4,2,256,128]{4,3,2,1,0:T(8,128)(2,1)} %get-tuple-element.56), channel_id=1, source_target_pairs={{2,0},{0,2},{6,4},{4,6},{10,8},{8,10},{14,12},{12,14},{18,16},{16,... | collective-permute-start | bytes 3145736 | tf_op jit(solution)/shard_map/cond/branch_1_fun/ppermute | solution.py:120
  111.5 5.5 %collective-permute-start.9 = (bf16[2,4,2,256,128]{4,3,2,1,0:T(8,128)(2,1)S(1)}, bf16[2,4,2,256,128]{4,3,2,1,0:T(8,128)(2,1)}, u32[]{:S(2)}, u32[]{:S(2)}) collective-permute-start(bf16[2,4,2,256,128]{4,3,2,1,0:T(8,128)(2,1)S(1)} %get-tuple-element.54), channel_id=1, source_target_pairs={{2,0},{0,2},{6,4},{4,6},{10,8},{8,10},{14,12},{12,14},{18,16},{16,... | collective-permute-start | bytes 3145736 | tf_op jit(solution)/shard_map/cond/branch_1_fun/ppermute | solution.py:120
  117.0 38.6 %collective-permute-start.29 = (bf16[8,2,256,128]{3,2,1,0:T(8,128)(2,1)}, bf16[8,2,256,128]{3,2,1,0:T(8,128)(2,1)}, u32[]{:S(2)}, u32[]{:S(2)}) collective-permute-start(bf16[8,2,256,128]{3,2,1,0:T(8,128)(2,1)} %get-tuple-element.125.refs_2_.refs_1_), channel_id=1, source_target_pairs={{24,0},{26,2},{12,4},{14,6},{0,8},{2,10},{20,12},{22,14},{8,16},{1... | collective-permute-start | bytes 3145736 | tf_op jit(solution)/shard_map/ppermute | solution.py:120
  117.5 38.4 %collective-permute-start.30 = (bf16[8,2,256,128]{3,2,1,0:T(8,128)(2,1)}, bf16[8,2,256,128]{3,2,1,0:T(8,128)(2,1)}, u32[]{:S(2)}, u32[]{:S(2)}) collective-permute-start(bf16[8,2,256,128]{3,2,1,0:T(8,128)(2,1)} %get-tuple-element.126.refs_7_), channel_id=1, source_target_pairs={{4,0},{6,2},{0,4},{2,6},{12,8},{14,10},{8,12},{10,14},{20,16},{22,... | collective-permute-start | bytes 3145736 | tf_op jit(solution)/shard_map/ppermute | solution.py:120
  133.4 4.5 %collective-permute-start.13 = (bf16[8,2,256,128]{3,2,1,0:T(8,128)(2,1)}, bf16[8,2,256,128]{3,2,1,0:T(8,128)(2,1)}, u32[]{:S(2)}, u32[]{:S(2)}) collective-permute-start(bf16[8,2,256,128]{3,2,1,0:T(8,128)(2,1)} %get-tuple-element.58), channel_id=1, source_target_pairs={{2,0},{0,2},{6,4},{4,6},{10,8},{8,10},{14,12},{12,14},{18,16},{16,... | collective-permute-start | bytes 3145736 | tf_op jit(solution)/shard_map/cond/branch_1_fun/ppermute | solution.py:120
  137.9 48.2 %collective-permute-start.35 = (bf16[2,4,2,256,128]{4,3,2,1,0:T(8,128)(2,1)S(1)}, bf16[2,4,2,256,128]{4,3,2,1,0:T(8,128)(2,1)}, u32[]{:S(2)}, u32[]{:S(2)}) collective-permute-start(bf16[2,4,2,256,128]{4,3,2,1,0:T(8,128)(2,1)S(1)} %get-tuple-element.130.refs_2_.refs_0_), channel_id=1, source_target_pairs={{24,0},{26,2},{12,4},{14,6},{0,8},{2,10},{20,12},{22,14},{8,16},{1... | collective-permute-start | bytes 3145736 | tf_op jit(solution)/shard_map/ppermute | solution.py:120
  138.4 47.7 %collective-permute-start.36 = (bf16[2,4,2,256,128]{4,3,2,1,0:T(8,128)(2,1)}, bf16[2,4,2,256,128]{4,3,2,1,0:T(8,128)(2,1)}, u32[]{:S(2)}, u32[]{:S(2)}) collective-permute-start(bf16[2,4,2,256,128]{4,3,2,1,0:T(8,128)(2,1)} %get-tuple-element.137.refs_3_), channel_id=1, source_target_pairs={{4,0},{6,2},{0,4},{2,6},{12,8},{14,10},{8,12},{10,14},{20,16},{22,... | collective-permute-start | bytes 3145736 | tf_op jit(solution)/shard_map/ppermute | solution.py:120
  155.9 4.5 %collective-permute-start.15 = (bf16[8,2,256,128]{3,2,1,0:T(8,128)(2,1)}, bf16[8,2,256,128]{3,2,1,0:T(8,128)(2,1)}, u32[]{:S(2)}, u32[]{:S(2)}) collective-permute-start(bf16[8,2,256,128]{3,2,1,0:T(8,128)(2,1)} %get-tuple-element.60), channel_id=1, source_target_pairs={{2,0},{0,2},{6,4},{4,6},{10,8},{8,10},{14,12},{12,14},{18,16},{16,... | collective-permute-start | bytes 3145736 | tf_op jit(solution)/shard_map/cond/branch_1_fun/ppermute | solution.py:120
  160.4 43.8 %collective-permute-start.33 = (bf16[2,4,2,256,128]{4,3,2,1,0:T(8,128)(2,1)}, bf16[2,4,2,256,128]{4,3,2,1,0:T(8,128)(2,1)}, u32[]{:S(2)}, u32[]{:S(2)}) collective-permute-start(bf16[2,4,2,256,128]{4,3,2,1,0:T(8,128)(2,1)} %get-tuple-element.134.refs_3_), channel_id=1, source_target_pairs={{4,0},{6,2},{0,4},{2,6},{12,8},{14,10},{8,12},{10,14},{20,16},{22,... | collective-permute-start | bytes 3145736 | tf_op jit(solution)/shard_map/ppermute | solution.py:120
  161.8 42.5 %collective-permute-start.34 = (bf16[2,4,2,256,128]{4,3,2,1,0:T(8,128)(2,1)S(1)}, bf16[2,4,2,256,128]{4,3,2,1,0:T(8,128)(2,1)}, u32[]{:S(2)}, u32[]{:S(2)}) collective-permute-start(bf16[2,4,2,256,128]{4,3,2,1,0:T(8,128)(2,1)S(1)} %get-tuple-element.133.refs_3_.refs_0_), channel_id=1, source_target_pairs={{24,0},{26,2},{12,4},{14,6},{0,8},{2,10},{20,12},{22,14},{8,16},{1... | collective-permute-start | bytes 3145736 | tf_op jit(solution)/shard_map/ppermute | solution.py:120
  186.3 4.5 %collective-permute-start.19 = (bf16[2,4,2,256,128]{4,3,2,1,0:T(8,128)(2,1)}, bf16[2,4,2,256,128]{4,3,2,1,0:T(8,128)(2,1)}, u32[]{:S(2)}, u32[]{:S(2)}) collective-permute-start(bf16[2,4,2,256,128]{4,3,2,1,0:T(8,128)(2,1)} %get-tuple-element.64), channel_id=1, source_target_pairs={{2,0},{0,2},{6,4},{4,6},{10,8},{8,10},{14,12},{12,14},{18,16},{16,... | collective-permute-start | bytes 3145736 | tf_op jit(solution)/shard_map/cond/branch_1_fun/ppermute | solution.py:120
  204.5 4.4 %collective-permute-start.17 = (bf16[2,4,2,256,128]{4,3,2,1,0:T(8,128)(2,1)}, bf16[2,4,2,256,128]{4,3,2,1,0:T(8,128)(2,1)}, u32[]{:S(2)}, u32[]{:S(2)}) collective-permute-start(bf16[2,4,2,256,128]{4,3,2,1,0:T(8,128)(2,1)} %get-tuple-element.62), channel_id=1, source_target_pairs={{2,0},{0,2},{6,4},{4,6},{10,8},{8,10},{14,12},{12,14},{18,16},{16,... | collective-permute-start | bytes 3145736 | tf_op jit(solution)/shard_map/cond/branch_1_fun/ppermute | solution.py:120
  (7 other events, 180.4 us)

commit v5 on v4

--- a/solution.py
+++ b/solution.py
@@ -302,7 +302,7 @@
 def on_device(voltages, input_flags, pair_order):
     weights = input_flags.astype(jnp.bfloat16)[None, None, :, None]
     if lax.axis_size("grp") == 16 and lax.axis_size("chan") == 2:
-        return split_exchange(voltages, weights, pair_order, (8, 4, 4))
+        return split_exchange(voltages, weights, pair_order, (7, 5, 4))
     return window_exchange(voltages, weights, pair_order)
 
 

time: 223 us -> 220 us (0.987)
  blocking collectives: 15.2 us -> 0 us
  starting transfers between devices: 39.6 us -> 51.6 us
  waiting for transfers between devices: 111 us -> 107 us
  other arithmetic: 5.79 us -> 8.81 us
    all_to_all x1 -> x0, blocking collectives: 15.2 us -> none  [split_exchange(): lax.all_to_all(mine, 'chan', split_axis=0, concat_axis=0)]
    ppermute x37, waiting for transfers between devices: 111 us -> 102 us  [permute(): return lambda block: lax.ppermute(block, axis, route)]
    ppermute x37, starting transfers between devices: 36 us -> 44.3 us  [permute(): return lambda block: lax.ppermute(block, axis, route)]
    all_to_all x1 -> x2, waiting for transfers between devices: 0.01 us -> 5.18 us  [split_exchange(): lax.all_to_all(mine, 'chan', split_axis=0, concat_axis=0)]
    all_to_all x1 -> x2, starting transfers between devices: 3.58 us -> 7.34 us  [split_exchange(): lax.all_to_all(mine, 'chan', split_axis=0, concat_axis=0)]
    mul x1 -> x2, other arithmetic: 2.73 us -> 4.89 us  [split_exchange(): mine = columns[:, first:first + size] * weights]
  transfers between devices with their start and end apart: 38 -> 39, of which waited for: 28 -> 32; matrix products, arithmetic and copies ran while one was open for 2% -> 3% of each run, Pallas kernels for 17% -> 17%
where the time goes in v5:
time: 220 us; the launch traced here: 219 us
  waiting for transfers between devices  107 us (49%)
  starting transfers between devices  51.6 us (23%)
  Pallas kernels  50.3 us (23%)
  other arithmetic  8.81 us (4%)
    ppermute x37, waiting for transfers between devices, permute(): return lambda block: lax.ppermute(block, axis, route)  102 us
    pallas_call x3, Pallas kernels, correlate(): pl.pallas_call(functools.partial(pair_kernel, variants, parts, len(source...  50.3 us
    ppermute x37, starting transfers between devices, permute(): return lambda block: lax.ppermute(block, axis, route)  44.3 us
    all_to_all x2, starting transfers between devices, split_exchange(): lax.all_to_all(mine, 'chan', split_axis=0, concat_axis=0)  7.34 us
    all_to_all x2, waiting for transfers between devices, split_exchange(): lax.all_to_all(mine, 'chan', split_axis=0, concat_axis=0)  5.18 us
    mul x2, other arithmetic, split_exchange(): mine = columns[:, first:first + size] * weights  4.89 us
  transfers between devices with their start and end apart: 39, of which 32 were waited for; matrix products, arithmetic and copies ran while one was open for 3% of the time, Pallas kernels for 17%

profile of v5, /device:TPU:0, one launch (start us, length us, event | category | flops | bytes accessed | tf_op | source)
XLA Modules:
  0.0 219.2 jit_solution(9367510517882064148)
XLA Ops:
  0.7 2.6 %dynamic-slice_multiply_fusion = (bf16[7,2,256,128]{3,2,1,0:T(8,128)(2,1)S(1)}, bf16[7,2,256,128]{3,2,1,0:T(8,128)(2,1)}) fusion(bf16[32,2,256,128]{3,2,1,0:T(8,128)(2,1)} %param.19, s32[]{:T(128)S(6)} %select_n.7, bf16[256]{0:T(256)(128)(2,1)S(1)} %convert_element_type.7, s32[]{:T(128)S(6)} %select_n.6), kind=kLoop, calls=%fused_computation.2 | loop fusion | flops 917504 | bytes 3670536 | tf_op jit(solution)/shard_map/mul | solution.py:212
  3.3 2.9 %collective-permute-start.20 = (bf16[7,2,256,128]{3,2,1,0:T(8,128)(2,1)}, bf16[7,2,256,128]{3,2,1,0:T(8,128)(2,1)}, u32[]{:S(2)}, u32[]{:S(2)}) collective-permute-start(bf16[7,2,256,128]{3,2,1,0:T(8,128)(2,1)} %get-tuple-element.148), channel_id=1, source_target_pairs={{0,1},{1,0},{2,3},{3,2},{4,5},{5,4},{6,7},{7,6},{8,9},{9,8},{10,11... | collective-permute-start | bytes 2752520 | tf_op jit(solution)/shard_map/ppermute | solution.py:120
  7.7 3.6 %collective-permute-start.23 = (bf16[7,2,256,128]{3,2,1,0:T(8,128)(2,1)S(1)}, bf16[7,2,256,128]{3,2,1,0:T(8,128)(2,1)}, u32[]{:S(2)}, u32[]{:S(2)}) collective-permute-start(bf16[7,2,256,128]{3,2,1,0:T(8,128)(2,1)S(1)} %get-tuple-element.147.refs_0_), channel_id=1, source_target_pairs={{8,0},{10,2},{28,4},{30,6},{16,8},{18,10},{4,12},{6,14},{24,16},{2... | collective-permute-start | bytes 2752520 | tf_op jit(solution)/shard_map/ppermute | solution.py:120
  11.3 2.5 %slice_multiply_fusion = bf16[2,5,2,256,128]{4,3,2,1,0:T(8,128)(2,1)} fusion(bf16[2,16,2,256,128]{4,3,2,1,0:T(8,128)(2,1)} %bitcast.4, bf16[256]{0:T(256)(128)(2,1)S(1)} %convert_element_type.7), kind=kLoop, calls=%fused_computation | loop fusion | flops 655360 | bytes 2621952 | tf_op jit(solution)/shard_map/mul | solution.py:219
  13.9 3.8 %all-to-all-start.1 = ((bf16[2,5,2,256,128]{4,3,2,1,0:T(8,128)(2,1)}), bf16[2,5,2,256,128]{4,3,2,1,0:T(8,128)(2,1)S(1)}, u32[]{:S(2)}, u32[]{:S(2)}) async-start(bf16[2,5,2,256,128]{4,3,2,1,0:T(8,128)(2,1)} %slice_multiply_fusion), calls=%async_computation.1 | async-start | bytes 2621440 | tf_op jit(solution)/shard_map/all_to_all | solution.py:221
  17.6 10.1 %collective-permute-done.20.refs_0_ = bf16[7,2,256,128]{3,2,1,0:T(8,128)(2,1)} collective-permute-done((bf16[7,2,256,128]{3,2,1,0:T(8,128)(2,1)}, bf16[7,2,256,128]{3,2,1,0:T(8,128)(2,1)}, u32[]{:S(2)}, u32[]{:S(2)}) %collective-permute-start.20) | collective-permute-done | bytes 917536 | tf_op jit(solution)/shard_map/ppermute | solution.py:120
  27.7 4.2 %collective-permute-start.21 = (bf16[7,2,256,128]{3,2,1,0:T(8,128)(2,1)}, bf16[7,2,256,128]{3,2,1,0:T(8,128)(2,1)}, u32[]{:S(2)}, u32[]{:S(2)}) collective-permute-start(bf16[7,2,256,128]{3,2,1,0:T(8,128)(2,1)} %collective-permute-done.20.refs_0_), channel_id=1, source_target_pairs={{8,0},{10,2},{28,4},{30,6},{16,8},{18,10},{4,12},{6,14},{24,16},{2... | collective-permute-start | bytes 2752520 | tf_op jit(solution)/shard_map/ppermute | solution.py:120
  32.9 5.2 %conditional.8 = (bf16[7,2,256,128]{3,2,1,0:T(8,128)(2,1)}, bf16[7,2,256,128]{3,2,1,0:T(8,128)(2,1)}, bf16[7,2,256,128]{3,2,1,0:T(8,128)(2,1)}) conditional(s32[]{:T(128)} %bitcast.2, () %tuple.68, (bf16[7,2,256,128]{3,2,1,0:T(8,128)(2,1)S(1)}, bf16[7,2,256,128]{3,2,1,0:T(8,128)(2,1)}, bf16[7,2,256,128]{3,2,1,0:T(8,128)(2,1)S(1)}) %tuple.69), branch_computations={%region_0.0_spmd, %region_1.0_spmd} | conditional | bytes 11010192 | solution.py:185
  33.4 3.4 %collective-permute-done = bf16[7,2,256,128]{3,2,1,0:T(8,128)(2,1)} collective-permute-done((bf16[7,2,256,128]{3,2,1,0:T(8,128)(2,1)S(1)}, bf16[7,2,256,128]{3,2,1,0:T(8,128)(2,1)}, u32[]{:S(2)}, u32[]{:S(2)}) %collective-permute-start) | collective-permute-done | bytes 917536 | tf_op jit(solution)/shard_map/cond/branch_1_fun/ppermute | solution.py:120
  38.1 2.7 %all-to-all-done.1.refs_0_ = bf16[2,5,2,256,128]{4,3,2,1,0:T(8,128)(2,1)S(1)} async-done(((bf16[2,5,2,256,128]{4,3,2,1,0:T(8,128)(2,1)}), bf16[2,5,2,256,128]{4,3,2,1,0:T(8,128)(2,1)S(1)}, u32[]{:S(2)}, u32[]{:S(2)}) %all-to-all-start.1) | async-done | bytes 1310752 | tf_op jit(solution)/shard_map/all_to_all | solution.py:221
  40.8 3.9 %collective-permute-start.27 = (bf16[2,5,2,256,128]{4,3,2,1,0:T(8,128)(2,1)S(1)}, bf16[2,5,2,256,128]{4,3,2,1,0:T(8,128)(2,1)}, u32[]{:S(2)}, u32[]{:S(2)}) collective-permute-start(bf16[2,5,2,256,128]{4,3,2,1,0:T(8,128)(2,1)S(1)} %shard_map.37.refs_2_.refs_0_), channel_id=1, source_target_pairs={{8,0},{10,2},{28,4},{30,6},{16,8},{18,10},{4,12},{6,14},{24,16},{2... | collective-permute-start | bytes 3932168 | tf_op jit(solution)/shard_map/ppermute | solution.py:120
  47.0 3.6 %all-to-all-start = ((bf16[2,4,2,256,128]{4,3,2,1,0:T(8,128)(2,1)}), bf16[2,4,2,256,128]{4,3,2,1,0:T(8,128)(2,1)S(1)}, u32[]{:S(2)}, u32[]{:S(2)}) async-start(bf16[2,4,2,256,128]{4,3,2,1,0:T(8,128)(2,1)} %slice_multiply_fusion.1), calls=%async_computation | async-start | bytes 2097152 | tf_op jit(solution)/shard_map/all_to_all | solution.py:221
  55.5 5.4 %conditional.9 = (bf16[7,2,256,128]{3,2,1,0:T(8,128)(2,1)}, bf16[7,2,256,128]{3,2,1,0:T(8,128)(2,1)}, bf16[7,2,256,128]{3,2,1,0:T(8,128)(2,1)}) conditional(s32[]{:T(128)} %bitcast.2, () %tuple.67, (bf16[7,2,256,128]{3,2,1,0:T(8,128)(2,1)}, bf16[7,2,256,128]{3,2,1,0:T(8,128)(2,1)}, bf16[7,2,256,128]{3,2,1,0:T(8,128)(2,1)}) %tuple.70), branch_computations={%region_2.0_spmd, %region_3.0_spmd} | conditional | bytes 11010192 | solution.py:185
  65.2 15.8 %collective-permute-done.27.refs_0_ = bf16[2,5,2,256,128]{4,3,2,1,0:T(8,128)(2,1)} collective-permute-done((bf16[2,5,2,256,128]{4,3,2,1,0:T(8,128)(2,1)S(1)}, bf16[2,5,2,256,128]{4,3,2,1,0:T(8,128)(2,1)}, u32[]{:S(2)}, u32[]{:S(2)}) %collective-permute-start.27) | collective-permute-done | bytes 1310752 | tf_op jit(solution)/shard_map/ppermute | solution.py:120
  81.0 2.6 %collective-permute-done.28.refs_1_ = bf16[2,5,2,256,128]{4,3,2,1,0:T(8,128)(2,1)} collective-permute-done((bf16[2,5,2,256,128]{4,3,2,1,0:T(8,128)(2,1)S(1)}, bf16[2,5,2,256,128]{4,3,2,1,0:T(8,128)(2,1)}, u32[]{:S(2)}, u32[]{:S(2)}) %collective-permute-start.28) | collective-permute-done | bytes 1310752 | tf_op jit(solution)/shard_map/ppermute | solution.py:120
  83.6 7.1 %conditional.10 = (bf16[2,5,2,256,128]{4,3,2,1,0:T(8,128)(2,1)}, bf16[2,5,2,256,128]{4,3,2,1,0:T(8,128)(2,1)}, bf16[2,5,2,256,128]{4,3,2,1,0:T(8,128)(2,1)}) conditional(s32[]{:T(128)} %bitcast.2, () %tuple.71, (bf16[2,5,2,256,128]{4,3,2,1,0:T(8,128)(2,1)S(1)}, bf16[2,5,2,256,128]{4,3,2,1,0:T(8,128)(2,1)}, ...), branch_computations={%region_4.0_spmd, %region_5.0_spmd} | conditional | bytes 15728784 | solution.py:185
  84.1 4.5 %collective-permute-done.6 = bf16[2,5,2,256,128]{4,3,2,1,0:T(8,128)(2,1)} collective-permute-done((bf16[2,5,2,256,128]{4,3,2,1,0:T(8,128)(2,1)S(1)}, bf16[2,5,2,256,128]{4,3,2,1,0:T(8,128)(2,1)}, u32[]{:S(2)}, u32[]{:S(2)}) %collective-permute-start.6) | collective-permute-done | bytes 1310752 | tf_op jit(solution)/shard_map/cond/branch_1_fun/ppermute | solution.py:120
  92.4 11.1 %collective-permute-done.25.refs_0_ = bf16[2,4,2,256,128]{4,3,2,1,0:T(8,128)(2,1)} collective-permute-done((bf16[2,4,2,256,128]{4,3,2,1,0:T(8,128)(2,1)S(1)}, bf16[2,4,2,256,128]{4,3,2,1,0:T(8,128)(2,1)}, u32[]{:S(2)}, u32[]{:S(2)}) %collective-permute-start.25) | collective-permute-done | bytes 1048608 | tf_op jit(solution)/shard_map/ppermute | solution.py:120
  103.5 2.5 %collective-permute-done.26.refs_1_ = bf16[2,4,2,256,128]{4,3,2,1,0:T(8,128)(2,1)} collective-permute-done((bf16[2,4,2,256,128]{4,3,2,1,0:T(8,128)(2,1)S(1)}, bf16[2,4,2,256,128]{4,3,2,1,0:T(8,128)(2,1)}, u32[]{:S(2)}, u32[]{:S(2)}) %collective-permute-start.26) | collective-permute-done | bytes 1048608 | tf_op jit(solution)/shard_map/ppermute | solution.py:120
  106.0 6.0 %conditional.11 = (bf16[2,4,2,256,128]{4,3,2,1,0:T(8,128)(2,1)}, bf16[2,4,2,256,128]{4,3,2,1,0:T(8,128)(2,1)}, bf16[2,4,2,256,128]{4,3,2,1,0:T(8,128)(2,1)}) conditional(s32[]{:T(128)} %bitcast.2, () %tuple.74, (bf16[2,4,2,256,128]{4,3,2,1,0:T(8,128)(2,1)S(1)}, bf16[2,4,2,256,128]{4,3,2,1,0:T(8,128)(2,1)}, ...), branch_computations={%region_6.0_spmd, %region_7.0_spmd} | conditional | bytes 12583056 | solution.py:185
  109.0 3.0 %collective-permute-done.11 = bf16[2,4,2,256,128]{4,3,2,1,0:T(8,128)(2,1)} collective-permute-done((bf16[2,4,2,256,128]{4,3,2,1,0:T(8,128)(2,1)}, bf16[2,4,2,256,128]{4,3,2,1,0:T(8,128)(2,1)}, u32[]{:S(2)}, u32[]{:S(2)}) %collective-permute-start.11) | collective-permute-done | bytes 1048608 | tf_op jit(solution)/shard_map/cond/branch_1_fun/ppermute | solution.py:120
  112.0 18.0 %collective-permute-start.30 = (bf16[7,2,256,128]{3,2,1,0:T(8,128)(2,1)}, bf16[7,2,256,128]{3,2,1,0:T(8,128)(2,1)}, u32[]{:S(2)}, u32[]{:S(2)}) collective-permute-start(bf16[7,2,256,128]{3,2,1,0:T(8,128)(2,1)} %get-tuple-element.126.refs_7_), channel_id=1, source_target_pairs={{4,0},{6,2},{0,4},{2,6},{12,8},{14,10},{8,12},{10,14},{20,16},{22,... | collective-permute-start | bytes 2752520 | tf_op jit(solution)/shard_map/ppermute | solution.py:120
  130.0 4.2 %conditional.12 = (bf16[7,2,256,128]{3,2,1,0:T(8,128)(2,1)}, bf16[7,2,256,128]{3,2,1,0:T(8,128)(2,1)}) conditional(s32[]{:T(128)} %bitcast.2, () %tuple.76, (bf16[7,2,256,128]{3,2,1,0:T(8,128)(2,1)}, bf16[7,2,256,128]{3,2,1,0:T(8,128)(2,1)}) %shard_map.44), branch_computations={%region_8.0_spmd, %region_9.0_spmd} | conditional | bytes 7340128 | solution.py:185
  134.7 8.2 %collective-permute-done.29.refs_0_ = bf16[7,2,256,128]{3,2,1,0:T(8,128)(2,1)} collective-permute-done((bf16[7,2,256,128]{3,2,1,0:T(8,128)(2,1)}, bf16[7,2,256,128]{3,2,1,0:T(8,128)(2,1)}, u32[]{:S(2)}, u32[]{:S(2)}) %collective-permute-start.29) | collective-permute-done | bytes 917536 | tf_op jit(solution)/shard_map/ppermute | solution.py:120
  143.0 8.5 %collective-permute-done.30.refs_1_ = bf16[7,2,256,128]{3,2,1,0:T(8,128)(2,1)} collective-permute-done((bf16[7,2,256,128]{3,2,1,0:T(8,128)(2,1)}, bf16[7,2,256,128]{3,2,1,0:T(8,128)(2,1)}, u32[]{:S(2)}, u32[]{:S(2)}) %collective-permute-start.30) | collective-permute-done | bytes 917536 | tf_op jit(solution)/shard_map/ppermute | solution.py:120
  151.5 4.1 %conditional.13 = (bf16[7,2,256,128]{3,2,1,0:T(8,128)(2,1)}, bf16[7,2,256,128]{3,2,1,0:T(8,128)(2,1)}) conditional(s32[]{:T(128)} %bitcast.2, () %tuple.73, (bf16[7,2,256,128]{3,2,1,0:T(8,128)(2,1)}, bf16[7,2,256,128]{3,2,1,0:T(8,128)(2,1)}) %shard_map.46), branch_computations={%region_10.0_spmd, %region_11.0_spmd} | conditional | bytes 7340128 | solution.py:185
  158.4 21.0 %shard_map.48.refs_2_ = f32[1,9,16,256,512]{4,3,2,1,0:T(8,128)} custom-call(s32[10]{0:T(128)} %pad_add_fusion.table, bf16[7,2,256,128]{3,2,1,0:T(8,128)(2,1)S(1)} %get-tuple-element.119.refs_2_.refs_0_, bf16[7,2,256,128]{3,2,1,0:T(8,128)(2,1)} %get-tuple-element.125.refs_2_.refs_1_, bf16[7,2,256,128]{3,2,1,0:T(8,128)(2,1)} %copy-done, ...), custom_call_target="tpu_custom_call" | custom-call | flops 4227858432 | bytes 24772608 | tf_op jit(solution)/shard_map/pallas_call | solution.py:84
  179.6 5.3 %conditional.15 = (bf16[2,5,2,256,128]{4,3,2,1,0:T(8,128)(2,1)}, bf16[2,5,2,256,128]{4,3,2,1,0:T(8,128)(2,1)}) conditional(s32[]{:T(128)} %bitcast.2, () %tuple.79, (bf16[2,5,2,256,128]{4,3,2,1,0:T(8,128)(2,1)}, bf16[2,5,2,256,128]{4,3,2,1,0:T(8,128)(2,1)}) %tuple.80), branch_computations={%region_14.0_spmd, %region_15.0_spmd} | conditional | bytes 10485856 | solution.py:185
  180.1 2.9 %collective-permute-done.18 = bf16[2,5,2,256,128]{4,3,2,1,0:T(8,128)(2,1)} collective-permute-done((bf16[2,5,2,256,128]{4,3,2,1,0:T(8,128)(2,1)}, bf16[2,5,2,256,128]{4,3,2,1,0:T(8,128)(2,1)}, u32[]{:S(2)}, u32[]{:S(2)}) %collective-permute-start.18) | collective-permute-done | bytes 1310752 | tf_op jit(solution)/shard_map/cond/branch_1_fun/ppermute | solution.py:120
  184.8 15.9 %shard_map.50.refs_10_ = f32[1,9,16,256,512]{4,3,2,1,0:T(8,128)} custom-call(s32[10]{0:T(128)} %pad_add_fusion.table, bf16[2,5,2,256,128]{4,3,2,1,0:T(8,128)(2,1)S(1)} %get-tuple-element.130.refs_2_.refs_0_, bf16[2,5,2,256,128]{4,3,2,1,0:T(8,128)(2,1)} %get-tuple-element.115.refs_4_.refs_1_, ...), custom_call_target="tpu_custom_call", output_to_operand_aliasing={{}: (11, {})} | custom-call | flops 3019898880 | bytes 17694720 | tf_op jit(solution)/shard_map/pallas_call | solution.py:84
  201.3 4.5 %conditional.14 = (bf16[2,4,2,256,128]{4,3,2,1,0:T(8,128)(2,1)}, bf16[2,4,2,256,128]{4,3,2,1,0:T(8,128)(2,1)}) conditional(s32[]{:T(128)} %bitcast.2, () %tuple.77, (bf16[2,4,2,256,128]{4,3,2,1,0:T(8,128)(2,1)}, bf16[2,4,2,256,128]{4,3,2,1,0:T(8,128)(2,1)}) %tuple.78), branch_computations={%region_12.0_spmd, %region_13.0_spmd} | conditional | bytes 8388704 | solution.py:185
  205.8 13.4 %shard_map.51 = f32[1,9,16,256,512]{4,3,2,1,0:T(8,128)} custom-call(s32[10]{0:T(128)} %pad_add_fusion.table, bf16[2,4,2,256,128]{4,3,2,1,0:T(8,128)(2,1)S(1)} %get-tuple-element.133.refs_3_.refs_0_, bf16[2,4,2,256,128]{4,3,2,1,0:T(8,128)(2,1)} %get-tuple-element.121.refs_4_.refs_1_, ...), custom_call_target="tpu_custom_call", output_to_operand_aliasing={{}: (11, {})} | custom-call | flops 2415919104 | bytes 14155776 | tf_op jit(solution)/shard_map/pallas_call | solution.py:84
  (78 shorter events, 48.5 us)
Async XLA Ops:
  3.3 24.4 %collective-permute-start.20 = (bf16[7,2,256,128]{3,2,1,0:T(8,128)(2,1)}, bf16[7,2,256,128]{3,2,1,0:T(8,128)(2,1)}, u32[]{:S(2)}, u32[]{:S(2)}) collective-permute-start(bf16[7,2,256,128]{3,2,1,0:T(8,128)(2,1)} %get-tuple-element.148), channel_id=1, source_target_pairs={{0,1},{1,0},{2,3},{3,2},{4,5},{5,4},{6,7},{7,6},{8,9},{9,8},{10,11... | collective-permute-start | bytes 2752520 | tf_op jit(solution)/shard_map/ppermute | solution.py:120
  6.2 25.7 %collective-permute-start.24 = (bf16[7,2,256,128]{3,2,1,0:T(8,128)(2,1)S(1)}, bf16[7,2,256,128]{3,2,1,0:T(8,128)(2,1)S(1)}, u32[]{:S(2)}, u32[]{:S(2)}) collective-permute-start(bf16[7,2,256,128]{3,2,1,0:T(8,128)(2,1)S(1)} %get-tuple-element.147.refs_0_), channel_id=1, source_target_pairs={{4,0},{6,2},{0,4},{2,6},{12,8},{14,10},{8,12},{10,14},{20,16},{22,... | collective-permute-start | bytes 2752520 | tf_op jit(solution)/shard_map/ppermute | solution.py:120
  7.7 24.2 %collective-permute-start.23 = (bf16[7,2,256,128]{3,2,1,0:T(8,128)(2,1)S(1)}, bf16[7,2,256,128]{3,2,1,0:T(8,128)(2,1)}, u32[]{:S(2)}, u32[]{:S(2)}) collective-permute-start(bf16[7,2,256,128]{3,2,1,0:T(8,128)(2,1)S(1)} %get-tuple-element.147.refs_0_), channel_id=1, source_target_pairs={{8,0},{10,2},{28,4},{30,6},{16,8},{18,10},{4,12},{6,14},{24,16},{2... | collective-permute-start | bytes 2752520 | tf_op jit(solution)/shard_map/ppermute | solution.py:120
  13.9 26.9 %all-to-all-start.1 = ((bf16[2,5,2,256,128]{4,3,2,1,0:T(8,128)(2,1)}), bf16[2,5,2,256,128]{4,3,2,1,0:T(8,128)(2,1)S(1)}, u32[]{:S(2)}, u32[]{:S(2)}) async-start(bf16[2,5,2,256,128]{4,3,2,1,0:T(8,128)(2,1)} %slice_multiply_fusion), calls=%async_computation.1 | async-start | bytes 2621440 | tf_op jit(solution)/shard_map/all_to_all | solution.py:221
  27.7 25.3 %collective-permute-start.21 = (bf16[7,2,256,128]{3,2,1,0:T(8,128)(2,1)}, bf16[7,2,256,128]{3,2,1,0:T(8,128)(2,1)}, u32[]{:S(2)}, u32[]{:S(2)}) collective-permute-start(bf16[7,2,256,128]{3,2,1,0:T(8,128)(2,1)} %collective-permute-done.20.refs_0_), channel_id=1, source_target_pairs={{8,0},{10,2},{28,4},{30,6},{16,8},{18,10},{4,12},{6,14},{24,16},{2... | collective-permute-start | bytes 2752520 | tf_op jit(solution)/shard_map/ppermute | solution.py:120
  31.9 23.6 %collective-permute-start.22 = (bf16[7,2,256,128]{3,2,1,0:T(8,128)(2,1)}, bf16[7,2,256,128]{3,2,1,0:T(8,128)(2,1)}, u32[]{:S(2)}, u32[]{:S(2)}) collective-permute-start(bf16[7,2,256,128]{3,2,1,0:T(8,128)(2,1)} %collective-permute-done.20.refs_0_), channel_id=1, source_target_pairs={{4,0},{6,2},{0,4},{2,6},{12,8},{14,10},{8,12},{10,14},{20,16},{22,... | collective-permute-start | bytes 2752520 | tf_op jit(solution)/shard_map/ppermute | solution.py:120
  32.9 5.1 %collective-permute-start.1 = (bf16[7,2,256,128]{3,2,1,0:T(8,128)(2,1)}, bf16[7,2,256,128]{3,2,1,0:T(8,128)(2,1)}, u32[]{:S(2)}, u32[]{:S(2)}) collective-permute-start(bf16[7,2,256,128]{3,2,1,0:T(8,128)(2,1)} %get-tuple-element.46), channel_id=1, source_target_pairs={{2,0},{0,2},{6,4},{4,6},{10,8},{8,10},{14,12},{12,14},{18,16},{16,... | collective-permute-start | bytes 2752520 | tf_op jit(solution)/shard_map/cond/branch_1_fun/ppermute | solution.py:120
  33.4 4.7 %collective-permute-start.2 = (bf16[7,2,256,128]{3,2,1,0:T(8,128)(2,1)S(1)}, bf16[7,2,256,128]{3,2,1,0:T(8,128)(2,1)}, u32[]{:S(2)}, u32[]{:S(2)}) collective-permute-start(bf16[7,2,256,128]{3,2,1,0:T(8,128)(2,1)S(1)} %get-tuple-element.47), channel_id=1, source_target_pairs={{2,0},{0,2},{6,4},{4,6},{10,8},{8,10},{14,12},{12,14},{18,16},{16,... | collective-permute-start | bytes 2752520 | tf_op jit(solution)/shard_map/cond/branch_1_fun/ppermute | solution.py:120
  40.8 40.2 %collective-permute-start.27 = (bf16[2,5,2,256,128]{4,3,2,1,0:T(8,128)(2,1)S(1)}, bf16[2,5,2,256,128]{4,3,2,1,0:T(8,128)(2,1)}, u32[]{:S(2)}, u32[]{:S(2)}) collective-permute-start(bf16[2,5,2,256,128]{4,3,2,1,0:T(8,128)(2,1)S(1)} %shard_map.37.refs_2_.refs_0_), channel_id=1, source_target_pairs={{8,0},{10,2},{28,4},{30,6},{16,8},{18,10},{4,12},{6,14},{24,16},{2... | collective-permute-start | bytes 3932168 | tf_op jit(solution)/shard_map/ppermute | solution.py:120
  44.7 38.9 %collective-permute-start.28 = (bf16[2,5,2,256,128]{4,3,2,1,0:T(8,128)(2,1)S(1)}, bf16[2,5,2,256,128]{4,3,2,1,0:T(8,128)(2,1)}, u32[]{:S(2)}, u32[]{:S(2)}) collective-permute-start(bf16[2,5,2,256,128]{4,3,2,1,0:T(8,128)(2,1)S(1)} %shard_map.37.refs_2_.refs_0_), channel_id=1, source_target_pairs={{4,0},{6,2},{0,4},{2,6},{12,8},{14,10},{8,12},{10,14},{20,16},{22,... | collective-permute-start | bytes 3932168 | tf_op jit(solution)/shard_map/ppermute | solution.py:120
  47.0 16.4 %all-to-all-start = ((bf16[2,4,2,256,128]{4,3,2,1,0:T(8,128)(2,1)}), bf16[2,4,2,256,128]{4,3,2,1,0:T(8,128)(2,1)S(1)}, u32[]{:S(2)}, u32[]{:S(2)}) async-start(bf16[2,4,2,256,128]{4,3,2,1,0:T(8,128)(2,1)} %slice_multiply_fusion.1), calls=%async_computation | async-start | bytes 2097152 | tf_op jit(solution)/shard_map/all_to_all | solution.py:221
  55.5 4.1 %collective-permute-start.4 = (bf16[7,2,256,128]{3,2,1,0:T(8,128)(2,1)}, bf16[7,2,256,128]{3,2,1,0:T(8,128)(2,1)}, u32[]{:S(2)}, u32[]{:S(2)}) collective-permute-start(bf16[7,2,256,128]{3,2,1,0:T(8,128)(2,1)} %get-tuple-element.49), channel_id=1, source_target_pairs={{2,0},{0,2},{6,4},{4,6},{10,8},{8,10},{14,12},{12,14},{18,16},{16,... | collective-permute-start | bytes 2752520 | tf_op jit(solution)/shard_map/cond/branch_1_fun/ppermute | solution.py:120
  56.0 4.9 %collective-permute-start.5 = (bf16[7,2,256,128]{3,2,1,0:T(8,128)(2,1)}, bf16[7,2,256,128]{3,2,1,0:T(8,128)(2,1)}, u32[]{:S(2)}, u32[]{:S(2)}) collective-permute-start(bf16[7,2,256,128]{3,2,1,0:T(8,128)(2,1)} %get-tuple-element.50), channel_id=1, source_target_pairs={{2,0},{0,2},{6,4},{4,6},{10,8},{8,10},{14,12},{12,14},{18,16},{16,... | collective-permute-start | bytes 2752520 | tf_op jit(solution)/shard_map/cond/branch_1_fun/ppermute | solution.py:120
  63.4 40.1 %collective-permute-start.25 = (bf16[2,4,2,256,128]{4,3,2,1,0:T(8,128)(2,1)S(1)}, bf16[2,4,2,256,128]{4,3,2,1,0:T(8,128)(2,1)}, u32[]{:S(2)}, u32[]{:S(2)}) collective-permute-start(bf16[2,4,2,256,128]{4,3,2,1,0:T(8,128)(2,1)S(1)} %shard_map.39.refs_2_.refs_0_), channel_id=1, source_target_pairs={{8,0},{10,2},{28,4},{30,6},{16,8},{18,10},{4,12},{6,14},{24,16},{2... | collective-permute-start | bytes 3145736 | tf_op jit(solution)/shard_map/ppermute | solution.py:120
  64.9 41.1 %collective-permute-start.26 = (bf16[2,4,2,256,128]{4,3,2,1,0:T(8,128)(2,1)S(1)}, bf16[2,4,2,256,128]{4,3,2,1,0:T(8,128)(2,1)}, u32[]{:S(2)}, u32[]{:S(2)}) collective-permute-start(bf16[2,4,2,256,128]{4,3,2,1,0:T(8,128)(2,1)S(1)} %shard_map.39.refs_2_.refs_0_), channel_id=1, source_target_pairs={{4,0},{6,2},{0,4},{2,6},{12,8},{14,10},{8,12},{10,14},{20,16},{22,... | collective-permute-start | bytes 3145736 | tf_op jit(solution)/shard_map/ppermute | solution.py:120
  83.6 5.0 %collective-permute-start.6 = (bf16[2,5,2,256,128]{4,3,2,1,0:T(8,128)(2,1)S(1)}, bf16[2,5,2,256,128]{4,3,2,1,0:T(8,128)(2,1)}, u32[]{:S(2)}, u32[]{:S(2)}) collective-permute-start(bf16[2,5,2,256,128]{4,3,2,1,0:T(8,128)(2,1)S(1)} %get-tuple-element.51), channel_id=1, source_target_pairs={{2,0},{0,2},{6,4},{4,6},{10,8},{8,10},{14,12},{12,14},{18,16},{16,... | collective-permute-start | bytes 3932168 | tf_op jit(solution)/shard_map/cond/branch_1_fun/ppermute | solution.py:120
  83.6 5.2 %collective-permute-start.7 = (bf16[2,5,2,256,128]{4,3,2,1,0:T(8,128)(2,1)}, bf16[2,5,2,256,128]{4,3,2,1,0:T(8,128)(2,1)}, u32[]{:S(2)}, u32[]{:S(2)}) collective-permute-start(bf16[2,5,2,256,128]{4,3,2,1,0:T(8,128)(2,1)} %get-tuple-element.52), channel_id=1, source_target_pairs={{2,0},{0,2},{6,4},{4,6},{10,8},{8,10},{14,12},{12,14},{18,16},{16,... | collective-permute-start | bytes 3932168 | tf_op jit(solution)/shard_map/cond/branch_1_fun/ppermute | solution.py:120
  84.1 6.6 %collective-permute-start.8 = (bf16[2,5,2,256,128]{4,3,2,1,0:T(8,128)(2,1)}, bf16[2,5,2,256,128]{4,3,2,1,0:T(8,128)(2,1)}, u32[]{:S(2)}, u32[]{:S(2)}) collective-permute-start(bf16[2,5,2,256,128]{4,3,2,1,0:T(8,128)(2,1)} %get-tuple-element.53), channel_id=1, source_target_pairs={{2,0},{0,2},{6,4},{4,6},{10,8},{8,10},{14,12},{12,14},{18,16},{16,... | collective-permute-start | bytes 3932168 | tf_op jit(solution)/shard_map/cond/branch_1_fun/ppermute | solution.py:120
  90.7 39.3 %collective-permute-start.31 = (bf16[7,2,256,128]{3,2,1,0:T(8,128)(2,1)S(1)}, bf16[7,2,256,128]{3,2,1,0:T(8,128)(2,1)}, u32[]{:S(2)}, u32[]{:S(2)}) collective-permute-start(bf16[7,2,256,128]{3,2,1,0:T(8,128)(2,1)S(1)} %get-tuple-element.119.refs_2_.refs_0_), channel_id=1, source_target_pairs={{24,0},{26,2},{12,4},{14,6},{0,8},{2,10},{20,12},{22,14},{8,16},{1... | collective-permute-start | bytes 2752520 | tf_op jit(solution)/shard_map/ppermute | solution.py:120
  90.7 39.3 %collective-permute-start.32 = (bf16[7,2,256,128]{3,2,1,0:T(8,128)(2,1)}, bf16[7,2,256,128]{3,2,1,0:T(8,128)(2,1)}, u32[]{:S(2)}, u32[]{:S(2)}) collective-permute-start(bf16[7,2,256,128]{3,2,1,0:T(8,128)(2,1)} %get-tuple-element.127.refs_6_), channel_id=1, source_target_pairs={{4,0},{6,2},{0,4},{2,6},{12,8},{14,10},{8,12},{10,14},{20,16},{22,... | collective-permute-start | bytes 2752520 | tf_op jit(solution)/shard_map/ppermute | solution.py:120
  106.0 6.0 %collective-permute-start.11 = (bf16[2,4,2,256,128]{4,3,2,1,0:T(8,128)(2,1)}, bf16[2,4,2,256,128]{4,3,2,1,0:T(8,128)(2,1)}, u32[]{:S(2)}, u32[]{:S(2)}) collective-permute-start(bf16[2,4,2,256,128]{4,3,2,1,0:T(8,128)(2,1)} %get-tuple-element.56), channel_id=1, source_target_pairs={{2,0},{0,2},{6,4},{4,6},{10,8},{8,10},{14,12},{12,14},{18,16},{16,... | collective-permute-start | bytes 3145736 | tf_op jit(solution)/shard_map/cond/branch_1_fun/ppermute | solution.py:120
  106.5 5.5 %collective-permute-start.9 = (bf16[2,4,2,256,128]{4,3,2,1,0:T(8,128)(2,1)S(1)}, bf16[2,4,2,256,128]{4,3,2,1,0:T(8,128)(2,1)}, u32[]{:S(2)}, u32[]{:S(2)}) collective-permute-start(bf16[2,4,2,256,128]{4,3,2,1,0:T(8,128)(2,1)S(1)} %get-tuple-element.54), channel_id=1, source_target_pairs={{2,0},{0,2},{6,4},{4,6},{10,8},{8,10},{14,12},{12,14},{18,16},{16,... | collective-permute-start | bytes 3145736 | tf_op jit(solution)/shard_map/cond/branch_1_fun/ppermute | solution.py:120
  112.0 30.9 %collective-permute-start.29 = (bf16[7,2,256,128]{3,2,1,0:T(8,128)(2,1)}, bf16[7,2,256,128]{3,2,1,0:T(8,128)(2,1)}, u32[]{:S(2)}, u32[]{:S(2)}) collective-permute-start(bf16[7,2,256,128]{3,2,1,0:T(8,128)(2,1)} %get-tuple-element.125.refs_2_.refs_1_), channel_id=1, source_target_pairs={{24,0},{26,2},{12,4},{14,6},{0,8},{2,10},{20,12},{22,14},{8,16},{1... | collective-permute-start | bytes 2752520 | tf_op jit(solution)/shard_map/ppermute | solution.py:120
  112.0 39.5 %collective-permute-start.30 = (bf16[7,2,256,128]{3,2,1,0:T(8,128)(2,1)}, bf16[7,2,256,128]{3,2,1,0:T(8,128)(2,1)}, u32[]{:S(2)}, u32[]{:S(2)}) collective-permute-start(bf16[7,2,256,128]{3,2,1,0:T(8,128)(2,1)} %get-tuple-element.126.refs_7_), channel_id=1, source_target_pairs={{4,0},{6,2},{0,4},{2,6},{12,8},{14,10},{8,12},{10,14},{20,16},{22,... | collective-permute-start | bytes 2752520 | tf_op jit(solution)/shard_map/ppermute | solution.py:120
  130.1 4.1 %collective-permute-start.13 = (bf16[7,2,256,128]{3,2,1,0:T(8,128)(2,1)}, bf16[7,2,256,128]{3,2,1,0:T(8,128)(2,1)}, u32[]{:S(2)}, u32[]{:S(2)}) collective-permute-start(bf16[7,2,256,128]{3,2,1,0:T(8,128)(2,1)} %get-tuple-element.58), channel_id=1, source_target_pairs={{2,0},{0,2},{6,4},{4,6},{10,8},{8,10},{14,12},{12,14},{18,16},{16,... | collective-permute-start | bytes 2752520 | tf_op jit(solution)/shard_map/cond/branch_1_fun/ppermute | solution.py:120
  134.2 45.1 %collective-permute-start.35 = (bf16[2,5,2,256,128]{4,3,2,1,0:T(8,128)(2,1)S(1)}, bf16[2,5,2,256,128]{4,3,2,1,0:T(8,128)(2,1)}, u32[]{:S(2)}, u32[]{:S(2)}) collective-permute-start(bf16[2,5,2,256,128]{4,3,2,1,0:T(8,128)(2,1)S(1)} %get-tuple-element.130.refs_2_.refs_0_), channel_id=1, source_target_pairs={{24,0},{26,2},{12,4},{14,6},{0,8},{2,10},{20,12},{22,14},{8,16},{1... | collective-permute-start | bytes 3932168 | tf_op jit(solution)/shard_map/ppermute | solution.py:120
  134.2 45.4 %collective-permute-start.36 = (bf16[2,5,2,256,128]{4,3,2,1,0:T(8,128)(2,1)}, bf16[2,5,2,256,128]{4,3,2,1,0:T(8,128)(2,1)}, u32[]{:S(2)}, u32[]{:S(2)}) collective-permute-start(bf16[2,5,2,256,128]{4,3,2,1,0:T(8,128)(2,1)} %get-tuple-element.137.refs_3_), channel_id=1, source_target_pairs={{4,0},{6,2},{0,4},{2,6},{12,8},{14,10},{8,12},{10,14},{20,16},{22,... | collective-permute-start | bytes 3932168 | tf_op jit(solution)/shard_map/ppermute | solution.py:120
  151.5 4.1 %collective-permute-start.15 = (bf16[7,2,256,128]{3,2,1,0:T(8,128)(2,1)}, bf16[7,2,256,128]{3,2,1,0:T(8,128)(2,1)}, u32[]{:S(2)}, u32[]{:S(2)}) collective-permute-start(bf16[7,2,256,128]{3,2,1,0:T(8,128)(2,1)} %get-tuple-element.60), channel_id=1, source_target_pairs={{2,0},{0,2},{6,4},{4,6},{10,8},{8,10},{14,12},{12,14},{18,16},{16,... | collective-permute-start | bytes 2752520 | tf_op jit(solution)/shard_map/cond/branch_1_fun/ppermute | solution.py:120
  155.6 45.6 %collective-permute-start.33 = (bf16[2,4,2,256,128]{4,3,2,1,0:T(8,128)(2,1)}, bf16[2,4,2,256,128]{4,3,2,1,0:T(8,128)(2,1)}, u32[]{:S(2)}, u32[]{:S(2)}) collective-permute-start(bf16[2,4,2,256,128]{4,3,2,1,0:T(8,128)(2,1)} %get-tuple-element.134.refs_3_), channel_id=1, source_target_pairs={{4,0},{6,2},{0,4},{2,6},{12,8},{14,10},{8,12},{10,14},{20,16},{22,... | collective-permute-start | bytes 3145736 | tf_op jit(solution)/shard_map/ppermute | solution.py:120
  157.7 43.6 %collective-permute-start.34 = (bf16[2,4,2,256,128]{4,3,2,1,0:T(8,128)(2,1)S(1)}, bf16[2,4,2,256,128]{4,3,2,1,0:T(8,128)(2,1)}, u32[]{:S(2)}, u32[]{:S(2)}) collective-permute-start(bf16[2,4,2,256,128]{4,3,2,1,0:T(8,128)(2,1)S(1)} %get-tuple-element.133.refs_3_.refs_0_), channel_id=1, source_target_pairs={{24,0},{26,2},{12,4},{14,6},{0,8},{2,10},{20,12},{22,14},{8,16},{1... | collective-permute-start | bytes 3145736 | tf_op jit(solution)/shard_map/ppermute | solution.py:120
  179.6 5.2 %collective-permute-start.19 = (bf16[2,5,2,256,128]{4,3,2,1,0:T(8,128)(2,1)}, bf16[2,5,2,256,128]{4,3,2,1,0:T(8,128)(2,1)}, u32[]{:S(2)}, u32[]{:S(2)}) collective-permute-start(bf16[2,5,2,256,128]{4,3,2,1,0:T(8,128)(2,1)} %get-tuple-element.64), channel_id=1, source_target_pairs={{2,0},{0,2},{6,4},{4,6},{10,8},{8,10},{14,12},{12,14},{18,16},{16,... | collective-permute-start | bytes 3932168 | tf_op jit(solution)/shard_map/cond/branch_1_fun/ppermute | solution.py:120
  201.3 4.5 %collective-permute-start.17 = (bf16[2,4,2,256,128]{4,3,2,1,0:T(8,128)(2,1)}, bf16[2,4,2,256,128]{4,3,2,1,0:T(8,128)(2,1)}, u32[]{:S(2)}, u32[]{:S(2)}) collective-permute-start(bf16[2,4,2,256,128]{4,3,2,1,0:T(8,128)(2,1)} %get-tuple-element.62), channel_id=1, source_target_pairs={{2,0},{0,2},{6,4},{4,6},{10,8},{8,10},{14,12},{12,14},{18,16},{16,... | collective-permute-start | bytes 3145736 | tf_op jit(solution)/shard_map/cond/branch_1_fun/ppermute | solution.py:120
  (9 other events, 40.7 us)
